TPU v7x, 32 devices: a whole 2x2x4 slice. The times are simulated.
32 devices in a mesh: wide: 8 (over z, x), narrow: 4 (over y, core).
Axes of the slice: x: 2, y: 2, z: 4, core: 2. Of those that a mesh axis runs over, the one named last changes fastest.
Arguments:
- pair_act: bfloat16 [768, 768, 128], P('wide', 'narrow'), may hold values from -6 to 6
- residue_mask: int32 [768], replicated, may hold values 0 or 1
- w_proj_start: bfloat16 [128, 512], replicated, may hold values from -0.5 to 0.5
- w_bias_start: bfloat16 [128, 4], replicated, may hold values from -40 to 40
- w_out_start: bfloat16 [128, 128], replicated, may hold values from -0.5 to 0.5
- w_proj_end: bfloat16 [128, 512], replicated, may hold values from -0.5 to 0.5
- w_bias_end: bfloat16 [128, 4], replicated, may hold values from -40 to 40
- w_out_end: bfloat16 [128, 128], replicated, may hold values from -0.5 to 0.5
Outputs:
- update_start: bfloat16 [768, 768, 128], P('wide', 'narrow')
- update_end: bfloat16 [768, 768, 128], P('wide', 'narrow')
All inputs are finite; a program needn't handle non-finite values.
Results may differ from a plain program's by a relative error of at most 0.012.
The roundings to bfloat16 on the way count: a program that leaves them out, or rounds other values in their place, can miss the bound.
Values may be sent and summed in bfloat16 or wider, within the bound.
No kernel may reach another device: no remote copies, remote signals or barrier semaphores. Data moves between devices by JAX's collectives and lax.ppermute only.
A program may use at most 128 MiB of HBM per device.

v0:
```python
import jax
import jax.numpy as jnp
from jax import lax
from jax.sharding import PartitionSpec as P

norm_eps = 1e-05
masked_score = -1000000000.0


def layer_norm(features):
    average = jnp.mean(features, axis=-1, keepdims=True)
    centred = features - average
    spread = jnp.mean(centred * centred, axis=-1, keepdims=True)
    return (centred * lax.rsqrt(spread + norm_eps)).astype(jnp.bfloat16)


def attend(projected, pair_bias, row_ok, key_ok, head_count, head_dim):
    length = projected.shape[1]
    inv_root = head_dim ** (-0.5)

    def one_row(item_pair):
        packed, valid_row = item_pair
        packed = packed.reshape(length, head_count, 4, head_dim)
        queries = packed[:, :, 0]
        keyset = packed[:, :, 1]
        values = packed[:, :, 2]
        gating = packed[:, :, 3]
        scores = (
            jnp.einsum("bhd,khd->hbk", queries, keyset, preferred_element_type=jnp.float32)
            * inv_root
            + pair_bias
        )
        allowed = jnp.logical_and(valid_row, key_ok)
        scores = jnp.where(allowed[None, None, :], scores, masked_score)
        weights = jax.nn.softmax(scores, axis=-1).astype(jnp.bfloat16)
        summed = jnp.einsum("hbk,khd->bhd", weights, values, preferred_element_type=jnp.float32)
        gated = (jax.nn.sigmoid(gating.astype(jnp.float32)) * summed).astype(jnp.bfloat16)
        return gated.reshape(length, head_count * head_dim)

    return lax.map(one_row, (projected, row_ok))


def on_device(
    pair_act,
    residue_mask,
    w_proj_start,
    w_bias_start,
    w_out_start,
    w_proj_end,
    w_bias_end,
    w_out_end,
):
    wide_count = lax.axis_size("wide")
    narrow_count = lax.axis_size("narrow")
    wide_at = lax.axis_index("wide")
    narrow_at = lax.axis_index("narrow")
    tile_rows, tile_cols, channels = pair_act.shape
    head_count = w_bias_start.shape[1]
    head_dim = w_out_start.shape[0] // head_count
    residue_ok = residue_mask > 0
    normed = layer_norm(pair_act.astype(jnp.float32))
    row_count = tile_rows // narrow_count
    row_lines = lax.all_to_all(normed, "narrow", split_axis=0, concat_axis=1, tiled=True)
    projected = jnp.einsum(
        "abc,cx->abx", row_lines, w_proj_start, preferred_element_type=jnp.float32
    ).astype(jnp.bfloat16)
    bias_part = jnp.einsum(
        "abc,ch->hab", row_lines, w_bias_start, preferred_element_type=jnp.float32
    )
    pair_bias = lax.all_gather(bias_part, ("wide", "narrow"), axis=1, tiled=True)
    first_row = wide_at * tile_rows + narrow_at * row_count
    row_ok = lax.dynamic_slice_in_dim(residue_ok, first_row, row_count)
    gated = attend(projected, pair_bias, row_ok, residue_ok, head_count, head_dim)
    upd_lines = jnp.einsum(
        "abx,xc->abc", gated, w_out_start, preferred_element_type=jnp.float32
    ).astype(jnp.bfloat16)
    update_start = lax.all_to_all(upd_lines, "narrow", split_axis=1, concat_axis=0, tiled=True)
    updated = pair_act.astype(jnp.float32) + update_start.astype(jnp.float32)
    normed_end = layer_norm(updated)
    col_count = tile_cols // wide_count
    col_lines = lax.all_to_all(normed_end, "wide", split_axis=1, concat_axis=0, tiled=True)
    projected_end = jnp.einsum(
        "abc,cx->bax", col_lines, w_proj_end, preferred_element_type=jnp.float32
    ).astype(jnp.bfloat16)
    bias_part_end = jnp.einsum(
        "abc,ch->hba", col_lines, w_bias_end, preferred_element_type=jnp.float32
    )
    half_bias = lax.all_gather(bias_part_end, "wide", axis=1, tiled=True)
    pair_bias_end = lax.all_gather(half_bias, "narrow", axis=1, tiled=True)
    first_col = narrow_at * tile_cols + wide_at * col_count
    col_ok = lax.dynamic_slice_in_dim(residue_ok, first_col, col_count)
    gated_end = attend(projected_end, pair_bias_end, col_ok, residue_ok, head_count, head_dim)
    upd_cols = jnp.einsum(
        "bax,xc->abc", gated_end, w_out_end, preferred_element_type=jnp.float32
    ).astype(jnp.bfloat16)
    update_end = lax.all_to_all(upd_cols, "wide", split_axis=0, concat_axis=1, tiled=True)
    return (update_start, update_end)


def solution(mesh):
    in_specs = (P("wide", "narrow", None), P(), P(), P(), P(), P(), P(), P())
    out_specs = (P("wide", "narrow", None), P("wide", "narrow", None))
    return jax.shard_map(
        on_device, mesh=mesh, in_specs=in_specs, out_specs=out_specs, check_vma=False
    )
```

profile of v0, /device:TPU:0, one launch (start us, length us, event | category | flops | bytes accessed | tf_op | source)
XLA Modules:
  0.0 1729.6 jit_solution(12411749659524013704)
XLA Ops:
  11.5 7.7 fusion.14
  25.1 57.8 %all_to_all.72 = bf16[96,192,128]{2,1,0:T(8,128)(2,1)S(1)} all-to-all(bf16[96,192,128]{2,1,0:T(8,128)(2,1)S(1)} %fusion.15), channel_id=1, replica_groups=mesh['wide'=8,'narrow'=4] {'narrow'}, dimensions={0} | all-to-all | bytes 9437184 | tf_op jit(solution)/shard_map/all_to_all | solution.py:63
  88.5 11.5 convolution_convert_fusion
  100.1 69.4 %all-gather.4.cloned.1.call-done = f32[4,768,768]{2,0,1:T(4,128)} async-done(((f32[4,24,768]{2,0,1:T(4,128)}), f32[4,768,768]{2,0,1:T(4,128)}) %all-gather.4.cloned.1.call-update) | async-done | bytes 9437200 | tf_op jit(solution)/shard_map/all_gather | solution.py:70
  169.5 11.9 copy.63
  184.2 541.1 %while.20 = (s32[]{:T(128)}, bf16[24,768,128]{1,2,0:T(8,128)(2,1)}, bf16[24,768,512]{2,1,0:T(8,128)(2,1)}, pred[24]{0:T(512)(128)(4,1)S(1)}, pred[768]{0:T(1024)...) while((s32[]{:T(128)}, bf16[24,768,128]{1,2,0:T(8,128)(2,1)}, bf16[24,768,512]{2,1,0:T(8,128)(2,1)}, ...), condition=%wide.region_5.6_spmd, body=%wide.region_2.5_spmd.sunk | while | flops 321459456 | bytes 89484400 | solution.py:40
  197.1 8.9 fusion.48
  219.7 8.9 fusion.48
  242.2 8.9 fusion.48
  264.7 8.9 fusion.48
  287.3 8.9 fusion.48
  309.8 8.9 fusion.48
  332.3 8.9 fusion.48
  354.9 8.9 fusion.48
  377.4 8.9 fusion.48
  400.0 8.9 fusion.48
  422.5 8.9 fusion.48
  445.0 8.9 fusion.48
  467.6 8.9 fusion.48
  490.1 8.9 fusion.48
  512.6 8.9 fusion.48
  535.2 8.9 fusion.48
  557.7 8.9 fusion.48
  580.2 8.9 fusion.48
  602.8 8.9 fusion.48
  625.3 8.9 fusion.48
  647.8 8.9 fusion.48
  670.4 8.9 fusion.48
  692.9 8.9 fusion.48
  715.4 8.9 fusion.48
  732.1 56.6 %all_to_all.73 = bf16[24,768,128]{2,0,1:T(8,128)(2,1)S(1)} all-to-all(bf16[24,768,128]{2,0,1:T(8,128)(2,1)S(1)} %copy.65), channel_id=1, replica_groups=mesh['wide'=8,'narrow'=4] {'narrow'}, dimensions={1} | all-to-all | bytes 9437184 | tf_op jit(solution)/shard_map/all_to_all | solution.py:77
  793.3 6.5 multiply_reduce_fusion
  809.2 108.5 %all_to_all.74 = bf16[96,192,128]{2,0,1:T(8,128)(2,1)S(1)} all-to-all(bf16[96,192,128]{2,0,1:T(8,128)(2,1)S(1)} %copy.67), channel_id=1, replica_groups=mesh['wide'=8,'narrow'=4] {'wide'}, dimensions={1} | all-to-all | bytes 9437184 | tf_op jit(solution)/shard_map/all_to_all | solution.py:81
  921.8 7.8 convolution_bitcast_fusion
  930.9 50.1 %all-gather.6.cloned.1.call-done = f32[4,192,768]{2,0,1:T(4,128)} async-done(((f32[4,24,768]{2,0,1:T(4,128)}), f32[4,192,768]{2,0,1:T(4,128)}) %all-gather.6.cloned.1.call-update) | async-done | bytes 2359312 | tf_op jit(solution)/shard_map/all_gather | solution.py:88
  981.0 14.2 convert_bitcast_fusion
  995.2 50.1 %all-gather.8.cloned.1.call-done = f32[4,768,768]{2,0,1:T(4,128)} async-done(((f32[4,192,768]{2,0,1:T(4,128)}), f32[4,768,768]{2,0,1:T(4,128)}) %all-gather.8.cloned.1.call-update) | async-done | bytes 9437200 | tf_op jit(solution)/shard_map/all_gather | solution.py:89
  1045.3 11.9 copy.73
  1060.0 542.4 %while.21 = (s32[]{:T(128)}, bf16[24,768,128]{1,2,0:T(8,128)(2,1)}, bf16[24,768,512]{2,1,0:T(8,128)(2,1)}, pred[24]{0:T(512)(128)(4,1)S(1)}, pred[768]{0:T(1024)...) while((s32[]{:T(128)}, bf16[24,768,128]{1,2,0:T(8,128)(2,1)}, bf16[24,768,512]{2,1,0:T(8,128)(2,1)}, ...), condition=%wide.region_11.12_spmd, body=%wide.region_8.11_spmd.sunk | while | flops 321459456 | bytes 89484400 | solution.py:40
  1073.0 8.9 fusion.52
  1095.6 8.9 fusion.52
  1118.2 8.9 fusion.52
  1140.8 8.9 fusion.52
  1163.4 8.9 fusion.52
  1186.0 8.9 fusion.52
  1208.6 8.9 fusion.52
  1231.1 8.9 fusion.52
  1253.7 8.9 fusion.52
  1276.3 8.9 fusion.52
  1298.9 8.9 fusion.52
  1321.5 8.9 fusion.52
  1344.1 8.9 fusion.52
  1366.7 8.9 fusion.52
  1389.3 8.9 fusion.52
  1411.9 8.9 fusion.52
  1434.5 8.9 fusion.52
  1457.1 8.9 fusion.52
  1479.6 8.9 fusion.52
  1502.2 8.9 fusion.52
  1524.8 8.9 fusion.52
  1547.4 8.9 fusion.52
  1570.0 8.9 fusion.52
  1592.6 8.9 fusion.52
  1609.2 110.1 %all_to_all.75 = bf16[768,24,128]{2,1,0:T(8,128)(2,1)S(1)} all-to-all(bf16[768,24,128]{2,1,0:T(8,128)(2,1)S(1)} %copy.75), channel_id=1, replica_groups=mesh['wide'=8,'narrow'=4] {'wide'}, dimensions={0} | all-to-all | bytes 9437184 | tf_op jit(solution)/shard_map/all_to_all | solution.py:96
  (492 shorter events, 712.5 us)
Async XLA Ops:
  7.2 81.4 %copy-start = (bf16[128,512]{1,0:T(8,128)(2,1)S(1)}, bf16[128,512]{1,0:T(8,128)(2,1)}, u32[]{:S(2)}) copy-start(bf16[128,512]{1,0:T(8,128)(2,1)} %param.14) | copy-start | bytes 393220
  7.2 162.3 %all-gather.4.cloned.1.call-start = ((), (), s32[]{:S(2)}) async-start(), calls=%async_computation.4 | async-start | bytes 9732096 | tf_op jit(solution)/shard_map/all_gather | solution.py:70
  7.2 12.0 copy-start.4
  25.1 60.5 %copy-start.12 = (bf16[128,4]{0,1:T(4,128)(2,1)S(1)}, bf16[128,4]{0,1:T(4,128)(2,1)}, u32[]{:S(2)}) copy-start(bf16[128,4]{0,1:T(4,128)(2,1)} %param.15) | copy-start | bytes 3076
  82.9 5.0 copy-start.11
  83.4 2.2 copy-start.6
  87.6 893.4 %all-gather.6.cloned.1.call-start = ((), (), s32[]{:S(2)}) async-start(), calls=%async_computation.5 | async-start | bytes 2654208 | tf_op jit(solution)/shard_map/all_gather | solution.py:88
  184.2 541.1 %copy-start.9 = (bf16[128,128]{1,0:T(8,128)(2,1)S(1)}, bf16[128,128]{1,0:T(8,128)(2,1)}, u32[]{:S(2)}) copy-start(bf16[128,128]{1,0:T(8,128)(2,1)} %param.16) | copy-start | bytes 98308
  191.8 3.6 copy-start.2
  214.4 3.6 copy-start.2
  236.9 3.6 copy-start.2
  259.4 3.6 copy-start.2
  282.0 3.6 copy-start.2
  304.5 3.6 copy-start.2
  327.0 3.6 copy-start.2
  349.6 3.6 copy-start.2
  372.1 3.6 copy-start.2
  394.7 3.6 copy-start.2
  417.2 3.6 copy-start.2
  439.7 3.6 copy-start.2
  462.3 3.6 copy-start.2
  484.8 3.6 copy-start.2
  507.3 3.6 copy-start.2
  529.9 3.6 copy-start.2
  552.4 3.6 copy-start.2
  574.9 3.6 copy-start.2
  597.5 3.6 copy-start.2
  620.0 3.6 copy-start.2
  642.5 3.6 copy-start.2
  665.1 3.6 copy-start.2
  687.6 3.6 copy-start.2
  710.1 3.6 copy-start.2
  732.1 57.9 %slice-start = ((s8[4718592]{0:T(1024)(128)(4,1)}), s8[4194304]{0:T(1024)(128)(4,1)S(1)}, s32[]{:S(2)}) async-start(s8[4718592]{0:T(1024)(128)(4,1)} %bitcast.156), calls=%async_computation.7 | async-start | bytes 8388608
  789.9 9.9 copy-start.5
  809.2 112.5 %copy-start.13 = (bf16[128,4]{0,1:T(4,128)(2,1)S(1)}, bf16[128,4]{0,1:T(4,128)(2,1)}, u32[]{:S(2)}) copy-start(bf16[128,4]{0,1:T(4,128)(2,1)} %param.18) | copy-start | bytes 3076
  917.7 63.3 %copy-start.8 = (bf16[128,512]{1,0:T(8,128)(2,1)S(1)}, bf16[128,512]{1,0:T(8,128)(2,1)}, u32[]{:S(2)}) copy-start(bf16[128,512]{1,0:T(8,128)(2,1)} %param.17) | copy-start | bytes 393220
  930.9 114.5 %all-gather.8.cloned.1.call-start = ((), (), s32[]{:S(2)}) async-start(), calls=%async_computation.6 | async-start | bytes 11796480 | tf_op jit(solution)/shard_map/all_gather | solution.py:89
  995.2 64.8 %copy-start.14 = (pred[24]{0:T(512)(128)(4,1)S(1)}, pred[24]{0:T(512)(128)(4,1)}, u32[]{:S(2)}) copy-start(pred[24]{0:T(512)(128)(4,1)} %get-tuple-element.216) | copy-start | bytes 76
  1060.0 542.4 %copy-start.10 = (bf16[128,128]{1,0:T(8,128)(2,1)S(1)}, bf16[128,128]{1,0:T(8,128)(2,1)}, u32[]{:S(2)}) copy-start(bf16[128,128]{1,0:T(8,128)(2,1)} %param.19) | copy-start | bytes 98308
  1067.7 3.6 copy-start.3
  1090.3 3.6 copy-start.3
  1112.9 3.6 copy-start.3
  1135.5 3.6 copy-start.3
  1158.1 3.6 copy-start.3
  1180.7 3.6 copy-start.3
  1203.3 3.6 copy-start.3
  1225.8 3.6 copy-start.3
  1248.4 3.6 copy-start.3
  1271.0 3.6 copy-start.3
  1293.6 3.6 copy-start.3
  1316.2 3.6 copy-start.3
  1338.8 3.6 copy-start.3
  1361.4 3.6 copy-start.3
  1384.0 3.6 copy-start.3
  1406.6 3.6 copy-start.3
  1429.2 3.6 copy-start.3
  1451.8 3.6 copy-start.3
  1474.3 3.6 copy-start.3
  1496.9 3.6 copy-start.3
  1519.5 3.6 copy-start.3
  1542.1 3.6 copy-start.3
  1564.7 3.6 copy-start.3
  1587.3 3.6 copy-start.3
  1606.2 116.7 %copy-start.1 = (bf16[128,512]{1,0:T(8,128)(2,1)S(1)}, bf16[128,512]{1,0:T(8,128)(2,1)}, u32[]{:S(2)}) copy-start(bf16[128,512]{1,0:T(8,128)(2,1)} %param.14) | copy-start | bytes 393220
  (2 other events, 3.4 us)
Sparse Core Ops, SparseCore 0:
  87.8 81.7 all-gather.3
  931.0 49.9 all-gather.5
  982.6 62.7 all-gather.7
where the time goes:
time: 1740 us; the launch traced here: 1730 us
  matrix products  707 us (41%)
  local copies, waits for them, and re-layouts  359 us (21%)
  blocking collectives  333 us (19%)
  waiting for transfers between devices  170 us (10%)
  other arithmetic  145 us (8%)
    dot_general x48, matrix products, one_row(): jnp.einsum('hbk,khd->bhd', weights, values, preferred_element_type=jnp.fl...  426 us
    dot_general x48, matrix products, one_row(): jnp.einsum('bhd,khd->hbk', queries, keyset, preferred_element_type=jnp.fl...  237 us
    while x96, local copies, waits for them, and re-layouts  174 us
    all_to_all x1, blocking collectives, on_device(): lax.all_to_all(upd_cols, 'wide', split_axis=0, concat_axis=1, tiled=True)  110 us
    all_to_all x1, blocking collectives, on_device(): lax.all_to_all(normed_end, 'wide', split_axis=1, concat_axis=0, tiled=True)  109 us
    dynamic_slice x144, local copies, waits for them, and re-layouts, attend(): return lax.map(one_row, (projected, row_ok))  99.8 us
    sub x48, other arithmetic, one_row(): weights = jax.nn.softmax(scores, axis=-1).astype(jnp.bfloat16)  79.9 us
    all_gather x1, waiting for transfers between devices, on_device(): lax.all_gather(bias_part, ('wide', 'narrow'), axis=1, tiled=True)  69.4 us
  transfers between devices with their start and end apart: 3, of which 3 were waited for; matrix products, arithmetic and copies ran while one was open for 2% of the time, Pallas kernels for 0%

commit v1 on v0

v1 whole, which is shorter than its diff:
```python
import functools

import jax
import jax.numpy as jnp
from jax import lax
from jax.experimental import pallas as pl
from jax.experimental.pallas import tpu as pltpu
from jax.sharding import PartitionSpec as P

norm_eps = 1e-05
log2e = 1.4426950408889634
far_below = -1e30
lanes = 128


def layer_norm(features):
    average = jnp.mean(features, axis=-1, keepdims=True)
    centred = features - average
    spread = jnp.mean(centred * centred, axis=-1, keepdims=True)
    return (centred * lax.rsqrt(spread + norm_eps)).astype(jnp.bfloat16)


def pack_projection(w_proj, head_count, head_dim):
    split = w_proj.reshape(w_proj.shape[0], head_count, 4, head_dim)
    twice = jnp.concatenate([split, split], axis=-1)
    parts = [twice[:, :, 0], twice[:, :, 1], split[:, :, 2], split[:, :, 3]]
    return jnp.concatenate([part.reshape(w_proj.shape[0], -1) for part in parts], axis=1)


def attend_kernel(
    row_ok_ref,
    key_ok_ref,
    x_ref,
    bias_ref,
    w_proj_ref,
    w_out_ref,
    *rest,
    head_count,
    head_dim,
    query_block,
    bias_swapped,
    emit_next,
):
    if emit_next:
        upd_ref, next_ref, bias_scr = rest
    else:
        upd_ref, bias_scr = rest
    length, channels = x_ref.shape[1], x_ref.shape[2]
    width = head_count * head_dim
    pair = 2 * width
    step = pl.program_id(0)

    @pl.when(step == 0)
    def _():
        allowed = key_ok_ref[...] > 0
        for h in range(head_count):
            plane = bias_ref[h]
            if bias_swapped:
                plane = plane.T
            bias_scr[h] = jnp.where(allowed, plane * log2e, far_below)

    if emit_next:
        features = x_ref[0].astype(jnp.float32)
        normed = layer_norm(features)
    else:
        normed = x_ref[0]
    projected = jnp.dot(normed, w_proj_ref[...], preferred_element_type=jnp.float32).astype(
        jnp.bfloat16
    )
    queries = projected[:, :pair].astype(jnp.float32) * (head_dim ** (-0.5) * log2e)
    keyset = projected[:, pair : 2 * pair]
    values = projected[:, 2 * pair : 2 * pair + width]
    gating = jax.nn.sigmoid(projected[:, 2 * pair + width :].astype(jnp.float32))

    def finish(summed):
        gated = (gating * summed).astype(jnp.bfloat16)
        update = jnp.dot(gated, w_out_ref[...], preferred_element_type=jnp.float32).astype(
            jnp.bfloat16
        )
        upd_ref[0] = update
        if emit_next:
            next_ref[0] = layer_norm(features + update.astype(jnp.float32))

    row_ok = row_ok_ref[step] > 0

    @pl.when(row_ok)
    def _():
        upper = queries.astype(jnp.bfloat16)
        lower = (queries - upper.astype(jnp.float32)).astype(jnp.bfloat16)
        spot = lax.broadcasted_iota(jnp.int32, (1, pair), 1)
        both = jnp.where(spot % (2 * head_dim) < head_dim, upper, lower)
        values_ones = jnp.concatenate([values, jnp.ones_like(values)], axis=1)
        owner = lax.broadcasted_iota(jnp.int32, (1, width), 1) // head_dim
        block_heads = lanes // (2 * head_dim)
        pieces = []
        for start in range(0, length, query_block):
            summed = jnp.zeros((query_block, width), jnp.float32)
            for h in range(head_count):
                base = h // block_heads * lanes
                local = lax.broadcasted_iota(jnp.int32, (1, lanes), 1) // (2 * head_dim)
                lhs = jnp.where(
                    local == h % block_heads,
                    both[start : start + query_block, base : base + lanes],
                    jnp.zeros((), jnp.bfloat16),
                )
                scores = lax.dot_general(
                    lhs,
                    keyset[:, base : base + lanes],
                    (((1,), (1,)), ((), ())),
                    preferred_element_type=jnp.float32,
                )
                scores = scores + bias_scr[h, start : start + query_block]
                top = jnp.max(scores, axis=-1, keepdims=True)
                weights = jnp.exp2(scores - top).astype(jnp.bfloat16)
                both_sums = jnp.dot(weights, values_ones, preferred_element_type=jnp.float32)
                ratio = both_sums[:, :width] / both_sums[:, width:]
                summed = jnp.where(owner == h, ratio, summed)
            pieces.append(summed)
        finish(jnp.concatenate(pieces, axis=0))

    @pl.when(jnp.logical_not(row_ok))
    def _():
        even = jnp.full((), 1.0 / length, jnp.float32).astype(jnp.bfloat16).astype(jnp.float32)
        total = jnp.sum(values.astype(jnp.float32), axis=0, keepdims=True)
        finish(jnp.broadcast_to(total * even, (length, width)))


def attend(row_ok, key_ok, lines, pair_bias, w_proj, w_out, bias_swapped, emit_next):
    count, length, channels = lines.shape
    head_count = pair_bias.shape[0]
    width = w_out.shape[0]
    head_dim = width // head_count
    query_block = min(length, 256)
    packed = pack_projection(w_proj, head_count, head_dim)
    line_spec = pl.BlockSpec((1, length, channels), lambda i, ok: (i, 0, 0))

    def whole(shape):
        return pl.BlockSpec(shape, lambda i, ok: (0,) * len(shape), pipeline_mode=pl.Buffered(1))

    out_count = 2 if emit_next else 1
    line_shape = jax.ShapeDtypeStruct((count, length, channels), jnp.bfloat16)
    scores = count * head_count * length * length
    return pl.pallas_call(
        functools.partial(
            attend_kernel,
            head_count=head_count,
            head_dim=head_dim,
            query_block=query_block,
            bias_swapped=bias_swapped,
            emit_next=emit_next,
        ),
        out_shape=[line_shape] * out_count,
        grid_spec=pltpu.PrefetchScalarGridSpec(
            num_scalar_prefetch=1,
            grid=(count,),
            in_specs=[
                whole((1, length)),
                line_spec,
                whole((head_count, length, length)),
                whole(packed.shape),
                whole(w_out.shape),
            ],
            out_specs=[line_spec] * out_count,
            scratch_shapes=[pltpu.VMEM((head_count, length, length), jnp.float32)],
        ),
        compiler_params=pltpu.CompilerParams(
            dimension_semantics=("arbitrary",), vmem_limit_bytes=56 * 1024 * 1024
        ),
        cost_estimate=pl.CostEstimate(
            flops=4 * scores * 128, bytes_accessed=8 * lines.size, transcendentals=scores
        ),
        name="attend_next" if emit_next else "attend_last",
    )(row_ok, key_ok[None, :], lines, pair_bias, packed, w_out)


def on_device(
    pair_act,
    residue_mask,
    w_proj_start,
    w_bias_start,
    w_out_start,
    w_proj_end,
    w_bias_end,
    w_out_end,
):
    wide_count = lax.axis_size("wide")
    narrow_count = lax.axis_size("narrow")
    wide_at = lax.axis_index("wide")
    narrow_at = lax.axis_index("narrow")
    tile_rows, tile_cols, channels = pair_act.shape
    row_count = tile_rows // narrow_count
    col_count = tile_cols // wide_count
    mask = (residue_mask > 0).astype(jnp.int32)

    rows = lax.all_to_all(pair_act, "narrow", split_axis=0, concat_axis=1, tiled=True)
    normed = layer_norm(rows.astype(jnp.float32))
    bias_part = jnp.einsum("abc,ch->hab", normed, w_bias_start, preferred_element_type=jnp.float32)
    pair_bias = lax.all_gather(bias_part, ("wide", "narrow"), axis=1, tiled=True)
    row_ok = lax.dynamic_slice_in_dim(mask, wide_at * tile_rows + narrow_at * row_count, row_count)
    upd_rows, next_rows = attend(
        row_ok, mask, rows, pair_bias, w_proj_start, w_out_start, False, True
    )
    update_start = lax.all_to_all(upd_rows, "narrow", split_axis=1, concat_axis=0, tiled=True)

    bias_part_end = jnp.einsum(
        "abc,ch->hab", next_rows, w_bias_end, preferred_element_type=jnp.float32
    )
    pair_bias_end = lax.all_gather(bias_part_end, ("wide", "narrow"), axis=1, tiled=True)
    next_tile = lax.all_to_all(next_rows, "narrow", split_axis=1, concat_axis=0, tiled=True)
    columns = lax.all_to_all(
        next_tile.transpose(1, 0, 2), "wide", split_axis=0, concat_axis=1, tiled=True
    )
    col_ok = lax.dynamic_slice_in_dim(mask, narrow_at * tile_cols + wide_at * col_count, col_count)
    (upd_cols,) = attend(
        col_ok, mask, columns, pair_bias_end, w_proj_end, w_out_end, True, False
    )
    upd_tile = lax.all_to_all(upd_cols, "wide", split_axis=1, concat_axis=0, tiled=True)
    return (update_start, upd_tile.transpose(1, 0, 2))


def solution(mesh):
    in_specs = (P("wide", "narrow", None), P(), P(), P(), P(), P(), P(), P())
    out_specs = (P("wide", "narrow", None), P("wide", "narrow", None))
    return jax.shard_map(
        on_device, mesh=mesh, in_specs=in_specs, out_specs=out_specs, check_vma=False
    )
```

time: 1740 us -> 715 us (0.41)
  matrix products: 707 us -> 11.1 us
  local copies, waits for them, and re-layouts: 359 us -> 51.2 us
  Pallas kernels: 0 us -> 201 us
  blocking collectives: 333 us -> 133 us
  other arithmetic: 145 us -> 9.78 us
  waiting for transfers between devices: 170 us -> 276 us
    dot_general x102 -> x2, matrix products: 707 us -> 11.1 us  [the longest x1 7.45 us: on_device(): jnp.einsum('abc,ch->hab', normed, w_bias_start, preferred_element_type=jn...]
    pallas_call x0 -> x2, Pallas kernels: none -> 201 us  [attend(): pl.pallas_call(functools.partial(attend_kernel, head_count=head_count, he...]
    all_to_all x4 -> x2, blocking collectives: 333 us -> 133 us  [the longest x1 75.2 us: on_device(): lax.all_to_all(next_rows, 'narrow', split_axis=1, concat_axis=0, tiled=True)]
    while x98 -> x0, local copies, waits for them, and re-layouts: 198 us -> none
    all_to_all x0 -> x3, waiting for transfers between devices: none -> 196 us  [the longest x1 99.1 us: on_device(): lax.all_to_all(upd_cols, 'wide', split_axis=1, concat_axis=0, tiled=True)]
    all_gather x2 -> x1, waiting for transfers between devices: 100 us -> 0.01 us  [on_device(): lax.all_gather(bias_part_end, ('wide', 'narrow'), axis=1, tiled=True)]
    dynamic_slice x145 -> x1, local copies, waits for them, and re-layouts: 100 us -> 0.62 us  [on_device(): lax.dynamic_slice_in_dim(mask, narrow_at * tile_cols + wide_at * col_coun...]
    sub x48 -> x0, other arithmetic: 79.9 us -> none  [one_row(): weights = jax.nn.softmax(scores, axis=-1).astype(jnp.bfloat16)]
  transfers between devices with their start and end apart: 3 -> 5, of which waited for: 3 -> 3; matrix products, arithmetic and copies ran while one was open for 2% -> 6% of each run, Pallas kernels for 0% -> 13%
where the time goes in v1:
time: 715 us; the launch traced here: 713 us
  waiting for transfers between devices  276 us (39%)
  Pallas kernels  201 us (28%)
  blocking collectives  133 us (19%)
  local copies, waits for them, and re-layouts  51.2 us (7%)
  starting transfers between devices  16.7 us (2%)
  between operations  14.3 us (2%)
  matrix products  11.1 us (2%)
  other arithmetic  9.78 us (1%)
    pallas_call x2, Pallas kernels, attend(): pl.pallas_call(functools.partial(attend_kernel, head_count=head_count, he...  201 us
    all_to_all x1, waiting for transfers between devices, on_device(): lax.all_to_all(upd_cols, 'wide', split_axis=1, concat_axis=0, tiled=True)  99.1 us
    all_to_all x1, waiting for transfers between devices, on_device(): lax.all_to_all(next_tile.transpose(1, 0, 2), 'wide', split_axis=0, concat...  96.6 us
    all_gather x1, waiting for transfers between devices, on_device(): lax.all_gather(bias_part, ('wide', 'narrow'), axis=1, tiled=True)  79.9 us
    all_to_all x1, blocking collectives, on_device(): lax.all_to_all(next_rows, 'narrow', split_axis=1, concat_axis=0, tiled=True)  75.2 us
    all_to_all x1, blocking collectives, on_device(): lax.all_to_all(pair_act, 'narrow', split_axis=0, concat_axis=1, tiled=True)  58.3 us
    pallas_call x3, local copies, waits for them, and re-layouts, attend(): pl.pallas_call(functools.partial(attend_kernel, head_count=head_count, he...  20.4 us
  transfers between devices with their start and end apart: 5, of which 3 were waited for; matrix products, arithmetic and copies ran while one was open for 6% of the time, Pallas kernels for 13%

profile of v1, /device:TPU:0, one launch (start us, length us, event | category | flops | bytes accessed | tf_op | source)
XLA Modules:
  0.0 713.0 jit_solution(13470109338910997425)
XLA Ops:
  7.2 0.0 copy-start
  7.2 0.0 all-gather.3.cloned.1.call-start
  7.2 58.3 %all_to_all.90 = bf16[96,192,128]{2,1,0:T(8,128)(2,1)S(1)} all-to-all(bf16[96,192,128]{2,1,0:T(8,128)(2,1)} %param.8), channel_id=1, replica_groups=mesh['wide'=8,'narrow'=4] {'narrow'}, dimensions={0} | all-to-all | bytes 9437184 | tf_op jit(solution)/shard_map/all_to_all | solution.py:195
  65.5 1.8 convert_reduce_fusion
  67.3 2.6 copy.61
  70.0 6.4 fusion.1
  76.4 0.1 div.9
  76.5 0.0 copy-start.2
  76.6 0.1 rsqrt.12
  76.7 0.0 copy-done
  76.7 0.0 copy-start.4
  76.7 7.5 %fusion.2 = f32[24,768,4]{1,2,0:T(4,128)S(1)} fusion(bf16[24,768,128]{2,1,0:T(8,128)(2,1)} %bitcast.54, f32[24,768]{1,0:T(8,128)S(1)} %rsqrt.12, f32[24,768]{1,0:T(8,128)S(1)} %div.9, bf16[128,4]{0,1:T(4,128)(2,1)S(1)} %copy-done), kind=kOutput, calls=%fused_computation.5 | convolution fusion | flops 28311552 | bytes 5161984 | tf_op jit(solution)/shard_map/abc,ch->hab/dot_general | solution.py:197
  84.1 0.8 copy.89
  84.9 0.0 all-gather.3.cloned.1.call-update
  84.9 0.2 all-gather.5.cloned.1.call-start
  85.2 0.0 copy-done.2
  85.2 0.1 copy.63
  85.3 0.1 copy.64
  85.5 0.1 copy.65
  85.6 0.1 copy.66
  85.7 0.1 copy.67
  85.8 0.0 copy-done.4
  85.8 0.6 broadcast_in_dim.2.key_ok_ref
  86.4 0.6 fusion.10
  87.1 0.7 pad_maximum_fusion.w_proj_ref
  87.8 79.9 %all-gather.3.cloned.1.call-done.bias_ref = f32[4,768,768]{2,1,0:T(8,128)} async-done(((f32[4,24,768]{2,1,0:T(8,128)}), f32[4,768,768]{2,1,0:T(8,128)}) %all-gather.3.cloned.1.call-update) | async-done | bytes 9437200 | tf_op jit(solution)/shard_map/all_gather | solution.py:198
  167.6 0.0 copy-start.5
  167.6 104.8 %attend_next.1 = (bf16[24,768,128]{2,1,0:T(8,128)(2,1)}, bf16[24,768,128]{2,1,0:T(8,128)(2,1)}) custom-call(s32[24]{0:T(128)} %get-tuple-element.15.row_ok_ref, s32[1,768]{1,0:T(1,128)} %broadcast_in_dim.2.key_ok_ref, bf16[24,768,128]{2,1,0:T(8,128)(2,1)} %bitcast.55, f32[4,768,768]{2,1,0:T(8,128)} %all-gather.3.cloned.1.call-done.bias_ref, ...), custom_call_target="tpu_custom_call" | custom-call | flops 28991029248 | bytes 18874368 | tf_op jit(solution)/shard_map/attend_next/pallas_call | solution.py:143
  272.4 0.0 copy-done.5
  272.5 3.7 fusion.5
  276.1 0.8 copy.88
  276.9 0.0 all-gather.5.cloned.1.call-update
  276.9 5.4 copy.70
  282.3 75.2 %all_to_all.91 = bf16[24,768,128]{2,0,1:T(8,128)(2,1)S(1)} all-to-all(bf16[24,768,128]{2,0,1:T(8,128)(2,1)S(1)} %copy.70), channel_id=1, replica_groups=mesh['wide'=8,'narrow'=4] {'narrow'}, dimensions={1} | all-to-all | bytes 9437184 | tf_op jit(solution)/shard_map/all_to_all | solution.py:209
  357.5 1.2 copy.72
  358.7 5.3 copy.73
  364.0 6.7 all-to-all-start.3
  370.7 7.6 %copy.68 = bf16[24,768,128]{2,0,1:T(8,128)(2,1)} copy(bf16[24,768,128]{2,1,0:T(8,128)(2,1)} %get-tuple-element.4) | data formatting | bytes 9437184 | tf_op jit(solution)/shard_map/attend_next/pallas_call | solution.py:143
  378.2 0.0 copy-start.3
  378.2 96.6 %all-to-all-done.3 = bf16[192,96,128]{2,1,0:T(8,128)(2,1)} async-done(((bf16[192,96,128]{2,1,0:T(8,128)(2,1)}), bf16[192,96,128]{2,1,0:T(8,128)(2,1)}, u32[]{:S(2)}, u32[]{:S(2)}) %all-to-all-start.3) | async-done | bytes 4718624 | tf_op jit(solution)/shard_map/all_to_all | solution.py:210
  474.9 5.2 all-to-all-start.1
  480.1 0.0 copy-done.3
  480.1 0.1 copy.76
  480.3 0.1 copy.77
  480.4 0.1 copy.78
  480.5 0.1 copy.79
  480.6 0.1 copy.80
  480.7 0.7 pad_maximum_fusion.1.w_proj_ref
  481.5 5.9 copy.74
  487.3 0.0 all-gather.5.cloned.1.call-done.bias_ref
  487.3 95.9 %attend_last.1 = bf16[24,768,128]{2,1,0:T(8,128)(2,1)} custom-call(s32[24]{0:T(128)} %get-tuple-element.14.row_ok_ref, s32[1,768]{1,0:T(1,128)} %broadcast_in_dim.2.key_ok_ref, bf16[24,768,128]{2,1,0:T(8,128)(2,1)} %bitcast.57, f32[4,768,768]{2,1,0:T(8,128)} %all-gather.5.cloned.1.call-done.bias_ref, bf16[128,768]{1,0:T(8,128)(2,1)} %pad_maximum_fusion.1.w_proj_ref, ...), custom_call_target="tpu_custom_call" | custom-call | flops 28991029248 | bytes 18874368 | tf_op jit(solution)/shard_map/attend_last/pallas_call | solution.py:143
  583.3 7.5 %copy.81 = bf16[24,768,128]{2,0,1:T(8,128)(2,1)} copy(bf16[24,768,128]{2,1,0:T(8,128)(2,1)} %attend_last.1) | data formatting | bytes 9437184 | tf_op jit(solution)/shard_map/attend_last/pallas_call | solution.py:143
  590.8 0.0 all-to-all-done.1
  590.8 4.6 all-to-all-start.4
  595.4 5.8 copy.69
  601.2 99.1 %all-to-all-done.4 = bf16[24,768,128]{2,0,1:T(8,128)(2,1)} async-done(((bf16[24,768,128]{2,0,1:T(8,128)(2,1)}), bf16[24,768,128]{2,0,1:T(8,128)(2,1)}, u32[]{:S(2)}, u32[]{:S(2)}) %all-to-all-start.4) | async-done | bytes 4718624 | tf_op jit(solution)/shard_map/all_to_all | solution.py:217
  700.3 0.0 copy-start.1
  700.3 5.9 copy.82
  706.2 0.0 copy-done.1
  (7 shorter events, 0.1 us)
Async XLA Ops:
  7.2 69.5 %copy-start = (bf16[128,4]{0,1:T(4,128)(2,1)S(1)}, bf16[128,4]{0,1:T(4,128)(2,1)}, u32[]{:S(2)}) copy-start(bf16[128,4]{0,1:T(4,128)(2,1)} %param.11) | copy-start | bytes 3076
  7.2 160.4 %all-gather.3.cloned.1.call-start = ((), (), s32[]{:S(2)}) async-start(), calls=%async_computation.5 | async-start | bytes 9732096 | tf_op jit(solution)/shard_map/all_gather | solution.py:198
  76.5 8.6 %copy-start.2 = (bf16[128,512]{1,0:T(8,128)(2,1)S(1)}, bf16[128,512]{1,0:T(8,128)(2,1)}, u32[]{:S(2)}) copy-start(bf16[128,512]{1,0:T(8,128)(2,1)} %param.10) | copy-start | bytes 393220
  76.7 9.2 %copy-start.4 = (s32[768]{0:T(1024)S(1)}, s32[768]{0:T(1024)}, u32[]{:S(2)}) copy-start(s32[768]{0:T(1024)} %param.9) | copy-start | bytes 9220
  84.9 402.4 %all-gather.5.cloned.1.call-start = ((), (), s32[]{:S(2)}) async-start(), calls=%async_computation.6 | async-start | bytes 9732096 | tf_op jit(solution)/shard_map/all_gather | solution.py:208
  167.6 104.8 %copy-start.5 = (bf16[128,4]{0,1:T(4,128)(2,1)S(1)}, bf16[128,4]{0,1:T(4,128)(2,1)}, u32[]{:S(2)}) copy-start(bf16[128,4]{0,1:T(4,128)(2,1)} %param.14) | copy-start | bytes 3076
  364.0 110.8 %all-to-all-start.3 = ((bf16[192,96,128]{2,1,0:T(8,128)(2,1)}), bf16[192,96,128]{2,1,0:T(8,128)(2,1)}, u32[]{:S(2)}, u32[]{:S(2)}) async-start(bf16[192,96,128]{2,1,0:T(8,128)(2,1)} %copy.73), calls=%async_computation.3 | async-start | bytes 9437184 | tf_op jit(solution)/shard_map/all_to_all | solution.py:210
  378.2 101.9 %copy-start.3 = (bf16[128,512]{1,0:T(8,128)(2,1)S(1)}, bf16[128,512]{1,0:T(8,128)(2,1)}, u32[]{:S(2)}) copy-start(bf16[128,512]{1,0:T(8,128)(2,1)} %param.13) | copy-start | bytes 393220
  474.9 115.9 %all-to-all-start.1 = ((bf16[24,768,128]{2,0,1:T(8,128)(2,1)}), bf16[24,768,128]{2,0,1:T(8,128)(2,1)}, u32[]{:S(2)}, u32[]{:S(2)}) async-start(bf16[24,768,128]{2,0,1:T(8,128)(2,1)} %copy.68), calls=%async_computation.1 | async-start | bytes 9437184 | tf_op jit(solution)/shard_map/all_to_all | solution.py:203
  590.8 109.5 %all-to-all-start.4 = ((bf16[24,768,128]{2,0,1:T(8,128)(2,1)}), bf16[24,768,128]{2,0,1:T(8,128)(2,1)}, u32[]{:S(2)}, u32[]{:S(2)}) async-start(bf16[24,768,128]{2,0,1:T(8,128)(2,1)} %copy.81), calls=%async_computation.4 | async-start | bytes 9437184 | tf_op jit(solution)/shard_map/all_to_all | solution.py:217
  700.3 5.9 copy-start.1
Sparse Core Ops, SparseCore 0:
  85.1 82.5 all-gather.2
  277.0 94.7 all-gather.4

commit v2 on v0

v2 whole, which is shorter than its diff:
```python
import functools

import jax
import jax.numpy as jnp
from jax import lax
from jax.experimental import pallas as pl
from jax.experimental.pallas import tpu as pltpu
from jax.sharding import PartitionSpec as P


norm_eps = 1e-05
log2e = 1.4426950408889634
far_below = -1e30
lanes = 128
both_axes = ("wide", "narrow")


def params(megabytes=60):
    return pltpu.CompilerParams(
        dimension_semantics=("arbitrary",), vmem_limit_bytes=megabytes * 1024 * 1024
    )


def once(shape):
    return pl.BlockSpec(
        shape, lambda *_: (0,) * len(shape), pipeline_mode=pl.Buffered(1)
    )


def layer_norm(features):
    average = jnp.mean(features, axis=-1, keepdims=True)
    centred = features - average
    spread = jnp.mean(centred * centred, axis=-1, keepdims=True)
    return (centred * lax.rsqrt(spread + norm_eps)).astype(jnp.bfloat16)


def pack_projection(w_proj, head_count, head_dim):
    split = w_proj.reshape(w_proj.shape[0], head_count, 4, head_dim)
    twice = jnp.concatenate([split, split], axis=-1)
    parts = [twice[:, :, 1], split[:, :, 2], twice[:, :, 0], split[:, :, 3]]
    return jnp.concatenate([part.reshape(w_proj.shape[0], -1) for part in parts], axis=1)


def tile_bias_kernel(x_ref, w_ref, out_ref, *, head_count):
    for i in range(x_ref.shape[0]):
        normed = layer_norm(x_ref[i].astype(jnp.float32))
        got = lax.dot_general(
            w_ref[...], normed, (((1,), (1,)), ((), ())), preferred_element_type=jnp.float32
        )
        for h in range(head_count):
            out_ref[h, i : i + 1, :] = got[h : h + 1]


def tile_bias(tile, w_bias_rows, head_count):
    rows, cols, channels = tile.shape
    block = 8 if rows % 8 == 0 else rows
    return pl.pallas_call(
        functools.partial(tile_bias_kernel, head_count=head_count),
        out_shape=jax.ShapeDtypeStruct((head_count, rows, cols), jnp.float32),
        grid=(rows // block,),
        in_specs=[
            pl.BlockSpec((block, cols, channels), lambda i: (i, 0, 0)),
            once(w_bias_rows.shape),
        ],
        out_specs=pl.BlockSpec((head_count, block, cols), lambda i: (0, i, 0)),
        compiler_params=params(16),
        cost_estimate=pl.CostEstimate(
            flops=32 * tile.size, bytes_accessed=2 * tile.size, transcendentals=0
        ),
        name="tile_bias",
    )(tile, w_bias_rows)


def pack_tile_bias(part):
    rows, cols = part.shape[1:]
    main = cols // lanes * lanes
    left, right = part[:, :, :main], part[:, :, main:]
    half = rows // 2
    tail = jnp.concatenate([right[:, :half], right[:, half:]], axis=2)
    split = [left[:, :, at : at + lanes] for at in range(0, main, lanes)]
    return jnp.concatenate(split + [tail], axis=1)


def place_bias_kernel(key_ok_ref, got_ref, out_ref, *, rows, cols):
    main = cols // lanes
    half_lanes = lanes // 2
    low = lax.broadcasted_iota(jnp.int32, (1, lanes), 1) < half_lanes
    for n in range(0, got_ref.shape[0], 2):
        for h in range(got_ref.shape[1]):
            blocks = []
            even = [got_ref[n, h, b * rows : (b + 1) * rows] for b in range(main)]
            odd = [got_ref[n + 1, h, b * rows : (b + 1) * rows] for b in range(main)]
            even_tail = got_ref[n, h, main * rows :]
            odd_tail = got_ref[n + 1, h, main * rows :]
            even_last = jnp.concatenate(
                [even_tail, pltpu.roll(even_tail, half_lanes, 1)], axis=0
            )
            odd_last = jnp.concatenate([pltpu.roll(odd_tail, half_lanes, 1), odd_tail], axis=0)
            turned = [pltpu.roll(piece, half_lanes, 1) for piece in odd]
            blocks = list(even)
            before = even_last
            for piece in turned:
                blocks.append(jnp.where(low, before, piece))
                before = piece
            blocks.append(jnp.where(low, before, odd_last))
            for at, block in enumerate(blocks):
                lane = n * cols + at * lanes
                allowed = key_ok_ref[:, lane : lane + lanes] > 0
                out_ref[h, :, lane : lane + lanes] = jnp.where(allowed, block * log2e, far_below)


def place_bias(key_ok, gathered, wide_count, rows, cols):
    narrow_count = gathered.shape[0] // wide_count
    head_count = gathered.shape[1]
    length = wide_count * rows
    return pl.pallas_call(
        functools.partial(place_bias_kernel, rows=rows, cols=cols),
        out_shape=jax.ShapeDtypeStruct((head_count, length, length), jnp.float32),
        grid=(wide_count,),
        in_specs=[
            once((1, length)),
            pl.BlockSpec((narrow_count,) + gathered.shape[1:], lambda i: (i, 0, 0, 0)),
        ],
        out_specs=pl.BlockSpec((head_count, rows, length), lambda i: (0, i, 0)),
        compiler_params=params(16),
        cost_estimate=pl.CostEstimate(
            flops=gathered.size, bytes_accessed=8 * gathered.size, transcendentals=0
        ),
        name="place_bias",
    )(key_ok[None, :], gathered)


def turn_bias_kernel(key_ok_ref, got_ref, out_ref):
    queries = got_ref.shape[-1]
    plane = got_ref[:, 0, 0].reshape(-1, queries)
    allowed = key_ok_ref[...] > 0
    out_ref[0] = jnp.where(allowed, plane.T * log2e, far_below)


def turn_bias(key_ok, gathered, part):
    devices, _, head_count, rows, queries = gathered.shape
    length = devices * rows
    return pl.pallas_call(
        turn_bias_kernel,
        out_shape=jax.ShapeDtypeStruct((head_count, queries, length), jnp.float32),
        grid=(head_count,),
        in_specs=[
            once((1, length)),
            pl.BlockSpec((devices, 1, 1, rows, queries), lambda h: (0, part, h, 0, 0)),
        ],
        out_specs=pl.BlockSpec((1, queries, length), lambda h: (h, 0, 0)),
        compiler_params=params(),
        cost_estimate=pl.CostEstimate(
            flops=gathered.size, bytes_accessed=8 * gathered.size, transcendentals=0
        ),
        name="turn_bias",
    )(key_ok[None, :], gathered)


def lines_per_step(count, most):
    return max(per for per in range(1, most + 1) if count % per == 0)


def project_kernel(x_ref, w_ref, *rest, head_count, head_dim, normalise, strided):
    out_ref, scratch = (rest[-2], rest[-1]) if strided else (rest[-1], None)
    width = head_count * head_dim
    pair = 2 * width
    channels = x_ref.shape[-1]
    per = out_ref.shape[0]
    if strided:
        stride = x_ref.shape[1]

        @pl.when(pl.program_id(0) == 0)
        def _():
            scratch[...] = x_ref[...].astype(jnp.float32).reshape(scratch.shape)

    for i in range(per):
        if strided:
            at = pl.program_id(0) * per + i
            normed = scratch[pl.ds(at, x_ref.shape[0], stride=stride), :].astype(jnp.bfloat16)
        elif normalise:
            normed = layer_norm(x_ref[:, i].reshape(-1, channels).astype(jnp.float32))
        else:
            normed = x_ref[i]
        projected = jnp.dot(normed, w_ref[...], preferred_element_type=jnp.float32).astype(
            jnp.bfloat16
        )
        first = pair + width
        queries = projected[:, first : first + pair].astype(jnp.float32)
        queries = queries * (head_dim ** (-0.5) * log2e)
        upper = queries.astype(jnp.bfloat16)
        lower = (queries - upper.astype(jnp.float32)).astype(jnp.bfloat16)
        spot = lax.broadcasted_iota(jnp.int32, (1, pair), 1)
        queries = jnp.where(spot % (2 * head_dim) < head_dim, upper, lower)
        for block in range(projected.shape[1] // lanes):
            at = block * lanes
            if first <= at < first + pair:
                out_ref[i, block] = queries[:, at - first : at - first + lanes]
            else:
                out_ref[i, block] = projected[:, at : at + lanes]


def project(lines, packed, head_count, head_dim, kind, before=None, first=0, total=None):
    channels = lines.shape[-1]
    scratch = []
    if kind == "rows":
        pieces, count, cols = lines.shape[:3]
        length = pieces * cols
        per = lines_per_step(count, 2)
        spec = pl.BlockSpec((pieces, per, cols, channels), lambda i: (0, i, 0, 0))
    elif kind == "columns":
        length, count = lines.shape[:2]
        per = lines_per_step(count, 2)
        spec = once(lines.shape)
        scratch = [pltpu.VMEM((length * count, channels), jnp.float32)]
    else:
        count, length = lines.shape[:2]
        per = 1
        spec = pl.BlockSpec((1, length, channels), lambda i: (i, 0, 0))
    outs = packed.shape[1]
    total = count if total is None else total
    in_specs, operands, aliases = [spec, once(packed.shape)], [lines, packed], {}
    if before is not None:
        in_specs.append(pl.BlockSpec(memory_space=pl.ANY))
        operands.append(before)
        aliases = {2: 0}
    skip = first // per
    return pl.pallas_call(
        functools.partial(
            project_kernel,
            head_count=head_count,
            head_dim=head_dim,
            normalise=kind == "rows",
            strided=kind == "columns",
        ),
        out_shape=jax.ShapeDtypeStruct((total, outs // lanes, length, lanes), jnp.bfloat16),
        grid=(count // per,),
        in_specs=in_specs,
        out_specs=pl.BlockSpec((per, outs // lanes, length, lanes), lambda i: (i + skip, 0, 0, 0)),
        scratch_shapes=scratch,
        input_output_aliases=aliases,
        compiler_params=params(),
        cost_estimate=pl.CostEstimate(
            flops=2 * lines.size * outs,
            bytes_accessed=2 * lines.size * (1 + outs // channels),
            transcendentals=0,
        ),
    )(*operands)


def attend_lines(query_ref, key_ref, bias_refs, oks, head_count, head_dim):
    width = head_count * head_dim
    pair_blocks = 2 * width // lanes
    length = key_ref.shape[2]
    local = lax.broadcasted_iota(jnp.int32, (1, lanes), 1) // (2 * head_dim)
    owner = lax.broadcasted_iota(jnp.int32, (1, width), 1) // head_dim
    block_heads = lanes // (2 * head_dim)
    nothing = jnp.zeros((), jnp.bfloat16)
    jobs = [
        (i, at, h)
        for i in range(key_ref.shape[0])
        for at in range(len(bias_refs))
        for h in range(head_count)
    ]

    def score(job):
        i, at, h = job
        block = h // block_heads
        queries = query_ref[i, block, :, at].reshape(-1, lanes)
        return lax.dot_general(
            jnp.where(local == h % block_heads, queries, nothing),
            key_ref[i, block],
            (((1,), (1,)), ((), ())),
            preferred_element_type=jnp.float32,
        )

    def together(ref, i, first, *rest):
        parts = [ref[(i, first + n) + rest] for n in range(width // lanes)]
        parts = [part.reshape(-1, lanes) for part in parts]
        return parts[0] if len(parts) == 1 else jnp.concatenate(parts, axis=1)

    gated = {}
    summed = None
    coming = score(jobs[0])
    for n, (i, at, h) in enumerate(jobs):
        scores = coming
        if n + 1 < len(jobs):
            coming = score(jobs[n + 1])
        scores = scores + bias_refs[at][h].reshape(-1, length)
        top = jnp.max(scores, axis=-1, keepdims=True)
        weights = jnp.exp2(scores - top).astype(jnp.bfloat16)
        values = together(key_ref, i, pair_blocks)
        values_ones = jnp.concatenate([values, jnp.ones_like(values)], axis=1)
        both_sums = jnp.dot(weights, values_ones, preferred_element_type=jnp.float32)
        ratio = both_sums[:, :width] / both_sums[:, width:]
        summed = ratio if h == 0 else jnp.where(owner == h, ratio, summed)
        if h == head_count - 1:
            even = jnp.full((), 1.0 / length, jnp.float32).astype(jnp.bfloat16)
            total = jnp.sum(values.astype(jnp.float32), axis=0, keepdims=True)
            final = jnp.where(oks[i], summed, total * even.astype(jnp.float32))
            gates = together(query_ref, i, pair_blocks, slice(None), at).astype(jnp.float32)
            gated[i, at] = (jax.nn.sigmoid(gates) * final).astype(jnp.bfloat16)
    return gated


def out_of(gated, w_out_ref):
    return jnp.dot(gated, w_out_ref[...], preferred_element_type=jnp.float32).astype(jnp.bfloat16)


def attend_rows_kernel(
    row_ok_ref, query_ref, key_ref, bias_ref, w_out_ref, x_ref, w_bias_ref, *rest, **sizes
):
    upd_ref, next_ref, nbias_ref = rest[-3:]
    per = key_ref.shape[0]
    lines = [pl.program_id(0) * per + i for i in range(per)]
    oks = [row_ok_ref[line] > 0 for line in lines]
    gated = attend_lines(query_ref, key_ref, [bias_ref], oks, **sizes)
    for i in range(per):
        update = out_of(gated[i, 0], w_out_ref)
        upd_ref[:, i] = update.reshape(upd_ref.shape[0], *upd_ref.shape[2:])
        features = x_ref[:, i].reshape(-1, x_ref.shape[-1]).astype(jnp.float32)
        normed = layer_norm(features + update.astype(jnp.float32))
        got = lax.dot_general(
            w_bias_ref[...], normed, (((1,), (1,)), ((), ())), preferred_element_type=jnp.float32
        )
        for h in range(nbias_ref.shape[0]):
            nbias_ref[h, pl.ds(lines[i], 1), :] = got[h : h + 1]
        if len(next_ref.shape) == 4:
            devices, _, cols, channels = next_ref.shape
            narrow_count = upd_ref.shape[0]
            spread = normed.astype(jnp.float32).reshape(
                narrow_count, devices // narrow_count, cols, channels
            )
            spread = spread.transpose(1, 0, 2, 3).reshape(devices, cols, channels)
            next_ref[:, i] = spread.astype(jnp.bfloat16)
        else:
            next_ref[i] = normed


def line_specs(projected, plan, per, first, parts, skip):
    blocks, chunks, piece = plan[:3]
    total, lane_blocks, length, _ = projected.shape
    half = lane_blocks // 2
    cut = projected.reshape(total, lane_blocks, blocks, chunks, piece, lanes)
    at = first // parts
    specs = [
        pl.BlockSpec(
            (per, half, blocks, parts, piece, lanes), lambda i, ok: (i + skip, 1, 0, at, 0, 0)
        ),
        pl.BlockSpec((per, half, length, lanes), lambda i, ok: (i + skip, 0, 0, 0)),
    ]
    return specs, [cut, projected]


def attend_rows(row_ok, projected, lines, bias, w_out, w_bias_rows, chunk, before, plan):
    blocks, chunks, piece, own, wide_count = plan
    pieces, count, cols, channels = lines.shape
    length = pieces * cols
    head_count = bias.shape[0]
    width = w_out.shape[0]
    head_dim = width // head_count
    direct = own % 8 == 0
    inner = blocks // pieces
    x_cut = lines.reshape(pieces, count, inner, chunks, piece, channels)
    bias_cut = bias.reshape(head_count, blocks, chunks, piece, length)
    per = lines_per_step(count, 2)
    queries = blocks * piece
    line_block = pl.BlockSpec(
        (pieces, per, inner, None, piece, channels), lambda i, ok: (0, i, 0, chunk, 0, 0)
    )
    if direct:
        next_shape = (wide_count * pieces, count, own, channels)
        next_spec = pl.BlockSpec(
            (wide_count * pieces, per, own, channels), lambda i, ok: (0, i, 0, 0)
        )
    else:
        next_shape = (count, queries, channels)
        next_spec = pl.BlockSpec((per, queries, channels), lambda i, ok: (i, 0, 0))
    nbias_shape = (head_count, count, queries)
    scores = count * head_count * length * queries
    in_specs, operands = line_specs(projected, plan, per, chunk, 1, 0)
    in_specs += [
        pl.BlockSpec(
            (head_count, blocks, None, piece, length),
            lambda i, ok: (0, 0, chunk, 0, 0),
            pipeline_mode=pl.Buffered(1),
        ),
        once(w_out.shape),
        line_block,
        once(w_bias_rows.shape),
    ]
    operands += [bias_cut, w_out, x_cut, w_bias_rows]
    aliases = {}
    if before is not None:
        in_specs.append(pl.BlockSpec(memory_space=pl.ANY))
        operands.append(before)
        aliases = {len(operands): 0}
    upd, nxt, nbias = pl.pallas_call(
        functools.partial(attend_rows_kernel, head_count=head_count, head_dim=head_dim),
        out_shape=[
            jax.ShapeDtypeStruct(x_cut.shape, jnp.bfloat16),
            jax.ShapeDtypeStruct(next_shape, jnp.bfloat16),
            jax.ShapeDtypeStruct(nbias_shape, jnp.float32),
        ],
        grid_spec=pltpu.PrefetchScalarGridSpec(
            num_scalar_prefetch=1,
            grid=(count // per,),
            in_specs=in_specs,
            out_specs=[line_block, next_spec, pl.BlockSpec(nbias_shape, lambda i, ok: (0, 0, 0))],
        ),
        input_output_aliases=aliases,
        compiler_params=params(),
        cost_estimate=pl.CostEstimate(
            flops=4 * scores * 128, bytes_accessed=8 * lines.size, transcendentals=scores
        ),
        name="attend_rows",
    )(row_ok, *operands)
    if not direct:
        nxt = nxt.reshape(count, pieces, wide_count, own, channels).transpose(2, 1, 0, 3, 4)
        nxt = nxt.reshape(wide_count * pieces, count, own, channels)
    return upd, nxt, nbias


def attend_columns_kernel(col_ok_ref, query_ref, key_ref, *rest, parts, **sizes):
    bias_refs, w_out_ref, out_ref = rest[:parts], rest[parts], rest[parts + 1]
    scratch = rest[parts + 2 :]
    per = key_ref.shape[0]
    blocks, piece = query_ref.shape[2], query_ref.shape[4]
    lines = [pl.program_id(0) * per + i for i in range(per)]
    oks = [col_ok_ref[line] > 0 for line in lines]
    gated = attend_lines(query_ref, key_ref, bias_refs, oks, **sizes)
    for i in range(per):
        for at in range(parts):
            update = out_of(gated[i, at], w_out_ref)
            if not scratch:
                out_ref[:, i] = update.reshape(blocks, piece, update.shape[1])
                continue
            stride = out_ref.shape[2]
            for m in range(blocks):
                first = (m * parts + at) * piece * stride + lines[i]
                scratch[0][pl.ds(first, piece, stride=stride), :] = update[
                    m * piece : (m + 1) * piece
                ].astype(jnp.float32)
    if scratch:

        @pl.when(pl.program_id(0) == pl.num_programs(0) - 1)
        def _():
            out_ref[...] = scratch[0][...].reshape(out_ref.shape).astype(jnp.bfloat16)


def attend_columns(col_ok, projected, biases, w_out, first, skip, plan):
    blocks, _, piece, own, _ = plan
    length = projected.shape[2]
    count = col_ok.shape[0]
    parts = len(biases)
    head_count = biases[0].shape[0]
    width = w_out.shape[0]
    head_dim = width // head_count
    scores = count * head_count * length * blocks * parts * piece
    per = lines_per_step(count, 2) if parts == 1 else 1
    if own % 8 == 0:
        out_shape = (blocks, parts * piece, count, width)
        out_spec = pl.BlockSpec(out_shape, lambda i, ok: (0, 0, 0, 0))
        scratch = [pltpu.VMEM((blocks * parts * piece * count, width), jnp.float32)]
    else:
        out_shape = (blocks, count, parts * piece, width)
        out_spec = pl.BlockSpec((blocks, per, parts * piece, width), lambda i, ok: (0, i, 0, 0))
        scratch = []
    in_specs, operands = line_specs(projected, plan, per, first, parts, skip // per)
    return pl.pallas_call(
        functools.partial(
            attend_columns_kernel, parts=parts, head_count=head_count, head_dim=head_dim
        ),
        out_shape=jax.ShapeDtypeStruct(out_shape, jnp.bfloat16),
        grid_spec=pltpu.PrefetchScalarGridSpec(
            num_scalar_prefetch=1,
            grid=(count // per,),
            in_specs=in_specs + [once(biases[0].shape)] * parts + [once(w_out.shape)],
            out_specs=out_spec,
            scratch_shapes=scratch,
        ),
        compiler_params=params(),
        cost_estimate=pl.CostEstimate(
            flops=4 * scores * 128, bytes_accessed=8 * count * length * width, transcendentals=scores
        ),
        name="attend_columns",
    )(col_ok, *operands, *biases, w_out)


def settle_kernel(*refs, order, plan):
    _, chunks, piece, own, wide_count = plan
    tile_rows = chunks * piece
    out_ref = refs[-1]
    for step, j in enumerate(order):
        ref, first = (refs[0], step * own) if len(refs) < chunks else (refs[step], 0)
        for w in range(wide_count):
            inner, within = divmod(w * own, piece)
            col = inner * tile_rows + j * piece + within
            out_ref[:, col : col + own, :] = ref[w, :, first : first + own, :]


def settle(parts, first_row, before, order, plan, shape):
    wide_count, rows, _, _ = parts[0].shape
    block = 16
    skip = first_row // block
    in_specs = [
        pl.BlockSpec((wide_count, block) + part.shape[2:], lambda i: (0, i, 0, 0))
        for part in parts
    ]
    operands, aliases = list(parts), {}
    if before is not None:
        in_specs.append(pl.BlockSpec(memory_space=pl.ANY))
        operands.append(before)
        aliases = {len(parts): 0}
    return pl.pallas_call(
        functools.partial(settle_kernel, order=order, plan=plan),
        out_shape=jax.ShapeDtypeStruct(shape, jnp.bfloat16),
        grid=(rows // block,),
        in_specs=in_specs,
        out_specs=pl.BlockSpec((block,) + shape[1:], lambda i: (i + skip, 0, 0)),
        input_output_aliases=aliases,
        compiler_params=params(),
        cost_estimate=pl.CostEstimate(
            flops=0, bytes_accessed=4 * parts[0].size * len(parts), transcendentals=0
        ),
        name="settle",
    )(*operands)


def bias_rows_of(w_bias):
    turned = w_bias.T
    return jnp.pad(turned, ((0, 16 - turned.shape[0]), (0, 0)))


def on_device(
    pair_act,
    residue_mask,
    w_proj_start,
    w_bias_start,
    w_out_start,
    w_proj_end,
    w_bias_end,
    w_out_end,
):
    wide_count = lax.axis_size("wide")
    narrow_count = lax.axis_size("narrow")
    wide_at = lax.axis_index("wide")
    narrow_at = lax.axis_index("narrow")
    tile_rows, tile_cols, channels = pair_act.shape
    head_count = w_bias_start.shape[1]
    head_dim = w_out_start.shape[0] // head_count
    length = wide_count * tile_rows
    row_count = tile_rows // narrow_count
    chunks = 1
    if tile_cols % tile_rows == 0:
        for tried in (3, 2):
            if tile_rows % (16 * tried) == 0 and tile_cols % (8 * tried * wide_count) == 0:
                chunks = tried
                break
    piece = tile_rows // chunks
    own = tile_cols // chunks // wide_count
    plan = (wide_count, chunks, piece, own, wide_count)
    key_ok = (residue_mask > 0).astype(jnp.int32)

    part = tile_bias(pair_act, bias_rows_of(w_bias_start), head_count)
    dense = tile_cols % lanes == lanes // 2 and tile_rows % 16 == 0 and narrow_count % 2 == 0
    if dense:
        part = pack_tile_bias(part)
    gathered = lax.all_gather(part, both_axes, axis=0, tiled=False)
    tile_in, part = lax.optimization_barrier((pair_act, part))
    lines = lax.all_to_all(
        tile_in.reshape(narrow_count, row_count, tile_cols, channels),
        "narrow",
        split_axis=0,
        concat_axis=0,
        tiled=True,
    )
    packed_start = pack_projection(w_proj_start, head_count, head_dim)
    projected = project(lines, packed_start, head_count, head_dim, "rows")
    if dense:
        bias = place_bias(key_ok, gathered, wide_count, tile_rows, tile_cols)
    else:
        bias = gathered.reshape(wide_count, narrow_count, head_count, tile_rows, tile_cols)
        bias = bias.transpose(2, 0, 3, 1, 4).reshape(head_count, length, length)
        bias = jnp.where(key_ok > 0, bias * log2e, far_below)

    row_ok = lax.dynamic_slice_in_dim(
        key_ok, wide_at * tile_rows + narrow_at * row_count, row_count
    )
    w_bias_rows = bias_rows_of(w_bias_end)
    order = [chunks - 1] + list(range(chunks - 1))
    columns, waiting, next_biases = {}, [], {}
    upd = None
    for step, j in enumerate(order):
        upd, nxt, nbias = attend_rows(
            row_ok, projected, lines, bias, w_out_start, w_bias_rows, j, upd, plan
        )
        waiting.append((j, nbias))
        if step in (0, chunks - 1):
            got = lax.all_gather(
                jnp.stack([nbias for _, nbias in waiting]), both_axes, axis=0, tiled=False
            )
            for n, (k, _) in enumerate(waiting):
                if row_count % 8 == 0:
                    turned = turn_bias(key_ok, got, n)
                else:
                    turned = got[:, n].transpose(1, 3, 0, 2).reshape(head_count, -1, length)
                    turned = jnp.where(key_ok > 0, turned * log2e, far_below)
                next_biases[k] = turned
            waiting = []
        got = lax.all_to_all(nxt, both_axes, split_axis=0, concat_axis=0, tiled=True)
        columns[j] = got.reshape(length, own, channels)
    mine = upd.reshape(narrow_count, row_count, tile_cols, channels)
    leaving = [
        lax.dynamic_index_in_dim(mine, (narrow_at + k) % narrow_count, 0)
        for k in range(1, narrow_count)
    ]
    leaving, mine = lax.optimization_barrier((leaving, mine))
    arrived = []
    for k in range(1, narrow_count):
        ring = [(n, (n + k) % narrow_count) for n in range(narrow_count)]
        arrived.append(lax.ppermute(leaving[k - 1], "narrow", ring))
    update_start = mine
    for k, got in enumerate(arrived, 1):
        source = (narrow_at + narrow_count - k) % narrow_count
        update_start = lax.dynamic_update_slice_in_dim(update_start, got, source, 0)
    update_start = update_start.reshape(tile_rows, tile_cols, channels)

    packed_end = pack_projection(w_proj_end, head_count, head_dim)
    projected_end, col_ok = None, []
    for step, j in enumerate(order):
        lines_end = columns[j]
        if own % 8:
            lines_end = lines_end.transpose(1, 0, 2)
        projected_end = project(
            lines_end,
            packed_end,
            head_count,
            head_dim,
            "plain" if own % 8 else "columns",
            projected_end,
            step * own,
            chunks * own,
        )
        at = wide_at * own + jnp.arange(own)
        at = narrow_at * tile_cols + at // piece * tile_rows + j * piece + at % piece
        col_ok.append(key_ok[at])

    got = attend_columns(
        jnp.concatenate(col_ok),
        projected_end,
        [next_biases[order[0]]],
        w_out_end,
        order[0],
        0,
        plan,
    )
    got = lax.all_to_all(got, "wide", split_axis=0, concat_axis=0, tiled=True)
    if chunks == 1:
        return (update_start, got.transpose(2, 0, 1, 3).reshape(pair_act.shape))
    settled = settle([got], (chunks - 1) * piece, None, order, plan, pair_act.shape)
    late = []
    for step, j in enumerate(order):
        got = attend_columns(
            col_ok[step],
            projected_end,
            [next_biases[k] for k in range(chunks - 1)],
            w_out_end,
            0,
            step * own,
            plan,
        )
        late.append(lax.all_to_all(got, "wide", split_axis=0, concat_axis=0, tiled=True))
    return (update_start, settle(late, 0, settled, order, plan, pair_act.shape))


def solution(mesh):
    in_specs = (P("wide", "narrow", None), P(), P(), P(), P(), P(), P(), P())
    out_specs = (P("wide", "narrow", None), P("wide", "narrow", None))
    return jax.shard_map(
        on_device, mesh=mesh, in_specs=in_specs, out_specs=out_specs, check_vma=False
    )
```

time: 1740 us -> 580 us (0.33)
  matrix products: 707 us -> 0 us
  local copies, waits for them, and re-layouts: 359 us -> 22.4 us
  Pallas kernels: 0 us -> 290 us
  blocking collectives: 333 us -> 53.6 us
  other arithmetic: 145 us -> 4.57 us
  starting transfers between devices: 0.33 us -> 31.9 us
    dot_general x102 -> x0, matrix products: 707 us -> none  [the longest x48 426 us: one_row(): jnp.einsum('hbk,khd->bhd', weights, values, preferred_element_type=jnp.fl...]
    pallas_call x0 -> x18, Pallas kernels: none -> 290 us  [the longest x3 111 us: attend_rows(): pl.pallas_call(functools.partial(attend_rows_kernel, head_count=head_coun...]
    all_to_all x4 -> x1, blocking collectives: 333 us -> 53.6 us  [on_device(): lax.all_to_all(nxt, both_axes, split_axis=0, concat_axis=0, tiled=True)]
    while x98 -> x0, local copies, waits for them, and re-layouts: 198 us -> none
    all_gather x3, waiting for transfers between devices: 170 us -> 3.1 us  [the longest x1 3.08 us: on_device(): gathered = lax.all_gather(part, both_axes, axis=0, tiled=False)]
    all_to_all x0 -> x7, waiting for transfers between devices: none -> 110 us  [the longest x1 67.4 us: on_device(): lax.all_to_all(tile_in.reshape(narrow_count, row_count, tile_cols, channe...]
    dynamic_slice x145 -> x2, local copies, waits for them, and re-layouts: 100 us -> 2.83 us  [the longest x1 2.21 us: on_device(): lax.dynamic_index_in_dim(mine, (narrow_at + k) % narrow_count, 0)]
    sub x48 -> x0, other arithmetic: 79.9 us -> none  [one_row(): weights = jax.nn.softmax(scores, axis=-1).astype(jnp.bfloat16)]
  transfers between devices with their start and end apart: 3 -> 13, of which waited for: 3 -> 10; matrix products, arithmetic and copies ran while one was open for 2% -> 2% of each run, Pallas kernels for 0% -> 41%
where the time goes in v2:
time: 580 us; the launch traced here: 577 us
  Pallas kernels  290 us (50%)
  waiting for transfers between devices  160 us (28%)
  blocking collectives  53.6 us (9%)
  starting transfers between devices  31.9 us (6%)
  local copies, waits for them, and re-layouts  22.4 us (4%)
  between operations  14.1 us (2%)
    pallas_call x3, Pallas kernels, attend_rows(): pl.pallas_call(functools.partial(attend_rows_kernel, head_count=head_coun...  111 us
    pallas_call x4, Pallas kernels, attend_columns(): pl.pallas_call(functools.partial(attend_columns_kernel, parts=parts, head...  108 us
    all_to_all x1, waiting for transfers between devices, on_device(): lax.all_to_all(tile_in.reshape(narrow_count, row_count, tile_cols, channe...  67.4 us
    all_to_all x1, blocking collectives, on_device(): lax.all_to_all(nxt, both_axes, split_axis=0, concat_axis=0, tiled=True)  53.6 us
    ppermute x3, waiting for transfers between devices, on_device(): arrived.append(lax.ppermute(leaving[k - 1], 'narrow', ring))  47.4 us
    pallas_call x4, Pallas kernels, project(): pl.pallas_call(functools.partial(project_kernel, head_count=head_count, h...  39.7 us
    all_to_all x2, waiting for transfers between devices, on_device(): lax.all_to_all(nxt, both_axes, split_axis=0, concat_axis=0, tiled=True)  36.8 us
    pallas_call x3, Pallas kernels, turn_bias(): pl.pallas_call(turn_bias_kernel, out_shape=jax.ShapeDtypeStruct((head_cou...  13.9 us
  transfers between devices with their start and end apart: 13, of which 10 were waited for; matrix products, arithmetic and copies ran while one was open for 2% of the time, Pallas kernels for 41%

profile of v2, /device:TPU:0, one launch (start us, length us, event | category | flops | bytes accessed | tf_op | source)
XLA Modules:
  0.0 577.5 jit_solution(2813876180139223407)
XLA Ops:
  7.2 0.7 pad.7.w_ref
  7.9 2.3 copy-done.1
  10.2 8.0 %tile_bias.1 = f32[4,96,192]{2,1,0:T(8,128)S(1)} custom-call(bf16[96,192,128]{2,1,0:T(8,128)(2,1)S(1)} %copy-done.1, bf16[16,128]{1,0:T(8,128)(2,1)S(1)} %pad.7.w_ref), custom_call_target="tpu_custom_call" | custom-call | flops 75497472 | bytes 4718592 | tf_op jit(solution)/shard_map/tile_bias/pallas_call | solution.py:57
  18.3 0.8 maximum_maximum_fusion
  19.2 5.1 all-to-all-start
  24.4 0.6 dynamic_slice.13.row_ok_ref
  25.0 0.1 copy.33
  25.4 0.1 copy.35
  25.5 0.1 copy.34
  25.6 0.6 pad.8.w_bias_ref
  26.2 0.7 pad_maximum_fusion.w_ref
  26.9 67.4 %all-to-all-done.x_ref = bf16[4,24,192,128]{3,2,1,0:T(8,128)(2,1)} async-done(((bf16[4,24,192,128]{3,2,1,0:T(8,128)(2,1)}), bf16[4,24,192,128]{3,2,1,0:T(8,128)(2,1)}, u32[]{:S(2)}, u32[]{:S(2)}) %all-to-all-start) | async-done | bytes 4718624 | tf_op jit(solution)/shard_map/all_to_all | solution.py:571
  94.4 19.1 %shard_map.95.key_ref = bf16[24,6,768,128]{3,2,1,0:T(8,128)(2,1)} custom-call(bf16[4,24,192,128]{3,2,1,0:T(8,128)(2,1)} %all-to-all-done.x_ref, bf16[128,768]{1,0:T(8,128)(2,1)} %pad_maximum_fusion.w_ref), custom_call_target="tpu_custom_call" | custom-call | flops 3623878656 | bytes 33030144 | tf_op jit(solution)/shard_map/pallas_call | solution.py:228
  113.5 3.1 all-gather.7.cloned.1.call-done
  116.6 3.7 copy-done.2
  120.3 3.0 place_bias.1
  123.3 3.7 copy-done
  127.0 36.9 %attend_rows.3 = (bf16[4,24,2,3,32,128]{5,4,3,2,1,0:T(8,128)(2,1)}, bf16[32,24,8,128]{3,2,1,0:T(8,128)(2,1)}, f32[4,24,256]{2,1,0:T(8,128)}) custom-call(s32[24]{0:T(128)} %dynamic_slice.13.row_ok_ref, bf16[24,6,8,3,32,128]{5,4,3,2,1,0:T(8,128)(2,1)} %bitcast.42, bf16[24,6,768,128]{3,2,1,0:T(8,128)(2,1)} %shard_map.95.key_ref, ...), custom_call_target="tpu_custom_call" | custom-call | flops 9663676416 | bytes 18874368 | tf_op jit(solution)/shard_map/attend_rows/pallas_call | solution.py:398
  163.9 36.9 %attend_rows.4 = (bf16[4,24,2,3,32,128]{5,4,3,2,1,0:T(8,128)(2,1)}, bf16[32,24,8,128]{3,2,1,0:T(8,128)(2,1)}, f32[4,24,256]{2,1,0:T(8,128)}) custom-call(s32[24]{0:T(128)} %dynamic_slice.13.row_ok_ref, bf16[24,6,8,3,32,128]{5,4,3,2,1,0:T(8,128)(2,1)} %bitcast.43, bf16[24,6,768,128]{3,2,1,0:T(8,128)(2,1)} %shard_map.95.key_ref, ...), custom_call_target="tpu_custom_call", output_to_operand_aliasing={{0}: (7, {})} | custom-call | flops 9663676416 | bytes 18874368 | tf_op jit(solution)/shard_map/attend_rows/pallas_call | solution.py:398
  200.8 3.3 all-to-all-start.2
  204.2 37.1 %attend_rows.5 = (bf16[4,24,2,3,32,128]{5,4,3,2,1,0:T(8,128)(2,1)}, bf16[32,24,8,128]{3,2,1,0:T(8,128)(2,1)}, f32[4,24,256]{2,1,0:T(8,128)}) custom-call(s32[24]{0:T(128)} %dynamic_slice.13.row_ok_ref, bf16[24,6,8,3,32,128]{5,4,3,2,1,0:T(8,128)(2,1)} %bitcast.44, bf16[24,6,768,128]{3,2,1,0:T(8,128)(2,1)} %shard_map.95.key_ref, ...), custom_call_target="tpu_custom_call", output_to_operand_aliasing={{0}: (7, {})} | custom-call | flops 9663676416 | bytes 18874368 | tf_op jit(solution)/shard_map/attend_rows/pallas_call | solution.py:398
  241.3 1.6 pad_maximum_fusion.2
  243.0 7.0 %all-to-all-done.2 = bf16[32,24,8,128]{3,2,1,0:T(8,128)(2,1)S(1)} async-done(((bf16[32,24,8,128]{3,2,1,0:T(8,128)(2,1)}), bf16[32,24,8,128]{3,2,1,0:T(8,128)(2,1)S(1)}, u32[]{:S(2)}, u32[]{:S(2)}) %all-to-all-start.2) | async-done | bytes 1572896 | tf_op jit(solution)/shard_map/all_to_all | solution.py:611
  250.0 53.6 %all_to_all.40 = bf16[32,24,8,128]{3,2,1,0:T(8,128)(2,1)} all-to-all(bf16[32,24,8,128]{3,2,1,0:T(8,128)(2,1)S(1)} %copy-done.10), channel_id=1, replica_groups=mesh['wide'=8,'narrow'=4] {'wide','narrow'}, dimensions={0} | all-to-all | bytes 3145728 | tf_op jit(solution)/shard_map/all_to_all | solution.py:611
  303.6 3.4 all-to-all-start.1
  307.0 0.6 gather_fusion
  307.7 0.1 copy.38
  307.8 0.1 copy.42
  308.2 0.1 copy.39
  308.3 0.6 gather_fusion.1
  309.0 0.6 gather_fusion.2
  309.6 0.6 pad_add_fusion.col_ok_ref
  310.3 0.7 pad_maximum_fusion.1.w_ref
  311.0 6.9 %shard_map.96.rest_0_ = bf16[24,6,768,128]{3,2,1,0:T(8,128)(2,1)} custom-call(bf16[768,8,128]{2,1,0:T(8,128)(2,1)} %bitcast.50, bf16[128,768]{1,0:T(8,128)(2,1)} %pad_maximum_fusion.1.w_ref), custom_call_target="tpu_custom_call" | custom-call | flops 1207959552 | bytes 11010048 | tf_op jit(solution)/shard_map/pallas_call | solution.py:228
  317.9 6.9 %shard_map.97.rest_0_ = bf16[24,6,768,128]{3,2,1,0:T(8,128)(2,1)} custom-call(bf16[768,8,128]{2,1,0:T(8,128)(2,1)} %bitcast.51, bf16[128,768]{1,0:T(8,128)(2,1)} %pad_maximum_fusion.1.w_ref, bf16[24,6,768,128]{3,2,1,0:T(8,128)(2,1)} %shard_map.96.rest_0_), custom_call_target="tpu_custom_call", output_to_operand_aliasing={{}: (2, {})} | custom-call | flops 1207959552 | bytes 11010048 | tf_op jit(solution)/shard_map/pallas_call | solution.py:228
  324.7 29.9 %all-to-all-done.1 = bf16[32,24,8,128]{3,2,1,0:T(8,128)(2,1)S(1)} async-done(((bf16[32,24,8,128]{3,2,1,0:T(8,128)(2,1)}), bf16[32,24,8,128]{3,2,1,0:T(8,128)(2,1)S(1)}, u32[]{:S(2)}, u32[]{:S(2)}) %all-to-all-start.1) | async-done | bytes 1572896 | tf_op jit(solution)/shard_map/all_to_all | solution.py:611
  354.6 1.1 copy-done.6
  355.7 6.8 %shard_map.98.key_ref = bf16[24,6,768,128]{3,2,1,0:T(8,128)(2,1)} custom-call(bf16[768,8,128]{2,1,0:T(8,128)(2,1)} %bitcast.52, bf16[128,768]{1,0:T(8,128)(2,1)} %pad_maximum_fusion.1.w_ref, bf16[24,6,768,128]{3,2,1,0:T(8,128)(2,1)} %shard_map.97.rest_0_), custom_call_target="tpu_custom_call", output_to_operand_aliasing={{}: (2, {})} | custom-call | flops 1207959552 | bytes 11010048 | tf_op jit(solution)/shard_map/pallas_call | solution.py:228
  362.5 4.6 turn_bias.5.rest_0_
  367.2 33.9 %attend_columns.7 = bf16[8,32,24,128]{3,2,1,0:T(8,128)(2,1)} custom-call(s32[24]{0:T(128)} %pad_add_fusion.col_ok_ref, bf16[24,6,8,3,32,128]{5,4,3,2,1,0:T(8,128)(2,1)} %bitcast.38, bf16[24,6,768,128]{3,2,1,0:T(8,128)(2,1)} %shard_map.98.key_ref, f32[4,256,768]{2,1,0:T(8,128)} %turn_bias.5.rest_0_, bf16[128,128]{1,0:T(8,128)(2,1)} %rest_1_.1), custom_call_target="tpu_custom_call" | custom-call | flops 9663676416 | bytes 18874368 | tf_op jit(solution)/shard_map/attend_columns/pallas_call | solution.py:470
  401.1 3.6 all-to-all-start.7
  404.7 4.6 turn_bias.3.rest_0_
  409.4 4.6 turn_bias.4.rest_1_
  414.0 24.7 %attend_columns.4 = bf16[8,64,8,128]{3,2,1,0:T(8,128)(2,1)} custom-call(s32[8]{0:T(128)} %copy-done.14, bf16[24,6,8,3,32,128]{5,4,3,2,1,0:T(8,128)(2,1)} %bitcast.39, bf16[24,6,768,128]{3,2,1,0:T(8,128)(2,1)} %shard_map.98.key_ref, f32[4,256,768]{2,1,0:T(8,128)} %turn_bias.3.rest_0_, f32[4,256,768]{2,1,0:T(8,128)} %turn_bias.4.rest_1_, bf16[128,128]{1,0:T(8,128)(2,1)} %rest_1_.1), custom_call_target="tpu_custom_call" | custom-call | flops 6442450944 | bytes 6291456 | tf_op jit(solution)/shard_map/attend_columns/pallas_call | solution.py:470
  438.7 3.4 all-to-all-done.7.refs_0_
  442.1 3.6 all-to-all-start.4
  445.8 24.7 %attend_columns.5 = bf16[8,64,8,128]{3,2,1,0:T(8,128)(2,1)} custom-call(s32[8]{0:T(128)} %copy-done.16, bf16[24,6,8,3,32,128]{5,4,3,2,1,0:T(8,128)(2,1)} %bitcast.40, bf16[24,6,768,128]{3,2,1,0:T(8,128)(2,1)} %shard_map.98.key_ref, f32[4,256,768]{2,1,0:T(8,128)} %turn_bias.3.rest_0_, f32[4,256,768]{2,1,0:T(8,128)} %turn_bias.4.rest_1_, bf16[128,128]{1,0:T(8,128)(2,1)} %rest_1_.1), custom_call_target="tpu_custom_call" | custom-call | flops 6442450944 | bytes 6291456 | tf_op jit(solution)/shard_map/attend_columns/pallas_call | solution.py:470
  470.4 1.3 all-to-all-done.4.refs_0_
  471.7 4.8 all-to-all-start.5
  476.5 24.7 %attend_columns.6 = bf16[8,64,8,128]{3,2,1,0:T(8,128)(2,1)} custom-call(s32[8]{0:T(128)} %copy-done.15, bf16[24,6,8,3,32,128]{5,4,3,2,1,0:T(8,128)(2,1)} %bitcast.41, bf16[24,6,768,128]{3,2,1,0:T(8,128)(2,1)} %shard_map.98.key_ref, f32[4,256,768]{2,1,0:T(8,128)} %turn_bias.3.rest_0_, f32[4,256,768]{2,1,0:T(8,128)} %turn_bias.4.rest_1_, bf16[128,128]{1,0:T(8,128)(2,1)} %rest_1_.1), custom_call_target="tpu_custom_call" | custom-call | flops 6442450944 | bytes 6291456 | tf_op jit(solution)/shard_map/attend_columns/pallas_call | solution.py:470
  501.1 0.9 all-to-all-done.5.refs_1_
  502.0 5.2 all-to-all-start.6
  507.2 2.2 constant_dynamic-slice_fusion
  509.5 1.5 collective-permute-start.1
  511.0 1.4 collective-permute-start.2
  512.4 24.7 %collective-permute-done = bf16[1,24,192,128]{3,2,1,0:T(8,128)(2,1)S(1)} collective-permute-done((bf16[1,24,192,128]{3,2,1,0:T(8,128)(2,1)S(1)}, bf16[1,24,192,128]{3,2,1,0:T(8,128)(2,1)S(1)}, u32[]{:S(2)}, u32[]{:S(2)}) %collective-permute-start) | collective-permute-done | bytes 1179680 | tf_op jit(solution)/shard_map/ppermute | solution.py:622
  537.1 1.1 constant_dynamic-update-slice_fusion.2
  538.1 0.2 collective-permute-done.1
  538.4 1.1 constant_dynamic-update-slice_fusion.1
  539.5 22.5 %collective-permute-done.2 = bf16[1,24,192,128]{3,2,1,0:T(8,128)(2,1)S(1)} collective-permute-done((bf16[1,24,192,128]{3,2,1,0:T(8,128)(2,1)S(1)}, bf16[1,24,192,128]{3,2,1,0:T(8,128)(2,1)S(1)}, u32[]{:S(2)}, u32[]{:S(2)}) %collective-permute-start.2) | collective-permute-done | bytes 1179680 | tf_op jit(solution)/shard_map/ppermute | solution.py:622
  562.0 1.1 constant_dynamic-update-slice_fusion
  563.0 2.5 settle.2.refs_3_
  565.5 1.0 copy-done.9
  566.5 4.4 settle.3
  (60 shorter events, 0.9 us)
Async XLA Ops:
  7.2 109.4 %all-gather.7.cloned.1.call-start = ((), (), s32[]{:S(2)}) async-start(), calls=%async_computation.8 | async-start | bytes 9732096 | tf_op jit(solution)/shard_map/all_gather | solution.py:569
  7.9 2.3 copy-start.1
  19.2 5.2 copy-start.17
  19.2 5.8 %copy-start.11 = (bf16[128,512]{1,0:T(8,128)(2,1)S(1)}, bf16[128,512]{1,0:T(8,128)(2,1)}, u32[]{:S(2)}) copy-start(bf16[128,512]{1,0:T(8,128)(2,1)} %param.10) | copy-start | bytes 393220
  19.2 6.4 %copy-start.18 = (bf16[128,4]{0,1:T(4,128)(2,1)S(1)}, bf16[128,4]{0,1:T(4,128)(2,1)}, u32[]{:S(2)}) copy-start(bf16[128,4]{0,1:T(4,128)(2,1)} %param.14) | copy-start | bytes 3076
  19.2 75.2 %all-to-all-start = ((bf16[4,24,192,128]{3,2,1,0:T(8,128)(2,1)}), bf16[4,24,192,128]{3,2,1,0:T(8,128)(2,1)}, u32[]{:S(2)}, u32[]{:S(2)}) async-start(bf16[4,24,192,128]{3,2,1,0:T(8,128)(2,1)} %bitcast.36), calls=%async_computation | async-start | bytes 9437184 | tf_op jit(solution)/shard_map/all_to_all | solution.py:571
  24.3 338.3 %all-gather.11.cloned.1.call-start = ((), (), s32[]{:S(2)}) async-start(), calls=%async_computation.10 | async-start | bytes 3244032 | tf_op jit(solution)/shard_map/all_gather | solution.py:600
  24.4 92.2 %copy-start.3 = (s32[1,768]{1,0:T(1,128)}, s32[1,768]{1,0:T(1,128)S(1)}, u32[]{:S(2)}) copy-start(s32[1,768]{1,0:T(1,128)S(1)} %broadcast_in_dim.2.key_ok_ref) | copy-start | bytes 9220
  116.6 3.7 copy-start.2
  123.3 3.7 copy-start
  200.8 49.2 %all-to-all-start.2 = ((bf16[32,24,8,128]{3,2,1,0:T(8,128)(2,1)}), bf16[32,24,8,128]{3,2,1,0:T(8,128)(2,1)S(1)}, u32[]{:S(2)}, u32[]{:S(2)}) async-start(bf16[32,24,8,128]{3,2,1,0:T(8,128)(2,1)} %get-tuple-element.25), calls=%async_computation.2 | async-start | bytes 3145728 | tf_op jit(solution)/shard_map/all_to_all | solution.py:611
  204.1 200.6 %all-gather.9.cloned.1.call-start = ((), (), s32[]{:S(2)}) async-start(), calls=%async_computation.9 | async-start | bytes 6488064 | tf_op jit(solution)/shard_map/all_gather | solution.py:600
  204.2 37.2 %copy-start.13 = (f32[4,24,256]{2,1,0:T(8,128)S(1)}, f32[4,24,256]{2,1,0:T(8,128)}, u32[]{:S(2)}) copy-start(f32[4,24,256]{2,1,0:T(8,128)} %get-tuple-element.27) | copy-start | bytes 294916
  204.2 45.8 %copy-start.10 = (bf16[32,24,8,128]{3,2,1,0:T(8,128)(2,1)S(1)}, bf16[32,24,8,128]{3,2,1,0:T(8,128)(2,1)}, u32[]{:S(2)}) copy-start(bf16[32,24,8,128]{3,2,1,0:T(8,128)(2,1)} %get-tuple-element.26) | copy-start | bytes 4718596
  241.3 66.3 %copy-start.12 = (bf16[128,512]{1,0:T(8,128)(2,1)S(1)}, bf16[128,512]{1,0:T(8,128)(2,1)}, u32[]{:S(2)}) copy-start(bf16[128,512]{1,0:T(8,128)(2,1)} %param.13) | copy-start | bytes 393220
  250.0 67.9 %copy-start.5 = (bf16[32,24,8,128]{3,2,1,0:T(8,128)(2,1)}, bf16[32,24,8,128]{3,2,1,0:T(8,128)(2,1)S(1)}, u32[]{:S(2)}) copy-start(bf16[32,24,8,128]{3,2,1,0:T(8,128)(2,1)S(1)} %all-to-all-done.2) | copy-start | bytes 4718596
  303.6 51.0 %all-to-all-start.1 = ((bf16[32,24,8,128]{3,2,1,0:T(8,128)(2,1)}), bf16[32,24,8,128]{3,2,1,0:T(8,128)(2,1)S(1)}, u32[]{:S(2)}, u32[]{:S(2)}) async-start(bf16[32,24,8,128]{3,2,1,0:T(8,128)(2,1)} %get-tuple-element.24), calls=%async_computation.1 | async-start | bytes 3145728 | tf_op jit(solution)/shard_map/all_to_all | solution.py:611
  307.7 10.2 %copy-start.14 = (s32[8]{0:T(128)}, s32[8]{0:T(128)S(1)}, u32[]{:S(2)}) copy-start(s32[8]{0:T(128)S(1)} %gather_fusion) | copy-start | bytes 100
  309.0 8.9 %copy-start.16 = (s32[8]{0:T(128)}, s32[8]{0:T(128)S(1)}, u32[]{:S(2)}) copy-start(s32[8]{0:T(128)S(1)} %gather_fusion.1) | copy-start | bytes 100
  309.6 8.2 %copy-start.15 = (s32[8]{0:T(128)}, s32[8]{0:T(128)S(1)}, u32[]{:S(2)}) copy-start(s32[8]{0:T(128)S(1)} %gather_fusion.2) | copy-start | bytes 100
  354.6 1.1 copy-start.6
  401.1 41.0 %all-to-all-start.7 = ((bf16[8,32,24,128]{3,2,1,0:T(8,128)(2,1)}), bf16[8,32,24,128]{3,2,1,0:T(8,128)(2,1)S(1)}, u32[]{:S(2)}, u32[]{:S(2)}) async-start(bf16[8,32,24,128]{3,2,1,0:T(8,128)(2,1)} %attend_columns.7), calls=%async_computation.7 | async-start | bytes 3145728 | tf_op jit(solution)/shard_map/all_to_all | solution.py:658
  442.1 28.3 %copy-start.4 = (bf16[8,32,24,128]{3,2,1,0:T(8,128)(2,1)}, bf16[8,32,24,128]{3,2,1,0:T(8,128)(2,1)S(1)}, u32[]{:S(2)}) copy-start(bf16[8,32,24,128]{3,2,1,0:T(8,128)(2,1)S(1)} %all-to-all-done.7.refs_0_) | copy-start | bytes 4718596
  442.1 29.6 %all-to-all-start.4 = ((bf16[8,64,8,128]{3,2,1,0:T(8,128)(2,1)}), bf16[8,64,8,128]{3,2,1,0:T(8,128)(2,1)S(1)}, u32[]{:S(2)}, u32[]{:S(2)}) async-start(bf16[8,64,8,128]{3,2,1,0:T(8,128)(2,1)} %attend_columns.4), calls=%async_computation.4 | async-start | bytes 2097152 | tf_op jit(solution)/shard_map/all_to_all | solution.py:673
  471.7 29.4 %copy-start.7 = (bf16[8,64,8,128]{3,2,1,0:T(8,128)(2,1)}, bf16[8,64,8,128]{3,2,1,0:T(8,128)(2,1)S(1)}, u32[]{:S(2)}) copy-start(bf16[8,64,8,128]{3,2,1,0:T(8,128)(2,1)S(1)} %all-to-all-done.4.refs_0_) | copy-start | bytes 3145732
  471.7 30.3 %all-to-all-start.5 = ((bf16[8,64,8,128]{3,2,1,0:T(8,128)(2,1)}), bf16[8,64,8,128]{3,2,1,0:T(8,128)(2,1)S(1)}, u32[]{:S(2)}, u32[]{:S(2)}) async-start(bf16[8,64,8,128]{3,2,1,0:T(8,128)(2,1)} %attend_columns.5), calls=%async_computation.5 | async-start | bytes 2097152 | tf_op jit(solution)/shard_map/all_to_all | solution.py:673
  502.0 36.1 %copy-start.8 = (bf16[8,64,8,128]{3,2,1,0:T(8,128)(2,1)}, bf16[8,64,8,128]{3,2,1,0:T(8,128)(2,1)S(1)}, u32[]{:S(2)}) copy-start(bf16[8,64,8,128]{3,2,1,0:T(8,128)(2,1)S(1)} %all-to-all-done.5.refs_1_) | copy-start | bytes 3145732
  502.0 63.5 %all-to-all-start.6 = ((bf16[8,64,8,128]{3,2,1,0:T(8,128)(2,1)}), bf16[8,64,8,128]{3,2,1,0:T(8,128)(2,1)S(1)}, u32[]{:S(2)}, u32[]{:S(2)}) async-start(bf16[8,64,8,128]{3,2,1,0:T(8,128)(2,1)} %attend_columns.6), calls=%async_computation.6 | async-start | bytes 2097152 | tf_op jit(solution)/shard_map/all_to_all | solution.py:673
  509.4 27.7 %collective-permute-start = (bf16[1,24,192,128]{3,2,1,0:T(8,128)(2,1)S(1)}, bf16[1,24,192,128]{3,2,1,0:T(8,128)(2,1)S(1)}, u32[]{:S(2)}, u32[]{:S(2)}) collective-permute-start(bf16[1,24,192,128]{3,2,1,0:T(8,128)(2,1)S(1)} %get-tuple-element.21), channel_id=1, source_target_pairs={{0,1},{1,2},{2,3},{3,0},{4,5},{5,6},{6,7},{7,4},{8,9},{9,10},{10,1... | collective-permute-start | bytes 3538952 | tf_op jit(solution)/shard_map/ppermute | solution.py:622
  509.5 28.9 %collective-permute-start.1 = (bf16[1,24,192,128]{3,2,1,0:T(8,128)(2,1)S(1)}, bf16[1,24,192,128]{3,2,1,0:T(8,128)(2,1)S(1)}, u32[]{:S(2)}, u32[]{:S(2)}) collective-permute-start(bf16[1,24,192,128]{3,2,1,0:T(8,128)(2,1)S(1)} %get-tuple-element.22), channel_id=1, source_target_pairs={{0,2},{1,3},{2,0},{3,1},{4,6},{5,7},{6,4},{7,5},{8,10},{9,11},{10,... | collective-permute-start | bytes 3538952 | tf_op jit(solution)/shard_map/ppermute | solution.py:622
  511.0 51.0 %collective-permute-start.2 = (bf16[1,24,192,128]{3,2,1,0:T(8,128)(2,1)S(1)}, bf16[1,24,192,128]{3,2,1,0:T(8,128)(2,1)S(1)}, u32[]{:S(2)}, u32[]{:S(2)}) collective-permute-start(bf16[1,24,192,128]{3,2,1,0:T(8,128)(2,1)S(1)} %get-tuple-element.23), channel_id=1, source_target_pairs={{0,3},{1,0},{2,1},{3,2},{4,7},{5,4},{6,5},{7,6},{8,11},{9,8},{10,9... | collective-permute-start | bytes 3538952 | tf_op jit(solution)/shard_map/ppermute | solution.py:622
  565.5 1.0 copy-start.9
Sparse Core Ops, SparseCore 0:
  19.3 97.2 all-gather.6
  164.0 70.4 all-gather.10
  243.1 98.8 all-gather.8

commit v3 on v2

--- a/solution.py
+++ b/solution.py
@@ -63,7 +63,7 @@
             once(w_bias_rows.shape),
         ],
         out_specs=pl.BlockSpec((head_count, block, cols), lambda i: (0, i, 0)),
-        compiler_params=params(16),
+        compiler_params=params(),
         cost_estimate=pl.CostEstimate(
             flops=32 * tile.size, bytes_accessed=2 * tile.size, transcendentals=0
         ),
@@ -85,9 +85,9 @@
     main = cols // lanes
     half_lanes = lanes // 2
     low = lax.broadcasted_iota(jnp.int32, (1, lanes), 1) < half_lanes
-    for n in range(0, got_ref.shape[0], 2):
-        for h in range(got_ref.shape[1]):
-            blocks = []
+
+    def one_head(h, _):
+        for n in range(0, got_ref.shape[0], 2):
             even = [got_ref[n, h, b * rows : (b + 1) * rows] for b in range(main)]
             odd = [got_ref[n + 1, h, b * rows : (b + 1) * rows] for b in range(main)]
             even_tail = got_ref[n, h, main * rows :]
@@ -107,6 +107,9 @@
                 lane = n * cols + at * lanes
                 allowed = key_ok_ref[:, lane : lane + lanes] > 0
                 out_ref[h, :, lane : lane + lanes] = jnp.where(allowed, block * log2e, far_below)
+        return 0
+
+    lax.fori_loop(0, got_ref.shape[1], one_head, 0)
 
 
 def place_bias(key_ok, gathered, wide_count, rows, cols):
@@ -122,7 +125,7 @@
             pl.BlockSpec((narrow_count,) + gathered.shape[1:], lambda i: (i, 0, 0, 0)),
         ],
         out_specs=pl.BlockSpec((head_count, rows, length), lambda i: (0, i, 0)),
-        compiler_params=params(16),
+        compiler_params=params(),
         cost_estimate=pl.CostEstimate(
             flops=gathered.size, bytes_accessed=8 * gathered.size, transcendentals=0
         ),
@@ -134,22 +137,25 @@
     queries = got_ref.shape[-1]
     plane = got_ref[:, 0, 0].reshape(-1, queries)
     allowed = key_ok_ref[...] > 0
-    out_ref[0] = jnp.where(allowed, plane.T * log2e, far_below)
-
-
-def turn_bias(key_ok, gathered, part):
-    devices, _, head_count, rows, queries = gathered.shape
+    out_ref[0, 0] = jnp.where(allowed, plane.T * log2e, far_below)
+
+
+def turn_bias(key_ok, gathered):
+    devices, parts, head_count, rows, queries = gathered.shape
     length = devices * rows
+    if rows % 8:
+        turned = gathered.transpose(1, 2, 4, 0, 3).reshape(parts, head_count, queries, length)
+        return jnp.where(key_ok > 0, turned * log2e, far_below)
     return pl.pallas_call(
         turn_bias_kernel,
-        out_shape=jax.ShapeDtypeStruct((head_count, queries, length), jnp.float32),
-        grid=(head_count,),
+        out_shape=jax.ShapeDtypeStruct((parts, head_count, queries, length), jnp.float32),
+        grid=(parts, head_count),
         in_specs=[
             once((1, length)),
-            pl.BlockSpec((devices, 1, 1, rows, queries), lambda h: (0, part, h, 0, 0)),
+            pl.BlockSpec((devices, 1, 1, rows, queries), lambda p, h: (0, p, h, 0, 0)),
         ],
-        out_specs=pl.BlockSpec((1, queries, length), lambda h: (h, 0, 0)),
-        compiler_params=params(),
+        out_specs=pl.BlockSpec((1, 1, queries, length), lambda p, h: (p, h, 0, 0)),
+        compiler_params=pltpu.CompilerParams(vmem_limit_bytes=60 * 1024 * 1024),
         cost_estimate=pl.CostEstimate(
             flops=gathered.size, bytes_accessed=8 * gathered.size, transcendentals=0
         ),
@@ -210,7 +216,7 @@
         spec = pl.BlockSpec((pieces, per, cols, channels), lambda i: (0, i, 0, 0))
     elif kind == "columns":
         length, count = lines.shape[:2]
-        per = lines_per_step(count, 2)
+        per = 1
         spec = once(lines.shape)
         scratch = [pltpu.VMEM((length * count, channels), jnp.float32)]
     else:
@@ -422,8 +428,9 @@
 
 
 def attend_columns_kernel(col_ok_ref, query_ref, key_ref, *rest, parts, **sizes):
-    bias_refs, w_out_ref, out_ref = rest[:parts], rest[parts], rest[parts + 1]
-    scratch = rest[parts + 2 :]
+    bias_refs = [rest[0].at[at] for at in range(parts)]
+    w_out_ref, out_ref = rest[1:3]
+    scratch = rest[3:]
     per = key_ref.shape[0]
     blocks, piece = query_ref.shape[2], query_ref.shape[4]
     lines = [pl.program_id(0) * per + i for i in range(per)]
@@ -452,12 +459,11 @@
     blocks, _, piece, own, _ = plan
     length = projected.shape[2]
     count = col_ok.shape[0]
-    parts = len(biases)
-    head_count = biases[0].shape[0]
+    parts, head_count = biases.shape[:2]
     width = w_out.shape[0]
     head_dim = width // head_count
     scores = count * head_count * length * blocks * parts * piece
-    per = lines_per_step(count, 2) if parts == 1 else 1
+    per = lines_per_step(count, 2) if parts == 1 and count > own else 1
     if own % 8 == 0:
         out_shape = (blocks, parts * piece, count, width)
         out_spec = pl.BlockSpec(out_shape, lambda i, ok: (0, 0, 0, 0))
@@ -475,7 +481,7 @@
         grid_spec=pltpu.PrefetchScalarGridSpec(
             num_scalar_prefetch=1,
             grid=(count // per,),
-            in_specs=in_specs + [once(biases[0].shape)] * parts + [once(w_out.shape)],
+            in_specs=in_specs + [once(biases.shape), once(w_out.shape)],
             out_specs=out_spec,
             scratch_shapes=scratch,
         ),
@@ -484,23 +490,23 @@
             flops=4 * scores * 128, bytes_accessed=8 * count * length * width, transcendentals=scores
         ),
         name="attend_columns",
-    )(col_ok, *operands, *biases, w_out)
-
-
-def settle_kernel(*refs, order, plan):
+    )(col_ok, *operands, biases, w_out)
+
+
+def settle_kernel(*refs, places, plan):
     _, chunks, piece, own, wide_count = plan
     tile_rows = chunks * piece
     out_ref = refs[-1]
-    for step, j in enumerate(order):
-        ref, first = (refs[0], step * own) if len(refs) < chunks else (refs[step], 0)
+    for j, (which, step) in enumerate(places):
+        first = step * own
         for w in range(wide_count):
             inner, within = divmod(w * own, piece)
             col = inner * tile_rows + j * piece + within
-            out_ref[:, col : col + own, :] = ref[w, :, first : first + own, :]
-
-
-def settle(parts, first_row, before, order, plan, shape):
-    wide_count, rows, _, _ = parts[0].shape
+            out_ref[:, col : col + own, :] = refs[which][w, :, first : first + own, :]
+
+
+def settle(parts, first_row, before, places, plan, shape):
+    wide_count, rows = parts[0].shape[:2]
     block = 16
     skip = first_row // block
     in_specs = [
@@ -513,7 +519,7 @@
         operands.append(before)
         aliases = {len(parts): 0}
     return pl.pallas_call(
-        functools.partial(settle_kernel, order=order, plan=plan),
+        functools.partial(settle_kernel, places=places, plan=plan),
         out_shape=jax.ShapeDtypeStruct(shape, jnp.bfloat16),
         grid=(rows // block,),
         in_specs=in_specs,
@@ -588,25 +594,20 @@
         key_ok, wide_at * tile_rows + narrow_at * row_count, row_count
     )
     w_bias_rows = bias_rows_of(w_bias_end)
-    order = [chunks - 1] + list(range(chunks - 1))
-    columns, waiting, next_biases = {}, [], {}
+    order = list(range(chunks))
+    soon = max(chunks - 1, 1)
+    columns, waiting, next_biases = {}, [], []
     upd = None
     for step, j in enumerate(order):
         upd, nxt, nbias = attend_rows(
             row_ok, projected, lines, bias, w_out_start, w_bias_rows, j, upd, plan
         )
         waiting.append((j, nbias))
-        if step in (0, chunks - 1):
+        if step in (soon - 1, chunks - 1):
             got = lax.all_gather(
                 jnp.stack([nbias for _, nbias in waiting]), both_axes, axis=0, tiled=False
             )
-            for n, (k, _) in enumerate(waiting):
-                if row_count % 8 == 0:
-                    turned = turn_bias(key_ok, got, n)
-                else:
-                    turned = got[:, n].transpose(1, 3, 0, 2).reshape(head_count, -1, length)
-                    turned = jnp.where(key_ok > 0, turned * log2e, far_below)
-                next_biases[k] = turned
+            next_biases.append(turn_bias(key_ok, got))
             waiting = []
         got = lax.all_to_all(nxt, both_axes, split_axis=0, concat_axis=0, tiled=True)
         columns[j] = got.reshape(length, own, channels)
@@ -627,51 +628,53 @@
     update_start = update_start.reshape(tile_rows, tile_cols, channels)
 
     packed_end = pack_projection(w_proj_end, head_count, head_dim)
-    projected_end, col_ok = None, []
+    projected_end, col_ok = {}, []
+    home_of = [(0, step) if step < soon else (soon, step - soon) for step in range(chunks)]
     for step, j in enumerate(order):
+        group, place = home_of[step]
         lines_end = columns[j]
         if own % 8:
             lines_end = lines_end.transpose(1, 0, 2)
-        projected_end = project(
+        projected_end[group] = project(
             lines_end,
             packed_end,
             head_count,
             head_dim,
             "plain" if own % 8 else "columns",
-            projected_end,
-            step * own,
-            chunks * own,
+            projected_end.get(group),
+            place * own,
+            (soon if group == 0 else chunks - soon) * own,
         )
         at = wide_at * own + jnp.arange(own)
         at = narrow_at * tile_cols + at // piece * tile_rows + j * piece + at % piece
         col_ok.append(key_ok[at])
 
-    got = attend_columns(
-        jnp.concatenate(col_ok),
-        projected_end,
-        [next_biases[order[0]]],
-        w_out_end,
-        order[0],
-        0,
-        plan,
-    )
-    got = lax.all_to_all(got, "wide", split_axis=0, concat_axis=0, tiled=True)
+    def columns_of(step, count, first):
+        return attend_columns(
+            jnp.concatenate(col_ok[step : step + count]),
+            projected_end[home_of[step][0]],
+            next_biases[0 if first == 0 else 1],
+            w_out_end,
+            first,
+            home_of[step][1] * own,
+            plan,
+        )
+
+    parts = []
+    for step in range(chunks):
+        got = columns_of(step, 1, 0)
+        parts.append(lax.all_to_all(got, "wide", split_axis=0, concat_axis=0, tiled=True))
     if chunks == 1:
-        return (update_start, got.transpose(2, 0, 1, 3).reshape(pair_act.shape))
-    settled = settle([got], (chunks - 1) * piece, None, order, plan, pair_act.shape)
+        if own % 8:
+            parts[0] = parts[0].transpose(0, 2, 1, 3)
+        return (update_start, parts[0].transpose(1, 0, 2, 3).reshape(pair_act.shape))
     late = []
-    for step, j in enumerate(order):
-        got = attend_columns(
-            col_ok[step],
-            projected_end,
-            [next_biases[k] for k in range(chunks - 1)],
-            w_out_end,
-            0,
-            step * own,
-            plan,
-        )
+    for step, count in ((0, soon), (soon, chunks - soon)):
+        got = columns_of(step, count, soon)
         late.append(lax.all_to_all(got, "wide", split_axis=0, concat_axis=0, tiled=True))
-    return (update_start, settle(late, 0, settled, order, plan, pair_act.shape))
+    settled = settle(parts, 0, None, [(n, 0) for n in order], plan, pair_act.shape)
+    places = [(0, n) for n in range(soon)] + [(1, n) for n in range(chunks - soon)]
+    return (update_start, settle(late, soon * piece, settled, places, plan, pair_act.shape))
 
 
 def solution(mesh):

time: 580 us -> 630 us (1.086)
  blocking collectives: 53.6 us -> 96.5 us
  Pallas kernels: 290 us -> 311 us
  waiting for transfers between devices: 160 us -> 148 us
  starting transfers between devices: 31.9 us -> 38.7 us
    all_to_all x1 -> x2, blocking collectives: 53.6 us -> 96.5 us  [on_device(): lax.all_to_all(nxt, both_axes, split_axis=0, concat_axis=0, tiled=True)]
    all_to_all x3 -> x5, starting transfers between devices: 13.5 us -> 26.9 us  [on_device(): lax.all_to_all(got, 'wide', split_axis=0, concat_axis=0, tiled=True)]
    unnamed x40 -> x34, local copies, waits for them, and re-layouts: 12.2 us -> 1.3 us
    pallas_call x1, Pallas kernels: 2.99 us -> 11.2 us  [place_bias(): pl.pallas_call(functools.partial(place_bias_kernel, rows=rows, cols=cols)...]
    all_to_all x2 -> x1, waiting for transfers between devices: 36.8 us -> 29.5 us  [on_device(): lax.all_to_all(nxt, both_axes, split_axis=0, concat_axis=0, tiled=True)]
    pallas_call x4 -> x5, Pallas kernels: 108 us -> 113 us  [attend_columns(): pl.pallas_call(functools.partial(attend_columns_kernel, parts=parts, head...]
    pallas_call x5 -> x4, Pallas kernels: 20.8 us -> 20.2 us  [the longest x2 13.3 us: turn_bias(): pl.pallas_call(turn_bias_kernel, out_shape=jax.ShapeDtypeStruct((parts, h...]
  transfers between devices with their start and end apart: 13 -> 13, of which waited for: 10 -> 7; matrix products, arithmetic and copies ran while one was open for 2% -> 2% of each run, Pallas kernels for 41% -> 28%
where the time goes in v3:
time: 630 us; the launch traced here: 628 us
  Pallas kernels  311 us (49%)
  waiting for transfers between devices  148 us (23%)
  blocking collectives  96.5 us (15%)
  starting transfers between devices  38.7 us (6%)
  local copies, waits for them, and re-layouts  16.3 us (3%)
  between operations  14.1 us (2%)
    pallas_call x5, Pallas kernels, attend_columns(): pl.pallas_call(functools.partial(attend_columns_kernel, parts=parts, head...  113 us
    pallas_call x3, Pallas kernels, attend_rows(): pl.pallas_call(functools.partial(attend_rows_kernel, head_count=head_coun...  111 us
    all_to_all x2, blocking collectives, on_device(): lax.all_to_all(nxt, both_axes, split_axis=0, concat_axis=0, tiled=True)  96.5 us
    all_to_all x1, waiting for transfers between devices, on_device(): lax.all_to_all(tile_in.reshape(narrow_count, row_count, tile_cols, channe...  66.8 us
    ppermute x3, waiting for transfers between devices, on_device(): arrived.append(lax.ppermute(leaving[k - 1], 'narrow', ring))  47.4 us
    pallas_call x4, Pallas kernels, project(): pl.pallas_call(functools.partial(project_kernel, head_count=head_count, h...  43.7 us
    all_to_all x1, waiting for transfers between devices, on_device(): lax.all_to_all(nxt, both_axes, split_axis=0, concat_axis=0, tiled=True)  29.5 us
    all_to_all x5, starting transfers between devices, on_device(): lax.all_to_all(got, 'wide', split_axis=0, concat_axis=0, tiled=True)  26.9 us
  transfers between devices with their start and end apart: 13, of which 7 were waited for; matrix products, arithmetic and copies ran while one was open for 2% of the time, Pallas kernels for 28%

profile of v3, /device:TPU:0, one launch (start us, length us, event | category | flops | bytes accessed | tf_op | source)
XLA Modules:
  0.0 627.5 jit_solution(2902674705006926525)
XLA Ops:
  7.2 1.3 pad.7.w_ref
  8.5 11.5 %tile_bias.1 = f32[4,96,192]{2,1,0:T(8,128)} custom-call(bf16[96,192,128]{2,1,0:T(8,128)(2,1)} %x_ref.1, bf16[16,128]{1,0:T(8,128)(2,1)} %pad.7.w_ref), custom_call_target="tpu_custom_call" | custom-call | flops 75497472 | bytes 4718592 | tf_op jit(solution)/shard_map/tile_bias/pallas_call | solution.py:57
  19.9 1.0 fusion.3
  20.9 0.9 slice.53
  21.9 0.8 maximum_maximum_fusion
  22.7 5.1 all-to-all-start
  27.9 0.6 broadcast_in_dim.2.key_ok_ref
  28.5 0.6 dynamic_slice.13.row_ok_ref
  29.1 0.1 copy.32
  29.3 0.1 copy.36
  29.4 0.1 copy.35
  29.5 0.1 copy.34
  29.6 0.1 copy.33
  29.8 0.6 pad.8.w_bias_ref
  30.4 0.7 pad_maximum_fusion.w_ref
  31.1 66.8 %all-to-all-done.x_ref = bf16[4,24,192,128]{3,2,1,0:T(8,128)(2,1)} async-done(((bf16[4,24,192,128]{3,2,1,0:T(8,128)(2,1)}), bf16[4,24,192,128]{3,2,1,0:T(8,128)(2,1)}, u32[]{:S(2)}, u32[]{:S(2)}) %all-to-all-start) | async-done | bytes 4718624 | tf_op jit(solution)/shard_map/all_to_all | solution.py:577
  97.9 19.1 %shard_map.95.key_ref = bf16[24,6,768,128]{3,2,1,0:T(8,128)(2,1)} custom-call(bf16[4,24,192,128]{3,2,1,0:T(8,128)(2,1)} %all-to-all-done.x_ref, bf16[128,768]{1,0:T(8,128)(2,1)} %pad_maximum_fusion.w_ref), custom_call_target="tpu_custom_call" | custom-call | flops 3623878656 | bytes 33030144 | tf_op jit(solution)/shard_map/pallas_call | solution.py:234
  117.0 3.1 all-gather.7.cloned.1.call-done
  120.1 11.2 %place_bias.1 = f32[4,768,768]{2,1,0:T(8,128)} custom-call(s32[1,768]{1,0:T(1,128)} %broadcast_in_dim.2.key_ok_ref, f32[32,4,144,128]{3,2,1,0:T(8,128)} %bitcast.49), custom_call_target="tpu_custom_call" | custom-call | flops 2359296 | bytes 18874368 | tf_op jit(solution)/shard_map/place_bias/pallas_call | solution.py:119
  131.3 36.9 %attend_rows.3 = (bf16[4,24,2,3,32,128]{5,4,3,2,1,0:T(8,128)(2,1)}, bf16[32,24,8,128]{3,2,1,0:T(8,128)(2,1)}, f32[4,24,256]{2,1,0:T(8,128)}) custom-call(s32[24]{0:T(128)} %dynamic_slice.13.row_ok_ref, bf16[24,6,8,3,32,128]{5,4,3,2,1,0:T(8,128)(2,1)} %bitcast.34, bf16[24,6,768,128]{3,2,1,0:T(8,128)(2,1)} %shard_map.95.key_ref, ...), custom_call_target="tpu_custom_call" | custom-call | flops 9663676416 | bytes 18874368 | tf_op jit(solution)/shard_map/attend_rows/pallas_call | solution.py:404
  168.2 36.9 %attend_rows.4 = (bf16[4,24,2,3,32,128]{5,4,3,2,1,0:T(8,128)(2,1)}, bf16[32,24,8,128]{3,2,1,0:T(8,128)(2,1)}, f32[4,24,256]{2,1,0:T(8,128)}) custom-call(s32[24]{0:T(128)} %dynamic_slice.13.row_ok_ref, bf16[24,6,8,3,32,128]{5,4,3,2,1,0:T(8,128)(2,1)} %bitcast.35, bf16[24,6,768,128]{3,2,1,0:T(8,128)(2,1)} %shard_map.95.key_ref, ...), custom_call_target="tpu_custom_call", output_to_operand_aliasing={{0}: (7, {})} | custom-call | flops 9663676416 | bytes 18874368 | tf_op jit(solution)/shard_map/attend_rows/pallas_call | solution.py:404
  205.2 37.1 %attend_rows.5 = (bf16[4,24,2,3,32,128]{5,4,3,2,1,0:T(8,128)(2,1)}, bf16[32,24,8,128]{3,2,1,0:T(8,128)(2,1)}, f32[4,24,256]{2,1,0:T(8,128)}) custom-call(s32[24]{0:T(128)} %dynamic_slice.13.row_ok_ref, bf16[24,6,8,3,32,128]{5,4,3,2,1,0:T(8,128)(2,1)} %bitcast.36, bf16[24,6,768,128]{3,2,1,0:T(8,128)(2,1)} %shard_map.95.key_ref, ...), custom_call_target="tpu_custom_call", output_to_operand_aliasing={{0}: (7, {})} | custom-call | flops 9663676416 | bytes 18874368 | tf_op jit(solution)/shard_map/attend_rows/pallas_call | solution.py:404
  242.3 0.7 pad_maximum_fusion.2
  243.1 47.7 %all_to_all.45 = bf16[32,24,8,128]{3,2,1,0:T(8,128)(2,1)} all-to-all(bf16[32,24,8,128]{3,2,1,0:T(8,128)(2,1)S(1)} %copy-done.6), channel_id=1, replica_groups=mesh['wide'=8,'narrow'=4] {'wide','narrow'}, dimensions={0} | all-to-all | bytes 3145728 | tf_op jit(solution)/shard_map/all_to_all | solution.py:612
  290.7 48.8 %all_to_all.46 = bf16[32,24,8,128]{3,2,1,0:T(8,128)(2,1)} all-to-all(bf16[32,24,8,128]{3,2,1,0:T(8,128)(2,1)S(1)} %copy-done.7), channel_id=1, replica_groups=mesh['wide'=8,'narrow'=4] {'wide','narrow'}, dimensions={0} | all-to-all | bytes 3145728 | tf_op jit(solution)/shard_map/all_to_all | solution.py:612
  339.5 3.6 all-to-all-start.2
  343.2 0.1 copy.37
  343.3 0.1 copy.41
  343.6 0.1 copy.39
  343.7 0.1 copy.38
  343.9 1.2 gather_fusion.2
  345.0 0.7 pad_maximum_fusion.1.w_ref
  345.7 8.2 %shard_map.98.key_ref = bf16[8,6,768,128]{3,2,1,0:T(8,128)(2,1)} custom-call(bf16[768,8,128]{2,1,0:T(8,128)(2,1)} %bitcast.53, bf16[128,768]{1,0:T(8,128)(2,1)} %pad_maximum_fusion.1.w_ref), custom_call_target="tpu_custom_call" | custom-call | flops 1207959552 | bytes 11010048 | tf_op jit(solution)/shard_map/pallas_call | solution.py:234
  353.9 4.6 turn_bias.2.rest_0_
  358.6 15.2 %attend_columns.6 = bf16[8,32,8,128]{3,2,1,0:T(8,128)(2,1)} custom-call(s32[8]{0:T(128)} %gather_fusion.2, bf16[8,6,8,3,32,128]{5,4,3,2,1,0:T(8,128)(2,1)} %bitcast.40, bf16[8,6,768,128]{3,2,1,0:T(8,128)(2,1)} %shard_map.98.key_ref, f32[1,4,256,768]{3,2,1,0:T(8,128)} %turn_bias.2.rest_0_, bf16[128,128]{1,0:T(8,128)(2,1)} %rest_1_.9), custom_call_target="tpu_custom_call" | custom-call | flops 3221225472 | bytes 6291456 | tf_op jit(solution)/shard_map/attend_columns/pallas_call | solution.py:476
  373.8 29.5 %all-to-all-done.2 = bf16[32,24,8,128]{3,2,1,0:T(8,128)(2,1)S(1)} async-done(((bf16[32,24,8,128]{3,2,1,0:T(8,128)(2,1)}), bf16[32,24,8,128]{3,2,1,0:T(8,128)(2,1)S(1)}, u32[]{:S(2)}, u32[]{:S(2)}) %all-to-all-start.2) | async-done | bytes 1572896 | tf_op jit(solution)/shard_map/all_to_all | solution.py:612
  403.3 3.5 all-to-all-start.5
  406.8 1.2 gather_fusion
  408.0 8.2 %shard_map.96.rest_0_ = bf16[16,6,768,128]{3,2,1,0:T(8,128)(2,1)} custom-call(bf16[768,8,128]{2,1,0:T(8,128)(2,1)} %bitcast.51, bf16[128,768]{1,0:T(8,128)(2,1)} %pad_maximum_fusion.1.w_ref), custom_call_target="tpu_custom_call" | custom-call | flops 1207959552 | bytes 11010048 | tf_op jit(solution)/shard_map/pallas_call | solution.py:234
  416.2 8.2 %shard_map.97.key_ref = bf16[16,6,768,128]{3,2,1,0:T(8,128)(2,1)} custom-call(bf16[768,8,128]{2,1,0:T(8,128)(2,1)} %bitcast.50, bf16[128,768]{1,0:T(8,128)(2,1)} %pad_maximum_fusion.1.w_ref, bf16[16,6,768,128]{3,2,1,0:T(8,128)(2,1)} %shard_map.96.rest_0_), custom_call_target="tpu_custom_call", output_to_operand_aliasing={{}: (2, {})} | custom-call | flops 1207959552 | bytes 11010048 | tf_op jit(solution)/shard_map/pallas_call | solution.py:234
  424.4 8.7 %turn_bias.3.rest_0_ = f32[2,4,256,768]{3,2,1,0:T(8,128)} custom-call(s32[1,768]{1,0:T(1,128)} %broadcast_in_dim.2.key_ok_ref, f32[32,2,4,24,256]{4,3,2,1,0:T(8,128)} %bitcast.52), custom_call_target="tpu_custom_call" | custom-call | flops 1572864 | bytes 12582912 | tf_op jit(solution)/shard_map/turn_bias/pallas_call | solution.py:149
  433.0 24.6 %attend_columns.7 = bf16[8,64,8,128]{3,2,1,0:T(8,128)(2,1)} custom-call(s32[8]{0:T(128)} %gather_fusion, bf16[16,6,8,3,32,128]{5,4,3,2,1,0:T(8,128)(2,1)} %bitcast.37, bf16[16,6,768,128]{3,2,1,0:T(8,128)(2,1)} %shard_map.97.key_ref, f32[2,4,256,768]{3,2,1,0:T(8,128)} %turn_bias.3.rest_0_, bf16[128,128]{1,0:T(8,128)(2,1)} %rest_1_.9), custom_call_target="tpu_custom_call" | custom-call | flops 6442450944 | bytes 6291456 | tf_op jit(solution)/shard_map/attend_columns/pallas_call | solution.py:476
  457.7 6.0 all-to-all-start.6
  463.7 1.2 gather_fusion.1
  464.9 24.6 %attend_columns.8 = bf16[8,64,8,128]{3,2,1,0:T(8,128)(2,1)} custom-call(s32[8]{0:T(128)} %gather_fusion.1, bf16[16,6,8,3,32,128]{5,4,3,2,1,0:T(8,128)(2,1)} %bitcast.38, bf16[16,6,768,128]{3,2,1,0:T(8,128)(2,1)} %shard_map.97.key_ref, f32[2,4,256,768]{3,2,1,0:T(8,128)} %turn_bias.3.rest_0_, bf16[128,128]{1,0:T(8,128)(2,1)} %rest_1_.9), custom_call_target="tpu_custom_call" | custom-call | flops 6442450944 | bytes 6291456 | tf_op jit(solution)/shard_map/attend_columns/pallas_call | solution.py:476
  489.5 6.0 all-to-all-start.7
  495.5 24.6 %attend_columns.9 = bf16[8,64,8,128]{3,2,1,0:T(8,128)(2,1)} custom-call(s32[8]{0:T(128)} %gather_fusion.2, bf16[8,6,8,3,32,128]{5,4,3,2,1,0:T(8,128)(2,1)} %bitcast.41, bf16[8,6,768,128]{3,2,1,0:T(8,128)(2,1)} %shard_map.98.key_ref, f32[2,4,256,768]{3,2,1,0:T(8,128)} %turn_bias.3.rest_0_, bf16[128,128]{1,0:T(8,128)(2,1)} %rest_1_.9), custom_call_target="tpu_custom_call" | custom-call | flops 6442450944 | bytes 6291456 | tf_op jit(solution)/shard_map/attend_columns/pallas_call | solution.py:476
  520.1 0.7 all-to-all-done.7.refs_1_
  520.8 5.5 all-to-all-start.8
  526.2 0.7 pad_add_fusion.col_ok_ref
  526.9 24.3 %attend_columns.5 = bf16[8,32,16,128]{3,2,1,0:T(8,128)(2,1)} custom-call(s32[16]{0:T(128)} %pad_add_fusion.col_ok_ref, bf16[16,6,8,3,32,128]{5,4,3,2,1,0:T(8,128)(2,1)} %bitcast.39, bf16[16,6,768,128]{3,2,1,0:T(8,128)(2,1)} %shard_map.97.key_ref, f32[1,4,256,768]{3,2,1,0:T(8,128)} %turn_bias.2.rest_0_, bf16[128,128]{1,0:T(8,128)(2,1)} %rest_1_.9), custom_call_target="tpu_custom_call" | custom-call | flops 6442450944 | bytes 12582912 | tf_op jit(solution)/shard_map/attend_columns/pallas_call | solution.py:476
  551.2 6.0 all-to-all-start.3
  557.2 2.2 constant_dynamic-slice_fusion
  559.5 1.5 collective-permute-start.1
  561.0 1.4 collective-permute-start.2
  562.4 24.7 %collective-permute-done = bf16[1,24,192,128]{3,2,1,0:T(8,128)(2,1)S(1)} collective-permute-done((bf16[1,24,192,128]{3,2,1,0:T(8,128)(2,1)S(1)}, bf16[1,24,192,128]{3,2,1,0:T(8,128)(2,1)S(1)}, u32[]{:S(2)}, u32[]{:S(2)}) %collective-permute-start) | collective-permute-done | bytes 1179680 | tf_op jit(solution)/shard_map/ppermute | solution.py:623
  587.1 1.1 constant_dynamic-update-slice_fusion.2
  588.2 0.2 collective-permute-done.1
  588.4 1.1 constant_dynamic-update-slice_fusion.1
  589.5 22.5 %collective-permute-done.2 = bf16[1,24,192,128]{3,2,1,0:T(8,128)(2,1)S(1)} collective-permute-done((bf16[1,24,192,128]{3,2,1,0:T(8,128)(2,1)S(1)}, bf16[1,24,192,128]{3,2,1,0:T(8,128)(2,1)S(1)}, u32[]{:S(2)}, u32[]{:S(2)}) %collective-permute-start.2) | collective-permute-done | bytes 1179680 | tf_op jit(solution)/shard_map/ppermute | solution.py:623
  612.0 1.1 constant_dynamic-update-slice_fusion
  613.1 4.4 settle.2.refs_2_
  617.5 1.0 copy-done.4
  618.5 2.5 settle.3
  (55 shorter events, 0.5 us)
Async XLA Ops:
  7.2 113.0 %all-gather.7.cloned.1.call-start = ((), (), s32[]{:S(2)}) async-start(), calls=%async_computation.9 | async-start | bytes 9732096 | tf_op jit(solution)/shard_map/all_gather | solution.py:575
  22.7 5.2 copy-start.12
  22.7 6.4 %copy-start.8 = (bf16[128,512]{1,0:T(8,128)(2,1)S(1)}, bf16[128,512]{1,0:T(8,128)(2,1)}, u32[]{:S(2)}) copy-start(bf16[128,512]{1,0:T(8,128)(2,1)} %param.10) | copy-start | bytes 393220
  22.7 7.0 %copy-start.15 = (bf16[128,4]{0,1:T(4,128)(2,1)S(1)}, bf16[128,4]{0,1:T(4,128)(2,1)}, u32[]{:S(2)}) copy-start(bf16[128,4]{0,1:T(4,128)(2,1)} %param.14) | copy-start | bytes 3076
  22.7 75.2 %all-to-all-start = ((bf16[4,24,192,128]{3,2,1,0:T(8,128)(2,1)}), bf16[4,24,192,128]{3,2,1,0:T(8,128)(2,1)}, u32[]{:S(2)}, u32[]{:S(2)}) async-start(bf16[4,24,192,128]{3,2,1,0:T(8,128)(2,1)} %bitcast.48), calls=%async_computation | async-start | bytes 9437184 | tf_op jit(solution)/shard_map/all_to_all | solution.py:577
  27.8 326.1 %all-gather.9.cloned.1.call-start = ((), (), s32[]{:S(2)}) async-start(), calls=%async_computation.10 | async-start | bytes 3244032 | tf_op jit(solution)/shard_map/all_gather | solution.py:607
  205.1 37.2 %copy-start.10 = (f32[4,24,256]{2,1,0:T(8,128)S(1)}, f32[4,24,256]{2,1,0:T(8,128)}, u32[]{:S(2)}) copy-start(f32[4,24,256]{2,1,0:T(8,128)} %get-tuple-element.28) | copy-start | bytes 294916
  205.1 37.2 %copy-start.11 = (f32[4,24,256]{2,1,0:T(8,128)S(1)}, f32[4,24,256]{2,1,0:T(8,128)}, u32[]{:S(2)}) copy-start(f32[4,24,256]{2,1,0:T(8,128)} %get-tuple-element.29) | copy-start | bytes 294916
  205.2 37.9 %copy-start.6 = (bf16[32,24,8,128]{3,2,1,0:T(8,128)(2,1)S(1)}, bf16[32,24,8,128]{3,2,1,0:T(8,128)(2,1)}, u32[]{:S(2)}) copy-start(bf16[32,24,8,128]{3,2,1,0:T(8,128)(2,1)} %get-tuple-element.24) | copy-start | bytes 4718596
  242.2 48.5 %copy-start.7 = (bf16[32,24,8,128]{3,2,1,0:T(8,128)(2,1)S(1)}, bf16[32,24,8,128]{3,2,1,0:T(8,128)(2,1)}, u32[]{:S(2)}) copy-start(bf16[32,24,8,128]{3,2,1,0:T(8,128)(2,1)} %get-tuple-element.27) | copy-start | bytes 4718596
  242.2 182.1 %all-gather.11.cloned.1.call-start = ((), (), s32[]{:S(2)}) async-start(), calls=%async_computation.11 | async-start | bytes 6488064 | tf_op jit(solution)/shard_map/all_gather | solution.py:607
  243.0 100.1 %copy-start.9 = (bf16[128,512]{1,0:T(8,128)(2,1)S(1)}, bf16[128,512]{1,0:T(8,128)(2,1)}, u32[]{:S(2)}) copy-start(bf16[128,512]{1,0:T(8,128)(2,1)} %param.13) | copy-start | bytes 393220
  339.5 63.7 %all-to-all-start.2 = ((bf16[32,24,8,128]{3,2,1,0:T(8,128)(2,1)}), bf16[32,24,8,128]{3,2,1,0:T(8,128)(2,1)S(1)}, u32[]{:S(2)}, u32[]{:S(2)}) async-start(bf16[32,24,8,128]{3,2,1,0:T(8,128)(2,1)} %get-tuple-element.25), calls=%async_computation.2 | async-start | bytes 3145728 | tf_op jit(solution)/shard_map/all_to_all | solution.py:612
  403.2 4.7 copy-start
  403.3 54.4 %all-to-all-start.5 = ((bf16[8,32,8,128]{3,2,1,0:T(8,128)(2,1)}), bf16[8,32,8,128]{3,2,1,0:T(8,128)(2,1)S(1)}, u32[]{:S(2)}, u32[]{:S(2)}) async-start(bf16[8,32,8,128]{3,2,1,0:T(8,128)(2,1)} %attend_columns.6), calls=%async_computation.5 | async-start | bytes 1048576 | tf_op jit(solution)/shard_map/all_to_all | solution.py:674
  457.7 31.8 %copy-start.5 = (bf16[8,32,8,128]{3,2,1,0:T(8,128)(2,1)}, bf16[8,32,8,128]{3,2,1,0:T(8,128)(2,1)S(1)}, u32[]{:S(2)}) copy-start(bf16[8,32,8,128]{3,2,1,0:T(8,128)(2,1)S(1)} %all-to-all-done.5.refs_1_) | copy-start | bytes 1572868
  457.7 31.8 %all-to-all-start.6 = ((bf16[8,64,8,128]{3,2,1,0:T(8,128)(2,1)}), bf16[8,64,8,128]{3,2,1,0:T(8,128)(2,1)S(1)}, u32[]{:S(2)}, u32[]{:S(2)}) async-start(bf16[8,64,8,128]{3,2,1,0:T(8,128)(2,1)} %attend_columns.7), calls=%async_computation.6 | async-start | bytes 2097152 | tf_op jit(solution)/shard_map/all_to_all | solution.py:666
  489.5 30.6 %copy-start.1 = (bf16[8,64,8,128]{3,2,1,0:T(8,128)(2,1)}, bf16[8,64,8,128]{3,2,1,0:T(8,128)(2,1)S(1)}, u32[]{:S(2)}) copy-start(bf16[8,64,8,128]{3,2,1,0:T(8,128)(2,1)S(1)} %all-to-all-done.6.refs_0_) | copy-start | bytes 3145732
  489.5 31.3 %all-to-all-start.7 = ((bf16[8,64,8,128]{3,2,1,0:T(8,128)(2,1)}), bf16[8,64,8,128]{3,2,1,0:T(8,128)(2,1)S(1)}, u32[]{:S(2)}, u32[]{:S(2)}) async-start(bf16[8,64,8,128]{3,2,1,0:T(8,128)(2,1)} %attend_columns.8), calls=%async_computation.7 | async-start | bytes 2097152 | tf_op jit(solution)/shard_map/all_to_all | solution.py:666
  495.5 30.8 %copy-start.13 = (s32[8]{0:T(128)S(1)}, s32[8]{0:T(128)}, u32[]{:S(2)}) copy-start(s32[8]{0:T(128)} %gather_fusion) | copy-start | bytes 100
  495.5 30.8 %copy-start.14 = (s32[8]{0:T(128)S(1)}, s32[8]{0:T(128)}, u32[]{:S(2)}) copy-start(s32[8]{0:T(128)} %gather_fusion.1) | copy-start | bytes 100
  520.8 30.4 %copy-start.2 = (bf16[8,64,8,128]{3,2,1,0:T(8,128)(2,1)}, bf16[8,64,8,128]{3,2,1,0:T(8,128)(2,1)S(1)}, u32[]{:S(2)}) copy-start(bf16[8,64,8,128]{3,2,1,0:T(8,128)(2,1)S(1)} %all-to-all-done.7.refs_1_) | copy-start | bytes 3145732
  520.8 30.4 %all-to-all-start.8 = ((bf16[8,64,8,128]{3,2,1,0:T(8,128)(2,1)}), bf16[8,64,8,128]{3,2,1,0:T(8,128)(2,1)S(1)}, u32[]{:S(2)}, u32[]{:S(2)}) async-start(bf16[8,64,8,128]{3,2,1,0:T(8,128)(2,1)} %attend_columns.9), calls=%async_computation.8 | async-start | bytes 2097152 | tf_op jit(solution)/shard_map/all_to_all | solution.py:666
  551.2 37.0 %copy-start.3 = (bf16[8,64,8,128]{3,2,1,0:T(8,128)(2,1)}, bf16[8,64,8,128]{3,2,1,0:T(8,128)(2,1)S(1)}, u32[]{:S(2)}) copy-start(bf16[8,64,8,128]{3,2,1,0:T(8,128)(2,1)S(1)} %all-to-all-done.8.refs_2_) | copy-start | bytes 3145732
  551.2 66.3 %all-to-all-start.3 = ((bf16[8,32,16,128]{3,2,1,0:T(8,128)(2,1)}), bf16[8,32,16,128]{3,2,1,0:T(8,128)(2,1)S(1)}, u32[]{:S(2)}, u32[]{:S(2)}) async-start(bf16[8,32,16,128]{3,2,1,0:T(8,128)(2,1)} %attend_columns.5), calls=%async_computation.3 | async-start | bytes 2097152 | tf_op jit(solution)/shard_map/all_to_all | solution.py:674
  559.4 27.7 %collective-permute-start = (bf16[1,24,192,128]{3,2,1,0:T(8,128)(2,1)S(1)}, bf16[1,24,192,128]{3,2,1,0:T(8,128)(2,1)S(1)}, u32[]{:S(2)}, u32[]{:S(2)}) collective-permute-start(bf16[1,24,192,128]{3,2,1,0:T(8,128)(2,1)S(1)} %get-tuple-element.21), channel_id=1, source_target_pairs={{0,1},{1,2},{2,3},{3,0},{4,5},{5,6},{6,7},{7,4},{8,9},{9,10},{10,1... | collective-permute-start | bytes 3538952 | tf_op jit(solution)/shard_map/ppermute | solution.py:623
  559.5 28.9 %collective-permute-start.1 = (bf16[1,24,192,128]{3,2,1,0:T(8,128)(2,1)S(1)}, bf16[1,24,192,128]{3,2,1,0:T(8,128)(2,1)S(1)}, u32[]{:S(2)}, u32[]{:S(2)}) collective-permute-start(bf16[1,24,192,128]{3,2,1,0:T(8,128)(2,1)S(1)} %get-tuple-element.22), channel_id=1, source_target_pairs={{0,2},{1,3},{2,0},{3,1},{4,6},{5,7},{6,4},{7,5},{8,10},{9,11},{10,... | collective-permute-start | bytes 3538952 | tf_op jit(solution)/shard_map/ppermute | solution.py:623
  561.0 51.0 %collective-permute-start.2 = (bf16[1,24,192,128]{3,2,1,0:T(8,128)(2,1)S(1)}, bf16[1,24,192,128]{3,2,1,0:T(8,128)(2,1)S(1)}, u32[]{:S(2)}, u32[]{:S(2)}) collective-permute-start(bf16[1,24,192,128]{3,2,1,0:T(8,128)(2,1)S(1)} %get-tuple-element.23), channel_id=1, source_target_pairs={{0,3},{1,0},{2,1},{3,2},{4,7},{5,4},{6,5},{7,6},{8,11},{9,8},{10,9... | collective-permute-start | bytes 3538952 | tf_op jit(solution)/shard_map/ppermute | solution.py:623
  617.5 1.0 copy-start.4
Sparse Core Ops, SparseCore 0:
  22.8 97.2 all-gather.6
  242.4 66.6 all-gather.8
  312.0 92.2 all-gather.10

commit v4 on v2

--- a/solution.py
+++ b/solution.py
@@ -11,6 +11,7 @@
 norm_eps = 1e-05
 log2e = 1.4426950408889634
 far_below = -1e30
+safe_product = 50.0
 lanes = 128
 both_axes = ("wide", "narrow")
 
@@ -32,6 +33,11 @@
     centred = features - average
     spread = jnp.mean(centred * centred, axis=-1, keepdims=True)
     return (centred * lax.rsqrt(spread + norm_eps)).astype(jnp.bfloat16)
+
+
+def masked_bias(bias, allowed):
+    bias = jnp.where(allowed, bias * log2e, far_below)
+    return bias - jnp.max(bias, axis=-1, keepdims=True)
 
 
 def pack_projection(w_proj, head_count, head_dim):
@@ -85,9 +91,10 @@
     main = cols // lanes
     half_lanes = lanes // 2
     low = lax.broadcasted_iota(jnp.int32, (1, lanes), 1) < half_lanes
-    for n in range(0, got_ref.shape[0], 2):
-        for h in range(got_ref.shape[1]):
-            blocks = []
+
+    def one_head(h, _):
+        placed = []
+        for n in range(0, got_ref.shape[0], 2):
             even = [got_ref[n, h, b * rows : (b + 1) * rows] for b in range(main)]
             odd = [got_ref[n + 1, h, b * rows : (b + 1) * rows] for b in range(main)]
             even_tail = got_ref[n, h, main * rows :]
@@ -106,7 +113,14 @@
             for at, block in enumerate(blocks):
                 lane = n * cols + at * lanes
                 allowed = key_ok_ref[:, lane : lane + lanes] > 0
-                out_ref[h, :, lane : lane + lanes] = jnp.where(allowed, block * log2e, far_below)
+                placed.append((lane, jnp.where(allowed, block * log2e, far_below)))
+        top = functools.reduce(jnp.maximum, [block for _, block in placed])
+        top = jnp.max(top, axis=-1, keepdims=True)
+        for lane, block in placed:
+            out_ref[h, :, lane : lane + lanes] = block - top
+        return 0
+
+    lax.fori_loop(0, got_ref.shape[1], one_head, 0)
 
 
 def place_bias(key_ok, gathered, wide_count, rows, cols):
@@ -134,7 +148,7 @@
     queries = got_ref.shape[-1]
     plane = got_ref[:, 0, 0].reshape(-1, queries)
     allowed = key_ok_ref[...] > 0
-    out_ref[0] = jnp.where(allowed, plane.T * log2e, far_below)
+    out_ref[0] = masked_bias(plane.T, allowed)
 
 
 def turn_bias(key_ok, gathered, part):
@@ -162,7 +176,8 @@
 
 
 def project_kernel(x_ref, w_ref, *rest, head_count, head_dim, normalise, strided):
-    out_ref, scratch = (rest[-2], rest[-1]) if strided else (rest[-1], None)
+    (*rest, scratch) = rest if strided else (*rest, None)
+    sum_ref, (out_ref, norm_ref) = rest[0], rest[-2:]
     width = head_count * head_dim
     pair = 2 * width
     channels = x_ref.shape[-1]
@@ -192,6 +207,11 @@
         lower = (queries - upper.astype(jnp.float32)).astype(jnp.bfloat16)
         spot = lax.broadcasted_iota(jnp.int32, (1, pair), 1)
         queries = jnp.where(spot % (2 * head_dim) < head_dim, upper, lower)
+        for spot, part in enumerate((queries, projected[:, :pair])):
+            squares = part.astype(jnp.float32)
+            squares = (squares * squares).astype(jnp.bfloat16)
+            sums = jnp.dot(squares, sum_ref[...], preferred_element_type=jnp.float32)
+            norm_ref[i, spot : spot + 1, :] = jnp.max(sums, axis=0, keepdims=True)
         for block in range(projected.shape[1] // lanes):
             at = block * lanes
             if first <= at < first + pair:
@@ -210,7 +230,7 @@
         spec = pl.BlockSpec((pieces, per, cols, channels), lambda i: (0, i, 0, 0))
     elif kind == "columns":
         length, count = lines.shape[:2]
-        per = lines_per_step(count, 2)
+        per = 1
         spec = once(lines.shape)
         scratch = [pltpu.VMEM((length * count, channels), jnp.float32)]
     else:
@@ -219,13 +239,17 @@
         spec = pl.BlockSpec((1, length, channels), lambda i: (i, 0, 0))
     outs = packed.shape[1]
     total = count if total is None else total
-    in_specs, operands, aliases = [spec, once(packed.shape)], [lines, packed], {}
+    pair = 2 * head_count * head_dim
+    owner = jnp.arange(pair)[:, None] // (2 * head_dim)
+    sums = (owner == jnp.arange(lanes)[None, :]).astype(jnp.bfloat16)
+    in_specs = [spec, once(packed.shape), once(sums.shape)]
+    operands, aliases = [lines, packed, sums], {}
     if before is not None:
         in_specs.append(pl.BlockSpec(memory_space=pl.ANY))
         operands.append(before)
-        aliases = {2: 0}
+        aliases = {3: 0}
     skip = first // per
-    return pl.pallas_call(
+    out, norms = pl.pallas_call(
         functools.partial(
             project_kernel,
             head_count=head_count,
@@ -233,10 +257,16 @@
             normalise=kind == "rows",
             strided=kind == "columns",
         ),
-        out_shape=jax.ShapeDtypeStruct((total, outs // lanes, length, lanes), jnp.bfloat16),
+        out_shape=[
+            jax.ShapeDtypeStruct((total, outs // lanes, length, lanes), jnp.bfloat16),
+            jax.ShapeDtypeStruct((count, 8, lanes), jnp.float32),
+        ],
         grid=(count // per,),
         in_specs=in_specs,
-        out_specs=pl.BlockSpec((per, outs // lanes, length, lanes), lambda i: (i + skip, 0, 0, 0)),
+        out_specs=[
+            pl.BlockSpec((per, outs // lanes, length, lanes), lambda i: (i + skip, 0, 0, 0)),
+            pl.BlockSpec((per, 8, lanes), lambda i: (i, 0, 0)),
+        ],
         scratch_shapes=scratch,
         input_output_aliases=aliases,
         compiler_params=params(),
@@ -246,9 +276,11 @@
             transcendentals=0,
         ),
     )(*operands)
-
-
-def attend_lines(query_ref, key_ref, bias_refs, oks, head_count, head_dim):
+    most = jnp.max(norms[:, 0, :head_count] * norms[:, 1, :head_count], axis=-1) / 2
+    return out, (most * 1.1 < safe_product**2).astype(jnp.int32)
+
+
+def attend_lines(query_ref, key_ref, bias_refs, oks, bounded, head_count, head_dim):
     width = head_count * head_dim
     pair_blocks = 2 * width // lanes
     length = key_ref.shape[2]
@@ -256,15 +288,13 @@
     owner = lax.broadcasted_iota(jnp.int32, (1, width), 1) // head_dim
     block_heads = lanes // (2 * head_dim)
     nothing = jnp.zeros((), jnp.bfloat16)
-    jobs = [
-        (i, at, h)
-        for i in range(key_ref.shape[0])
-        for at in range(len(bias_refs))
-        for h in range(head_count)
-    ]
-
-    def score(job):
-        i, at, h = job
+
+    def together(ref, i, first, *rest):
+        parts = [ref[(i, first + n) + rest] for n in range(width // lanes)]
+        parts = [part.reshape(-1, lanes) for part in parts]
+        return parts[0] if len(parts) == 1 else jnp.concatenate(parts, axis=1)
+
+    def score(i, at, h):
         block = h // block_heads
         queries = query_ref[i, block, :, at].reshape(-1, lanes)
         return lax.dot_general(
@@ -274,33 +304,55 @@
             preferred_element_type=jnp.float32,
         )
 
-    def together(ref, i, first, *rest):
-        parts = [ref[(i, first + n) + rest] for n in range(width // lanes)]
-        parts = [part.reshape(-1, lanes) for part in parts]
-        return parts[0] if len(parts) == 1 else jnp.concatenate(parts, axis=1)
-
+    def head_sums(i, at, h, scores):
+        scores = scores + bias_refs[at][h].reshape(-1, length)
+        if not bounded:
+            scores = scores - jnp.max(scores, axis=-1, keepdims=True)
+        weights = jnp.exp2(scores).astype(jnp.bfloat16)
+        values = together(key_ref, i, pair_blocks)
+        values_ones = jnp.concatenate([values, jnp.ones_like(values)], axis=1)
+        both_sums = jnp.dot(weights, values_ones, preferred_element_type=jnp.float32)
+        return both_sums[:, :width] / both_sums[:, width:]
+
+    def finish(i, at, summed):
+        even = jnp.full((), 1.0 / length, jnp.float32).astype(jnp.bfloat16)
+        values = together(key_ref, i, pair_blocks)
+        total = jnp.sum(values.astype(jnp.float32), axis=0, keepdims=True)
+        final = jnp.where(oks[i], summed, total * even.astype(jnp.float32))
+        gates = together(query_ref, i, pair_blocks, slice(None), at).astype(jnp.float32)
+        return (jax.nn.sigmoid(gates) * final).astype(jnp.bfloat16)
+
+    spots = [(i, at) for i in range(key_ref.shape[0]) for at in range(len(bias_refs))]
     gated = {}
+    if not bounded:
+        queries = query_ref.shape[2] * query_ref.shape[4]
+        for i, at in spots:
+
+            def one_head(h, summed):
+                return jnp.where(owner == h, head_sums(i, at, h, score(i, at, h)), summed)
+
+            start = jnp.zeros((queries, width), jnp.float32)
+            gated[i, at] = finish(i, at, lax.fori_loop(0, head_count, one_head, start))
+        return gated
+
+    jobs = [(i, at, h) for i, at in spots for h in range(head_count)]
+    coming = score(*jobs[0])
     summed = None
-    coming = score(jobs[0])
     for n, (i, at, h) in enumerate(jobs):
         scores = coming
         if n + 1 < len(jobs):
-            coming = score(jobs[n + 1])
-        scores = scores + bias_refs[at][h].reshape(-1, length)
-        top = jnp.max(scores, axis=-1, keepdims=True)
-        weights = jnp.exp2(scores - top).astype(jnp.bfloat16)
-        values = together(key_ref, i, pair_blocks)
-        values_ones = jnp.concatenate([values, jnp.ones_like(values)], axis=1)
-        both_sums = jnp.dot(weights, values_ones, preferred_element_type=jnp.float32)
-        ratio = both_sums[:, :width] / both_sums[:, width:]
+            coming = score(*jobs[n + 1])
+        ratio = head_sums(i, at, h, scores)
         summed = ratio if h == 0 else jnp.where(owner == h, ratio, summed)
         if h == head_count - 1:
-            even = jnp.full((), 1.0 / length, jnp.float32).astype(jnp.bfloat16)
-            total = jnp.sum(values.astype(jnp.float32), axis=0, keepdims=True)
-            final = jnp.where(oks[i], summed, total * even.astype(jnp.float32))
-            gates = together(query_ref, i, pair_blocks, slice(None), at).astype(jnp.float32)
-            gated[i, at] = (jax.nn.sigmoid(gates) * final).astype(jnp.bfloat16)
+            gated[i, at] = finish(i, at, summed)
     return gated
+
+
+def either_way(bounded_ref, lines, run):
+    bounded = functools.reduce(jnp.minimum, [bounded_ref[line] for line in lines]) > 0
+    pl.when(bounded)(lambda: run(True))
+    pl.when(jnp.logical_not(bounded))(lambda: run(False))
 
 
 def out_of(gated, w_out_ref):
@@ -308,33 +360,37 @@
 
 
 def attend_rows_kernel(
-    row_ok_ref, query_ref, key_ref, bias_ref, w_out_ref, x_ref, w_bias_ref, *rest, **sizes
+    row_ok_ref, bounded_ref, query_ref, key_ref, bias_ref, w_out_ref, x_ref, w_bias_ref, *rest, **sizes
 ):
     upd_ref, next_ref, nbias_ref = rest[-3:]
     per = key_ref.shape[0]
     lines = [pl.program_id(0) * per + i for i in range(per)]
     oks = [row_ok_ref[line] > 0 for line in lines]
-    gated = attend_lines(query_ref, key_ref, [bias_ref], oks, **sizes)
-    for i in range(per):
-        update = out_of(gated[i, 0], w_out_ref)
-        upd_ref[:, i] = update.reshape(upd_ref.shape[0], *upd_ref.shape[2:])
-        features = x_ref[:, i].reshape(-1, x_ref.shape[-1]).astype(jnp.float32)
-        normed = layer_norm(features + update.astype(jnp.float32))
-        got = lax.dot_general(
-            w_bias_ref[...], normed, (((1,), (1,)), ((), ())), preferred_element_type=jnp.float32
-        )
-        for h in range(nbias_ref.shape[0]):
-            nbias_ref[h, pl.ds(lines[i], 1), :] = got[h : h + 1]
-        if len(next_ref.shape) == 4:
-            devices, _, cols, channels = next_ref.shape
-            narrow_count = upd_ref.shape[0]
-            spread = normed.astype(jnp.float32).reshape(
-                narrow_count, devices // narrow_count, cols, channels
+
+    def run(bounded):
+        gated = attend_lines(query_ref, key_ref, [bias_ref], oks, bounded, **sizes)
+        for i in range(per):
+            update = out_of(gated[i, 0], w_out_ref)
+            upd_ref[:, i] = update.reshape(upd_ref.shape[0], *upd_ref.shape[2:])
+            features = x_ref[:, i].reshape(-1, x_ref.shape[-1]).astype(jnp.float32)
+            normed = layer_norm(features + update.astype(jnp.float32))
+            got = lax.dot_general(
+                w_bias_ref[...], normed, (((1,), (1,)), ((), ())), preferred_element_type=jnp.float32
             )
-            spread = spread.transpose(1, 0, 2, 3).reshape(devices, cols, channels)
-            next_ref[:, i] = spread.astype(jnp.bfloat16)
-        else:
-            next_ref[i] = normed
+            for h in range(nbias_ref.shape[0]):
+                nbias_ref[h, pl.ds(lines[i], 1), :] = got[h : h + 1]
+            if len(next_ref.shape) == 4:
+                devices, _, cols, channels = next_ref.shape
+                narrow_count = upd_ref.shape[0]
+                spread = normed.astype(jnp.float32).reshape(
+                    narrow_count, devices // narrow_count, cols, channels
+                )
+                spread = spread.transpose(1, 0, 2, 3).reshape(devices, cols, channels)
+                next_ref[:, i] = spread.astype(jnp.bfloat16)
+            else:
+                next_ref[i] = normed
+
+    either_way(bounded_ref, lines, run)
 
 
 def line_specs(projected, plan, per, first, parts, skip):
@@ -345,14 +401,14 @@
     at = first // parts
     specs = [
         pl.BlockSpec(
-            (per, half, blocks, parts, piece, lanes), lambda i, ok: (i + skip, 1, 0, at, 0, 0)
-        ),
-        pl.BlockSpec((per, half, length, lanes), lambda i, ok: (i + skip, 0, 0, 0)),
+            (per, half, blocks, parts, piece, lanes), lambda i, *_: (i + skip, 1, 0, at, 0, 0)
+        ),
+        pl.BlockSpec((per, half, length, lanes), lambda i, *_: (i + skip, 0, 0, 0)),
     ]
     return specs, [cut, projected]
 
 
-def attend_rows(row_ok, projected, lines, bias, w_out, w_bias_rows, chunk, before, plan):
+def attend_rows(row_ok, bounded, projected, lines, bias, w_out, w_bias_rows, chunk, before, plan):
     blocks, chunks, piece, own, wide_count = plan
     pieces, count, cols, channels = lines.shape
     length = pieces * cols
@@ -366,23 +422,23 @@
     per = lines_per_step(count, 2)
     queries = blocks * piece
     line_block = pl.BlockSpec(
-        (pieces, per, inner, None, piece, channels), lambda i, ok: (0, i, 0, chunk, 0, 0)
+        (pieces, per, inner, None, piece, channels), lambda i, *_: (0, i, 0, chunk, 0, 0)
     )
     if direct:
         next_shape = (wide_count * pieces, count, own, channels)
         next_spec = pl.BlockSpec(
-            (wide_count * pieces, per, own, channels), lambda i, ok: (0, i, 0, 0)
+            (wide_count * pieces, per, own, channels), lambda i, *_: (0, i, 0, 0)
         )
     else:
         next_shape = (count, queries, channels)
-        next_spec = pl.BlockSpec((per, queries, channels), lambda i, ok: (i, 0, 0))
+        next_spec = pl.BlockSpec((per, queries, channels), lambda i, *_: (i, 0, 0))
     nbias_shape = (head_count, count, queries)
     scores = count * head_count * length * queries
     in_specs, operands = line_specs(projected, plan, per, chunk, 1, 0)
     in_specs += [
         pl.BlockSpec(
             (head_count, blocks, None, piece, length),
-            lambda i, ok: (0, 0, chunk, 0, 0),
+            lambda i, *_: (0, 0, chunk, 0, 0),
             pipeline_mode=pl.Buffered(1),
         ),
         once(w_out.shape),
@@ -394,7 +450,7 @@
     if before is not None:
         in_specs.append(pl.BlockSpec(memory_space=pl.ANY))
         operands.append(before)
-        aliases = {len(operands): 0}
+        aliases = {len(operands) + 1: 0}
     upd, nxt, nbias = pl.pallas_call(
         functools.partial(attend_rows_kernel, head_count=head_count, head_dim=head_dim),
         out_shape=[
@@ -403,10 +459,10 @@
             jax.ShapeDtypeStruct(nbias_shape, jnp.float32),
         ],
         grid_spec=pltpu.PrefetchScalarGridSpec(
-            num_scalar_prefetch=1,
+            num_scalar_prefetch=2,
             grid=(count // per,),
             in_specs=in_specs,
-            out_specs=[line_block, next_spec, pl.BlockSpec(nbias_shape, lambda i, ok: (0, 0, 0))],
+            out_specs=[line_block, next_spec, pl.BlockSpec(nbias_shape, lambda i, *_: (0, 0, 0))],
         ),
         input_output_aliases=aliases,
         compiler_params=params(),
@@ -414,33 +470,37 @@
             flops=4 * scores * 128, bytes_accessed=8 * lines.size, transcendentals=scores
         ),
         name="attend_rows",
-    )(row_ok, *operands)
+    )(row_ok, bounded, *operands)
     if not direct:
         nxt = nxt.reshape(count, pieces, wide_count, own, channels).transpose(2, 1, 0, 3, 4)
         nxt = nxt.reshape(wide_count * pieces, count, own, channels)
     return upd, nxt, nbias
 
 
-def attend_columns_kernel(col_ok_ref, query_ref, key_ref, *rest, parts, **sizes):
+def attend_columns_kernel(col_ok_ref, bounded_ref, query_ref, key_ref, *rest, parts, **sizes):
     bias_refs, w_out_ref, out_ref = rest[:parts], rest[parts], rest[parts + 1]
     scratch = rest[parts + 2 :]
     per = key_ref.shape[0]
     blocks, piece = query_ref.shape[2], query_ref.shape[4]
     lines = [pl.program_id(0) * per + i for i in range(per)]
     oks = [col_ok_ref[line] > 0 for line in lines]
-    gated = attend_lines(query_ref, key_ref, bias_refs, oks, **sizes)
-    for i in range(per):
-        for at in range(parts):
-            update = out_of(gated[i, at], w_out_ref)
-            if not scratch:
-                out_ref[:, i] = update.reshape(blocks, piece, update.shape[1])
-                continue
-            stride = out_ref.shape[2]
-            for m in range(blocks):
-                first = (m * parts + at) * piece * stride + lines[i]
-                scratch[0][pl.ds(first, piece, stride=stride), :] = update[
-                    m * piece : (m + 1) * piece
-                ].astype(jnp.float32)
+
+    def run(bounded):
+        gated = attend_lines(query_ref, key_ref, bias_refs, oks, bounded, **sizes)
+        for i in range(per):
+            for at in range(parts):
+                update = out_of(gated[i, at], w_out_ref)
+                if not scratch:
+                    out_ref[:, i] = update.reshape(blocks, piece, update.shape[1])
+                    continue
+                stride = out_ref.shape[2]
+                for m in range(blocks):
+                    first = (m * parts + at) * piece * stride + lines[i]
+                    scratch[0][pl.ds(first, piece, stride=stride), :] = update[
+                        m * piece : (m + 1) * piece
+                    ].astype(jnp.float32)
+
+    either_way(bounded_ref, lines, run)
     if scratch:
 
         @pl.when(pl.program_id(0) == pl.num_programs(0) - 1)
@@ -448,7 +508,7 @@
             out_ref[...] = scratch[0][...].reshape(out_ref.shape).astype(jnp.bfloat16)
 
 
-def attend_columns(col_ok, projected, biases, w_out, first, skip, plan):
+def attend_columns(col_ok, bounded, projected, biases, w_out, first, skip, plan):
     blocks, _, piece, own, _ = plan
     length = projected.shape[2]
     count = col_ok.shape[0]
@@ -460,11 +520,11 @@
     per = lines_per_step(count, 2) if parts == 1 else 1
     if own % 8 == 0:
         out_shape = (blocks, parts * piece, count, width)
-        out_spec = pl.BlockSpec(out_shape, lambda i, ok: (0, 0, 0, 0))
+        out_spec = pl.BlockSpec(out_shape, lambda i, *_: (0, 0, 0, 0))
         scratch = [pltpu.VMEM((blocks * parts * piece * count, width), jnp.float32)]
     else:
         out_shape = (blocks, count, parts * piece, width)
-        out_spec = pl.BlockSpec((blocks, per, parts * piece, width), lambda i, ok: (0, i, 0, 0))
+        out_spec = pl.BlockSpec((blocks, per, parts * piece, width), lambda i, *_: (0, i, 0, 0))
         scratch = []
     in_specs, operands = line_specs(projected, plan, per, first, parts, skip // per)
     return pl.pallas_call(
@@ -473,7 +533,7 @@
         ),
         out_shape=jax.ShapeDtypeStruct(out_shape, jnp.bfloat16),
         grid_spec=pltpu.PrefetchScalarGridSpec(
-            num_scalar_prefetch=1,
+            num_scalar_prefetch=2,
             grid=(count // per,),
             in_specs=in_specs + [once(biases[0].shape)] * parts + [once(w_out.shape)],
             out_specs=out_spec,
@@ -484,7 +544,7 @@
             flops=4 * scores * 128, bytes_accessed=8 * count * length * width, transcendentals=scores
         ),
         name="attend_columns",
-    )(col_ok, *operands, *biases, w_out)
+    )(col_ok, bounded, *operands, *biases, w_out)
 
 
 def settle_kernel(*refs, order, plan):
@@ -576,13 +636,13 @@
         tiled=True,
     )
     packed_start = pack_projection(w_proj_start, head_count, head_dim)
-    projected = project(lines, packed_start, head_count, head_dim, "rows")
+    projected, bounded = project(lines, packed_start, head_count, head_dim, "rows")
     if dense:
         bias = place_bias(key_ok, gathered, wide_count, tile_rows, tile_cols)
     else:
         bias = gathered.reshape(wide_count, narrow_count, head_count, tile_rows, tile_cols)
         bias = bias.transpose(2, 0, 3, 1, 4).reshape(head_count, length, length)
-        bias = jnp.where(key_ok > 0, bias * log2e, far_below)
+        bias = masked_bias(bias, key_ok > 0)
 
     row_ok = lax.dynamic_slice_in_dim(
         key_ok, wide_at * tile_rows + narrow_at * row_count, row_count
@@ -593,7 +653,7 @@
     upd = None
     for step, j in enumerate(order):
         upd, nxt, nbias = attend_rows(
-            row_ok, projected, lines, bias, w_out_start, w_bias_rows, j, upd, plan
+            row_ok, bounded, projected, lines, bias, w_out_start, w_bias_rows, j, upd, plan
         )
         waiting.append((j, nbias))
         if step in (0, chunks - 1):
@@ -605,7 +665,7 @@
                     turned = turn_bias(key_ok, got, n)
                 else:
                     turned = got[:, n].transpose(1, 3, 0, 2).reshape(head_count, -1, length)
-                    turned = jnp.where(key_ok > 0, turned * log2e, far_below)
+                    turned = masked_bias(turned, key_ok > 0)
                 next_biases[k] = turned
             waiting = []
         got = lax.all_to_all(nxt, both_axes, split_axis=0, concat_axis=0, tiled=True)
@@ -627,12 +687,12 @@
     update_start = update_start.reshape(tile_rows, tile_cols, channels)
 
     packed_end = pack_projection(w_proj_end, head_count, head_dim)
-    projected_end, col_ok = None, []
+    projected_end, col_ok, bounded_end = None, [], []
     for step, j in enumerate(order):
         lines_end = columns[j]
         if own % 8:
             lines_end = lines_end.transpose(1, 0, 2)
-        projected_end = project(
+        projected_end, bounded = project(
             lines_end,
             packed_end,
             head_count,
@@ -645,9 +705,11 @@
         at = wide_at * own + jnp.arange(own)
         at = narrow_at * tile_cols + at // piece * tile_rows + j * piece + at % piece
         col_ok.append(key_ok[at])
+        bounded_end.append(bounded)
 
     got = attend_columns(
         jnp.concatenate(col_ok),
+        jnp.concatenate(bounded_end),
         projected_end,
         [next_biases[order[0]]],
         w_out_end,
@@ -663,6 +725,7 @@
     for step, j in enumerate(order):
         got = attend_columns(
             col_ok[step],
+            bounded_end[step],
             projected_end,
             [next_biases[k] for k in range(chunks - 1)],
             w_out_end,

time: 580 us -> 577 us (level)
  Pallas kernels: 290 us -> 283 us
  other arithmetic: 4.57 us -> 10.7 us
    pallas_call x4, Pallas kernels: 108 us -> 95 us  [attend_columns(): pl.pallas_call(functools.partial(attend_columns_kernel, parts=parts, head...]
    pallas_call x4, Pallas kernels: 39.7 us -> 49.6 us  [project(): pl.pallas_call(functools.partial(project_kernel, head_count=head_count, h...]
    pallas_call x3, Pallas kernels: 111 us -> 101 us  [attend_rows(): pl.pallas_call(functools.partial(attend_rows_kernel, head_count=head_coun...]
    all_to_all x2, waiting for transfers between devices: 36.8 us -> 27.7 us  [on_device(): lax.all_to_all(nxt, both_axes, split_axis=0, concat_axis=0, tiled=True)]
    all_to_all x3, waiting for transfers between devices: 2.14 us -> 8.16 us  [on_device(): lax.all_to_all(got, 'wide', split_axis=0, concat_axis=0, tiled=True)]
    unnamed x40 -> x46, local copies, waits for them, and re-layouts: 12.2 us -> 12.1 us
  transfers between devices with their start and end apart: 13 -> 13, of which waited for: 10 -> 8; matrix products, arithmetic and copies ran while one was open for 2% -> 3% of each run, Pallas kernels for 41% -> 40%
where the time goes in v4:
time: 577 us; the launch traced here: 575 us
  Pallas kernels  283 us (49%)
  waiting for transfers between devices  156 us (27%)
  blocking collectives  56.4 us (10%)
  starting transfers between devices  32.7 us (6%)
  local copies, waits for them, and re-layouts  22.4 us (4%)
  between operations  14.2 us (2%)
  other arithmetic  10.7 us (2%)
    pallas_call x3, Pallas kernels, attend_rows(): pl.pallas_call(functools.partial(attend_rows_kernel, head_count=head_coun...  101 us
    pallas_call x4, Pallas kernels, attend_columns(): pl.pallas_call(functools.partial(attend_columns_kernel, parts=parts, head...  95 us
    all_to_all x1, waiting for transfers between devices, on_device(): lax.all_to_all(tile_in.reshape(narrow_count, row_count, tile_cols, channe...  66.7 us
    all_to_all x1, blocking collectives, on_device(): lax.all_to_all(nxt, both_axes, split_axis=0, concat_axis=0, tiled=True)  56.4 us
    pallas_call x4, Pallas kernels, project(): pl.pallas_call(functools.partial(project_kernel, head_count=head_count, h...  49.6 us
    ppermute x3, waiting for transfers between devices, on_device(): arrived.append(lax.ppermute(leaving[k - 1], 'narrow', ring))  47.4 us
    all_to_all x2, waiting for transfers between devices, on_device(): lax.all_to_all(nxt, both_axes, split_axis=0, concat_axis=0, tiled=True)  27.7 us
    pallas_call x3, Pallas kernels, turn_bias(): pl.pallas_call(turn_bias_kernel, out_shape=jax.ShapeDtypeStruct((head_cou...  14.7 us
  transfers between devices with their start and end apart: 13, of which 8 were waited for; matrix products, arithmetic and copies ran while one was open for 3% of the time, Pallas kernels for 40%

profile of v4, /device:TPU:0, one launch (start us, length us, event | category | flops | bytes accessed | tf_op | source)
XLA Modules:
  0.0 575.2 jit_solution(5120771437341861669)
XLA Ops:
  7.2 0.7 pad.7.w_ref
  7.9 2.3 copy-done.1
  10.2 8.0 %tile_bias.1 = f32[4,96,192]{2,1,0:T(8,128)S(1)} custom-call(bf16[96,192,128]{2,1,0:T(8,128)(2,1)S(1)} %copy-done.1, bf16[16,128]{1,0:T(8,128)(2,1)S(1)} %pad.7.w_ref), custom_call_target="tpu_custom_call" | custom-call | flops 75497472 | bytes 4718592 | tf_op jit(solution)/shard_map/tile_bias/pallas_call | solution.py:63
  18.3 0.8 maximum_maximum_fusion
  19.2 5.1 all-to-all-start
  24.4 0.7 dynamic_slice.13.row_ok_ref
  25.7 0.6 pad.8.w_bias_ref
  26.3 0.7 pad_maximum_fusion.w_ref
  27.0 0.7 fusion.rest_0_
  27.7 66.7 %all-to-all-done.x_ref = bf16[4,24,192,128]{3,2,1,0:T(8,128)(2,1)} async-done(((bf16[4,24,192,128]{3,2,1,0:T(8,128)(2,1)}), bf16[4,24,192,128]{3,2,1,0:T(8,128)(2,1)}, u32[]{:S(2)}, u32[]{:S(2)}) %all-to-all-start) | async-done | bytes 4718624 | tf_op jit(solution)/shard_map/all_to_all | solution.py:631
  94.4 23.0 %shard_map.95 = (bf16[24,6,768,128]{3,2,1,0:T(8,128)(2,1)}, f32[24,8,128]{2,1,0:T(8,128)}) custom-call(bf16[4,24,192,128]{3,2,1,0:T(8,128)(2,1)} %all-to-all-done.x_ref, bf16[128,768]{1,0:T(8,128)(2,1)} %pad_maximum_fusion.w_ref, bf16[256,128]{1,0:T(8,128)(2,1)} %fusion.rest_0_), custom_call_target="tpu_custom_call" | custom-call | flops 3623878656 | bytes 33030144 | tf_op jit(solution)/shard_map/pallas_call | solution.py:252
  117.4 1.2 multiply_reduce_fusion
  118.7 0.5 compare_convert_fusion.4.bounded_ref
  119.2 3.7 copy-done.2
  122.9 7.5 %place_bias.1 = f32[4,768,768]{2,1,0:T(8,128)S(1)} custom-call(s32[1,768]{1,0:T(1,128)S(1)} %broadcast_in_dim.2.key_ok_ref, f32[32,4,144,128]{3,2,1,0:T(8,128)S(1)} %bitcast.37), custom_call_target="tpu_custom_call" | custom-call | flops 2359296 | bytes 18874368 | tf_op jit(solution)/shard_map/place_bias/pallas_call | solution.py:130
  130.4 3.7 copy-done
  134.1 33.6 %attend_rows.3 = (bf16[4,24,2,3,32,128]{5,4,3,2,1,0:T(8,128)(2,1)}, bf16[32,24,8,128]{3,2,1,0:T(8,128)(2,1)}, f32[4,24,256]{2,1,0:T(8,128)}) custom-call(s32[24]{0:T(128)} %dynamic_slice.13.row_ok_ref, s32[24]{0:T(128)} %compare_convert_fusion.4.bounded_ref, bf16[24,6,8,3,32,128]{5,4,3,2,1,0:T(8,128)(2,1)} %bitcast.42, ...), custom_call_target="tpu_custom_call" | custom-call | flops 9663676416 | bytes 18874368 | tf_op jit(solution)/shard_map/attend_rows/pallas_call | solution.py:454
  167.7 6.4 %all-to-all-start.1 = ((bf16[32,24,8,128]{3,2,1,0:T(8,128)(2,1)}), bf16[32,24,8,128]{3,2,1,0:T(8,128)(2,1)S(1)}, u32[]{:S(2)}, u32[]{:S(2)}) async-start(bf16[32,24,8,128]{3,2,1,0:T(8,128)(2,1)} %get-tuple-element.34), calls=%async_computation.1 | async-start | bytes 3145728 | tf_op jit(solution)/shard_map/all_to_all | solution.py:671
  174.2 0.2 all-gather.9.cloned.1.call-start
  174.4 33.7 %attend_rows.4 = (bf16[4,24,2,3,32,128]{5,4,3,2,1,0:T(8,128)(2,1)}, bf16[32,24,8,128]{3,2,1,0:T(8,128)(2,1)}, f32[4,24,256]{2,1,0:T(8,128)}) custom-call(s32[24]{0:T(128)} %dynamic_slice.13.row_ok_ref, s32[24]{0:T(128)} %compare_convert_fusion.4.bounded_ref, bf16[24,6,8,3,32,128]{5,4,3,2,1,0:T(8,128)(2,1)} %bitcast.43, ...), custom_call_target="tpu_custom_call", output_to_operand_aliasing={{0}: (8, {})} | custom-call | flops 9663676416 | bytes 18874368 | tf_op jit(solution)/shard_map/attend_rows/pallas_call | solution.py:454
  208.1 33.8 %attend_rows.5 = (bf16[4,24,2,3,32,128]{5,4,3,2,1,0:T(8,128)(2,1)}, bf16[32,24,8,128]{3,2,1,0:T(8,128)(2,1)}, f32[4,24,256]{2,1,0:T(8,128)}) custom-call(s32[24]{0:T(128)} %dynamic_slice.13.row_ok_ref, s32[24]{0:T(128)} %compare_convert_fusion.4.bounded_ref, bf16[24,6,8,3,32,128]{5,4,3,2,1,0:T(8,128)(2,1)} %bitcast.44, ...), custom_call_target="tpu_custom_call", output_to_operand_aliasing={{0}: (8, {})} | custom-call | flops 9663676416 | bytes 18874368 | tf_op jit(solution)/shard_map/attend_rows/pallas_call | solution.py:454
  242.0 1.6 pad_maximum_fusion.2
  243.6 56.4 %all_to_all.40 = bf16[32,24,8,128]{3,2,1,0:T(8,128)(2,1)} all-to-all(bf16[32,24,8,128]{3,2,1,0:T(8,128)(2,1)S(1)} %copy-done.10), channel_id=1, replica_groups=mesh['wide'=8,'narrow'=4] {'wide','narrow'}, dimensions={0} | all-to-all | bytes 3145728 | tf_op jit(solution)/shard_map/all_to_all | solution.py:671
  300.1 3.2 all-to-all-start.2
  303.3 0.6 gather_fusion
  304.6 0.6 gather_fusion.1
  305.3 0.6 gather_fusion.2
  306.0 0.7 pad_add_fusion.col_ok_ref
  306.6 0.7 pad_maximum_fusion.1.w_ref
  307.3 8.8 %shard_map.96 = (bf16[24,6,768,128]{3,2,1,0:T(8,128)(2,1)}, f32[8,8,128]{2,1,0:T(8,128)}) custom-call(bf16[768,8,128]{2,1,0:T(8,128)(2,1)} %bitcast.53, bf16[128,768]{1,0:T(8,128)(2,1)} %pad_maximum_fusion.1.w_ref, bf16[256,128]{1,0:T(8,128)(2,1)} %fusion.rest_0_), custom_call_target="tpu_custom_call" | custom-call | flops 1207959552 | bytes 11010048 | tf_op jit(solution)/shard_map/pallas_call | solution.py:252
  316.2 8.9 %shard_map.97 = (bf16[24,6,768,128]{3,2,1,0:T(8,128)(2,1)}, f32[8,8,128]{2,1,0:T(8,128)}) custom-call(bf16[768,8,128]{2,1,0:T(8,128)(2,1)} %bitcast.51, bf16[128,768]{1,0:T(8,128)(2,1)} %pad_maximum_fusion.1.w_ref, bf16[256,128]{1,0:T(8,128)(2,1)} %fusion.rest_0_, bf16[24,6,768,128]{3,2,1,0:T(8,128)(2,1)} %get-tuple-element.38.rest_1_), custom_call_target="tpu_custom_call", output_to_operand_aliasing={{0}: (3, {})} | custom-call | flops 1207959552 | bytes 11010048 | tf_op jit(solution)/shard_map/pallas_call | solution.py:252
  325.1 27.7 %all-to-all-done.2 = bf16[32,24,8,128]{3,2,1,0:T(8,128)(2,1)S(1)} async-done(((bf16[32,24,8,128]{3,2,1,0:T(8,128)(2,1)}), bf16[32,24,8,128]{3,2,1,0:T(8,128)(2,1)S(1)}, u32[]{:S(2)}, u32[]{:S(2)}) %all-to-all-start.2) | async-done | bytes 1572896 | tf_op jit(solution)/shard_map/all_to_all | solution.py:671
  352.8 1.1 copy-done.4
  353.9 8.8 %shard_map.98 = (bf16[24,6,768,128]{3,2,1,0:T(8,128)(2,1)}, f32[8,8,128]{2,1,0:T(8,128)}) custom-call(bf16[768,8,128]{2,1,0:T(8,128)(2,1)} %bitcast.50, bf16[128,768]{1,0:T(8,128)(2,1)} %pad_maximum_fusion.1.w_ref, bf16[256,128]{1,0:T(8,128)(2,1)} %fusion.rest_0_, bf16[24,6,768,128]{3,2,1,0:T(8,128)(2,1)} %get-tuple-element.39.rest_1_), custom_call_target="tpu_custom_call", output_to_operand_aliasing={{0}: (3, {})} | custom-call | flops 1207959552 | bytes 11010048 | tf_op jit(solution)/shard_map/pallas_call | solution.py:252
  362.8 1.0 multiply_reduce_fusion.3
  363.7 1.0 multiply_reduce_fusion.1
  364.7 1.0 multiply_reduce_fusion.2
  365.7 0.7 pad_add_fusion.1.bounded_ref
  366.4 4.9 turn_bias.5.rest_0_
  371.3 29.7 %attend_columns.7 = bf16[8,32,24,128]{3,2,1,0:T(8,128)(2,1)} custom-call(s32[24]{0:T(128)} %pad_add_fusion.col_ok_ref, s32[24]{0:T(128)} %pad_add_fusion.1.bounded_ref, bf16[24,6,8,3,32,128]{5,4,3,2,1,0:T(8,128)(2,1)} %bitcast.38, bf16[24,6,768,128]{3,2,1,0:T(8,128)(2,1)} %get-tuple-element.40.key_ref, f32[4,256,768]{2,1,0:T(8,128)} %turn_bias.5.rest_0_, ...), custom_call_target="tpu_custom_call" | custom-call | flops 9663676416 | bytes 18874368 | tf_op jit(solution)/shard_map/attend_columns/pallas_call | solution.py:530
  401.0 3.6 all-to-all-start.7
  404.6 4.9 turn_bias.3.rest_0_
  409.5 4.9 turn_bias.4.rest_1_
  414.4 21.8 %attend_columns.4 = bf16[8,64,8,128]{3,2,1,0:T(8,128)(2,1)} custom-call(s32[8]{0:T(128)} %copy-done.16, s32[8]{0:T(128)} %copy-done.20, bf16[24,6,8,3,32,128]{5,4,3,2,1,0:T(8,128)(2,1)} %bitcast.39, bf16[24,6,768,128]{3,2,1,0:T(8,128)(2,1)} %get-tuple-element.40.key_ref, f32[4,256,768]{2,1,0:T(8,128)} %turn_bias.3.rest_0_, f32[4,256,768]{2,1,0:T(8,128)} %turn_bias.4.rest_1_, ...), custom_call_target="tpu_custom_call" | custom-call | flops 6442450944 | bytes 6291456 | tf_op jit(solution)/shard_map/attend_columns/pallas_call | solution.py:530
  436.2 5.8 %all-to-all-done.7.refs_0_ = bf16[8,32,24,128]{3,2,1,0:T(8,128)(2,1)S(1)} async-done(((bf16[8,32,24,128]{3,2,1,0:T(8,128)(2,1)}), bf16[8,32,24,128]{3,2,1,0:T(8,128)(2,1)S(1)}, u32[]{:S(2)}, u32[]{:S(2)}) %all-to-all-start.7) | async-done | bytes 1572896 | tf_op jit(solution)/shard_map/all_to_all | solution.py:720
  442.0 3.8 all-to-all-start.4
  445.8 21.8 %attend_columns.5 = bf16[8,64,8,128]{3,2,1,0:T(8,128)(2,1)} custom-call(s32[8]{0:T(128)} %copy-done.18, s32[8]{0:T(128)} %copy-done.15, bf16[24,6,8,3,32,128]{5,4,3,2,1,0:T(8,128)(2,1)} %bitcast.40, bf16[24,6,768,128]{3,2,1,0:T(8,128)(2,1)} %get-tuple-element.40.key_ref, f32[4,256,768]{2,1,0:T(8,128)} %turn_bias.3.rest_0_, f32[4,256,768]{2,1,0:T(8,128)} %turn_bias.4.rest_1_, ...), custom_call_target="tpu_custom_call" | custom-call | flops 6442450944 | bytes 6291456 | tf_op jit(solution)/shard_map/attend_columns/pallas_call | solution.py:530
  467.6 4.0 all-to-all-done.4.refs_0_
  471.7 3.6 all-to-all-start.5
  475.2 21.8 %attend_columns.6 = bf16[8,64,8,128]{3,2,1,0:T(8,128)(2,1)} custom-call(s32[8]{0:T(128)} %copy-done.17, s32[8]{0:T(128)} %copy-done.14, bf16[24,6,8,3,32,128]{5,4,3,2,1,0:T(8,128)(2,1)} %bitcast.41, bf16[24,6,768,128]{3,2,1,0:T(8,128)(2,1)} %get-tuple-element.40.key_ref, f32[4,256,768]{2,1,0:T(8,128)} %turn_bias.3.rest_0_, f32[4,256,768]{2,1,0:T(8,128)} %turn_bias.4.rest_1_, ...), custom_call_target="tpu_custom_call" | custom-call | flops 6442450944 | bytes 6291456 | tf_op jit(solution)/shard_map/attend_columns/pallas_call | solution.py:530
  497.0 4.1 all-to-all-done.5.refs_1_
  501.2 3.6 all-to-all-start.6
  504.8 2.2 constant_dynamic-slice_fusion
  507.1 1.6 collective-permute-start.1
  508.7 1.4 collective-permute-start.2
  510.1 24.6 %collective-permute-done = bf16[1,24,192,128]{3,2,1,0:T(8,128)(2,1)S(1)} collective-permute-done((bf16[1,24,192,128]{3,2,1,0:T(8,128)(2,1)S(1)}, bf16[1,24,192,128]{3,2,1,0:T(8,128)(2,1)S(1)}, u32[]{:S(2)}, u32[]{:S(2)}) %collective-permute-start) | collective-permute-done | bytes 1179680 | tf_op jit(solution)/shard_map/ppermute | solution.py:682
  534.7 1.1 constant_dynamic-update-slice_fusion.2
  535.8 0.2 collective-permute-done.1
  536.0 1.1 constant_dynamic-update-slice_fusion.1
  537.1 22.6 %collective-permute-done.2 = bf16[1,24,192,128]{3,2,1,0:T(8,128)(2,1)S(1)} collective-permute-done((bf16[1,24,192,128]{3,2,1,0:T(8,128)(2,1)S(1)}, bf16[1,24,192,128]{3,2,1,0:T(8,128)(2,1)S(1)}, u32[]{:S(2)}, u32[]{:S(2)}) %collective-permute-start.2) | collective-permute-done | bytes 1179680 | tf_op jit(solution)/shard_map/ppermute | solution.py:682
  559.7 1.1 constant_dynamic-update-slice_fusion
  560.7 2.5 settle.2.refs_3_
  563.2 1.0 copy-done.8
  564.2 4.4 settle.3
  (76 shorter events, 1.6 us)
Async XLA Ops:
  7.2 112.0 %all-gather.7.cloned.1.call-start = ((), (), s32[]{:S(2)}) async-start(), calls=%async_computation.8 | async-start | bytes 9732096 | tf_op jit(solution)/shard_map/all_gather | solution.py:629
  7.9 2.3 copy-start.1
  19.2 5.2 copy-start.19
  19.2 5.9 %copy-start.11 = (bf16[128,512]{1,0:T(8,128)(2,1)S(1)}, bf16[128,512]{1,0:T(8,128)(2,1)}, u32[]{:S(2)}) copy-start(bf16[128,512]{1,0:T(8,128)(2,1)} %param.10) | copy-start | bytes 393220
  19.2 6.5 %copy-start.21 = (bf16[128,4]{0,1:T(4,128)(2,1)S(1)}, bf16[128,4]{0,1:T(4,128)(2,1)}, u32[]{:S(2)}) copy-start(bf16[128,4]{0,1:T(4,128)(2,1)} %param.14) | copy-start | bytes 3076
  19.2 75.2 %all-to-all-start = ((bf16[4,24,192,128]{3,2,1,0:T(8,128)(2,1)}), bf16[4,24,192,128]{3,2,1,0:T(8,128)(2,1)}, u32[]{:S(2)}, u32[]{:S(2)}) async-start(bf16[4,24,192,128]{3,2,1,0:T(8,128)(2,1)} %bitcast.36), calls=%async_computation | async-start | bytes 9437184 | tf_op jit(solution)/shard_map/all_to_all | solution.py:631
  24.3 342.1 %all-gather.11.cloned.1.call-start = ((), (), s32[]{:S(2)}) async-start(), calls=%async_computation.10 | async-start | bytes 3244032 | tf_op jit(solution)/shard_map/all_gather | solution.py:660
  24.4 94.8 %copy-start.3 = (s32[1,768]{1,0:T(1,128)}, s32[1,768]{1,0:T(1,128)S(1)}, u32[]{:S(2)}) copy-start(s32[1,768]{1,0:T(1,128)S(1)} %broadcast_in_dim.2.key_ok_ref) | copy-start | bytes 9220
  119.2 3.7 copy-start.2
  130.4 3.7 copy-start
  167.7 75.9 %all-to-all-start.1 = ((bf16[32,24,8,128]{3,2,1,0:T(8,128)(2,1)}), bf16[32,24,8,128]{3,2,1,0:T(8,128)(2,1)S(1)}, u32[]{:S(2)}, u32[]{:S(2)}) async-start(bf16[32,24,8,128]{3,2,1,0:T(8,128)(2,1)} %get-tuple-element.34), calls=%async_computation.1 | async-start | bytes 3145728 | tf_op jit(solution)/shard_map/all_to_all | solution.py:671
  174.2 230.4 %all-gather.9.cloned.1.call-start = ((), (), s32[]{:S(2)}) async-start(), calls=%async_computation.9 | async-start | bytes 6488064 | tf_op jit(solution)/shard_map/all_gather | solution.py:660
  208.1 33.9 %copy-start.13 = (f32[4,24,256]{2,1,0:T(8,128)S(1)}, f32[4,24,256]{2,1,0:T(8,128)}, u32[]{:S(2)}) copy-start(f32[4,24,256]{2,1,0:T(8,128)} %get-tuple-element.41) | copy-start | bytes 294916
  208.1 35.5 %copy-start.10 = (bf16[32,24,8,128]{3,2,1,0:T(8,128)(2,1)S(1)}, bf16[32,24,8,128]{3,2,1,0:T(8,128)(2,1)}, u32[]{:S(2)}) copy-start(bf16[32,24,8,128]{3,2,1,0:T(8,128)(2,1)} %get-tuple-element.37) | copy-start | bytes 4718596
  242.0 62.0 %copy-start.12 = (bf16[128,512]{1,0:T(8,128)(2,1)S(1)}, bf16[128,512]{1,0:T(8,128)(2,1)}, u32[]{:S(2)}) copy-start(bf16[128,512]{1,0:T(8,128)(2,1)} %param.13) | copy-start | bytes 393220
  243.6 63.7 %copy-start.9 = (bf16[32,24,8,128]{3,2,1,0:T(8,128)(2,1)}, bf16[32,24,8,128]{3,2,1,0:T(8,128)(2,1)S(1)}, u32[]{:S(2)}) copy-start(bf16[32,24,8,128]{3,2,1,0:T(8,128)(2,1)S(1)} %all-to-all-done.1) | copy-start | bytes 4718596
  300.1 52.7 %all-to-all-start.2 = ((bf16[32,24,8,128]{3,2,1,0:T(8,128)(2,1)}), bf16[32,24,8,128]{3,2,1,0:T(8,128)(2,1)S(1)}, u32[]{:S(2)}, u32[]{:S(2)}) async-start(bf16[32,24,8,128]{3,2,1,0:T(8,128)(2,1)} %get-tuple-element.36), calls=%async_computation.2 | async-start | bytes 3145728 | tf_op jit(solution)/shard_map/all_to_all | solution.py:671
  304.0 21.1 %copy-start.16 = (s32[8]{0:T(128)}, s32[8]{0:T(128)S(1)}, u32[]{:S(2)}) copy-start(s32[8]{0:T(128)S(1)} %gather_fusion) | copy-start | bytes 100
  305.3 19.8 %copy-start.18 = (s32[8]{0:T(128)}, s32[8]{0:T(128)S(1)}, u32[]{:S(2)}) copy-start(s32[8]{0:T(128)S(1)} %gather_fusion.1) | copy-start | bytes 100
  305.9 19.1 %copy-start.17 = (s32[8]{0:T(128)}, s32[8]{0:T(128)S(1)}, u32[]{:S(2)}) copy-start(s32[8]{0:T(128)S(1)} %gather_fusion.2) | copy-start | bytes 100
  352.8 1.1 copy-start.4
  365.7 35.3 %copy-start.20 = (s32[8]{0:T(128)}, s32[8]{0:T(128)S(1)}, u32[]{:S(2)}) copy-start(s32[8]{0:T(128)S(1)} %compare_convert_fusion.3.bounded_ref) | copy-start | bytes 100
  365.7 35.3 %copy-start.14 = (s32[8]{0:T(128)}, s32[8]{0:T(128)S(1)}, u32[]{:S(2)}) copy-start(s32[8]{0:T(128)S(1)} %get-tuple-element.61.bounded_ref) | copy-start | bytes 100
  365.7 35.3 %copy-start.15 = (s32[8]{0:T(128)}, s32[8]{0:T(128)S(1)}, u32[]{:S(2)}) copy-start(s32[8]{0:T(128)S(1)} %get-tuple-element.62.bounded_ref) | copy-start | bytes 100
  401.0 41.0 %all-to-all-start.7 = ((bf16[8,32,24,128]{3,2,1,0:T(8,128)(2,1)}), bf16[8,32,24,128]{3,2,1,0:T(8,128)(2,1)S(1)}, u32[]{:S(2)}, u32[]{:S(2)}) async-start(bf16[8,32,24,128]{3,2,1,0:T(8,128)(2,1)} %attend_columns.7), calls=%async_computation.7 | async-start | bytes 3145728 | tf_op jit(solution)/shard_map/all_to_all | solution.py:720
  442.0 25.6 %copy-start.5 = (bf16[8,32,24,128]{3,2,1,0:T(8,128)(2,1)}, bf16[8,32,24,128]{3,2,1,0:T(8,128)(2,1)S(1)}, u32[]{:S(2)}) copy-start(bf16[8,32,24,128]{3,2,1,0:T(8,128)(2,1)S(1)} %all-to-all-done.7.refs_0_) | copy-start | bytes 4718596
  442.0 29.6 %all-to-all-start.4 = ((bf16[8,64,8,128]{3,2,1,0:T(8,128)(2,1)}), bf16[8,64,8,128]{3,2,1,0:T(8,128)(2,1)S(1)}, u32[]{:S(2)}, u32[]{:S(2)}) async-start(bf16[8,64,8,128]{3,2,1,0:T(8,128)(2,1)} %attend_columns.4), calls=%async_computation.4 | async-start | bytes 2097152 | tf_op jit(solution)/shard_map/all_to_all | solution.py:736
  471.7 25.4 %copy-start.6 = (bf16[8,64,8,128]{3,2,1,0:T(8,128)(2,1)}, bf16[8,64,8,128]{3,2,1,0:T(8,128)(2,1)S(1)}, u32[]{:S(2)}) copy-start(bf16[8,64,8,128]{3,2,1,0:T(8,128)(2,1)S(1)} %all-to-all-done.4.refs_0_) | copy-start | bytes 3145732
  471.7 29.5 %all-to-all-start.5 = ((bf16[8,64,8,128]{3,2,1,0:T(8,128)(2,1)}), bf16[8,64,8,128]{3,2,1,0:T(8,128)(2,1)S(1)}, u32[]{:S(2)}, u32[]{:S(2)}) async-start(bf16[8,64,8,128]{3,2,1,0:T(8,128)(2,1)} %attend_columns.5), calls=%async_computation.5 | async-start | bytes 2097152 | tf_op jit(solution)/shard_map/all_to_all | solution.py:736
  501.2 34.6 %copy-start.7 = (bf16[8,64,8,128]{3,2,1,0:T(8,128)(2,1)}, bf16[8,64,8,128]{3,2,1,0:T(8,128)(2,1)S(1)}, u32[]{:S(2)}) copy-start(bf16[8,64,8,128]{3,2,1,0:T(8,128)(2,1)S(1)} %all-to-all-done.5.refs_1_) | copy-start | bytes 3145732
  501.2 62.0 %all-to-all-start.6 = ((bf16[8,64,8,128]{3,2,1,0:T(8,128)(2,1)}), bf16[8,64,8,128]{3,2,1,0:T(8,128)(2,1)S(1)}, u32[]{:S(2)}, u32[]{:S(2)}) async-start(bf16[8,64,8,128]{3,2,1,0:T(8,128)(2,1)} %attend_columns.6), calls=%async_computation.6 | async-start | bytes 2097152 | tf_op jit(solution)/shard_map/all_to_all | solution.py:736
  507.0 27.7 %collective-permute-start = (bf16[1,24,192,128]{3,2,1,0:T(8,128)(2,1)S(1)}, bf16[1,24,192,128]{3,2,1,0:T(8,128)(2,1)S(1)}, u32[]{:S(2)}, u32[]{:S(2)}) collective-permute-start(bf16[1,24,192,128]{3,2,1,0:T(8,128)(2,1)S(1)} %get-tuple-element.31), channel_id=1, source_target_pairs={{0,1},{1,2},{2,3},{3,0},{4,5},{5,6},{6,7},{7,4},{8,9},{9,10},{10,1... | collective-permute-start | bytes 3538952 | tf_op jit(solution)/shard_map/ppermute | solution.py:682
  507.1 28.9 %collective-permute-start.1 = (bf16[1,24,192,128]{3,2,1,0:T(8,128)(2,1)S(1)}, bf16[1,24,192,128]{3,2,1,0:T(8,128)(2,1)S(1)}, u32[]{:S(2)}, u32[]{:S(2)}) collective-permute-start(bf16[1,24,192,128]{3,2,1,0:T(8,128)(2,1)S(1)} %get-tuple-element.32), channel_id=1, source_target_pairs={{0,2},{1,3},{2,0},{3,1},{4,6},{5,7},{6,4},{7,5},{8,10},{9,11},{10,... | collective-permute-start | bytes 3538952 | tf_op jit(solution)/shard_map/ppermute | solution.py:682
  508.7 51.0 %collective-permute-start.2 = (bf16[1,24,192,128]{3,2,1,0:T(8,128)(2,1)S(1)}, bf16[1,24,192,128]{3,2,1,0:T(8,128)(2,1)S(1)}, u32[]{:S(2)}, u32[]{:S(2)}) collective-permute-start(bf16[1,24,192,128]{3,2,1,0:T(8,128)(2,1)S(1)} %get-tuple-element.33), channel_id=1, source_target_pairs={{0,3},{1,0},{2,1},{3,2},{4,7},{5,4},{6,5},{7,6},{8,11},{9,8},{10,9... | collective-permute-start | bytes 3538952 | tf_op jit(solution)/shard_map/ppermute | solution.py:682
  563.2 1.0 copy-start.8
Sparse Core Ops, SparseCore 0:
  19.3 97.3 all-gather.6
  167.9 67.1 all-gather.10
  243.7 97.5 all-gather.8

commit v5 on v4

--- a/solution.py
+++ b/solution.py
@@ -91,10 +91,9 @@
     main = cols // lanes
     half_lanes = lanes // 2
     low = lax.broadcasted_iota(jnp.int32, (1, lanes), 1) < half_lanes
-
-    def one_head(h, _):
-        placed = []
-        for n in range(0, got_ref.shape[0], 2):
+    for n in range(0, got_ref.shape[0], 2):
+        for h in range(got_ref.shape[1]):
+            blocks = []
             even = [got_ref[n, h, b * rows : (b + 1) * rows] for b in range(main)]
             odd = [got_ref[n + 1, h, b * rows : (b + 1) * rows] for b in range(main)]
             even_tail = got_ref[n, h, main * rows :]
@@ -113,14 +112,7 @@
             for at, block in enumerate(blocks):
                 lane = n * cols + at * lanes
                 allowed = key_ok_ref[:, lane : lane + lanes] > 0
-                placed.append((lane, jnp.where(allowed, block * log2e, far_below)))
-        top = functools.reduce(jnp.maximum, [block for _, block in placed])
-        top = jnp.max(top, axis=-1, keepdims=True)
-        for lane, block in placed:
-            out_ref[h, :, lane : lane + lanes] = block - top
-        return 0
-
-    lax.fori_loop(0, got_ref.shape[1], one_head, 0)
+                out_ref[h, :, lane : lane + lanes] = jnp.where(allowed, block * log2e, far_below)
 
 
 def place_bias(key_ok, gathered, wide_count, rows, cols):
@@ -177,7 +169,7 @@
 
 def project_kernel(x_ref, w_ref, *rest, head_count, head_dim, normalise, strided):
     (*rest, scratch) = rest if strided else (*rest, None)
-    sum_ref, (out_ref, norm_ref) = rest[0], rest[-2:]
+    sum_ref, (out_ref, norm_ref) = rest[0], ((rest[-1], None) if normalise else rest[-2:])
     width = head_count * head_dim
     pair = 2 * width
     channels = x_ref.shape[-1]
@@ -207,7 +199,8 @@
         lower = (queries - upper.astype(jnp.float32)).astype(jnp.bfloat16)
         spot = lax.broadcasted_iota(jnp.int32, (1, pair), 1)
         queries = jnp.where(spot % (2 * head_dim) < head_dim, upper, lower)
-        for spot, part in enumerate((queries, projected[:, :pair])):
+        measured = () if normalise else (queries, projected[:, :pair])
+        for spot, part in enumerate(measured):
             squares = part.astype(jnp.float32)
             squares = (squares * squares).astype(jnp.bfloat16)
             sums = jnp.dot(squares, sum_ref[...], preferred_element_type=jnp.float32)
@@ -249,7 +242,8 @@
         operands.append(before)
         aliases = {3: 0}
     skip = first // per
-    out, norms = pl.pallas_call(
+    measured = kind != "rows"
+    got = pl.pallas_call(
         functools.partial(
             project_kernel,
             head_count=head_count,
@@ -260,13 +254,13 @@
         out_shape=[
             jax.ShapeDtypeStruct((total, outs // lanes, length, lanes), jnp.bfloat16),
             jax.ShapeDtypeStruct((count, 8, lanes), jnp.float32),
-        ],
+        ][: 1 + measured],
         grid=(count // per,),
         in_specs=in_specs,
         out_specs=[
             pl.BlockSpec((per, outs // lanes, length, lanes), lambda i: (i + skip, 0, 0, 0)),
             pl.BlockSpec((per, 8, lanes), lambda i: (i, 0, 0)),
-        ],
+        ][: 1 + measured],
         scratch_shapes=scratch,
         input_output_aliases=aliases,
         compiler_params=params(),
@@ -276,6 +270,9 @@
             transcendentals=0,
         ),
     )(*operands)
+    if not measured:
+        return got[0]
+    out, norms = got
     most = jnp.max(norms[:, 0, :head_count] * norms[:, 1, :head_count], axis=-1) / 2
     return out, (most * 1.1 < safe_product**2).astype(jnp.int32)
 
@@ -324,7 +321,7 @@
 
     spots = [(i, at) for i in range(key_ref.shape[0]) for at in range(len(bias_refs))]
     gated = {}
-    if not bounded:
+    if bounded is False:
         queries = query_ref.shape[2] * query_ref.shape[4]
         for i, at in spots:
 
@@ -360,37 +357,33 @@
 
 
 def attend_rows_kernel(
-    row_ok_ref, bounded_ref, query_ref, key_ref, bias_ref, w_out_ref, x_ref, w_bias_ref, *rest, **sizes
+    row_ok_ref, query_ref, key_ref, bias_ref, w_out_ref, x_ref, w_bias_ref, *rest, **sizes
 ):
     upd_ref, next_ref, nbias_ref = rest[-3:]
     per = key_ref.shape[0]
     lines = [pl.program_id(0) * per + i for i in range(per)]
     oks = [row_ok_ref[line] > 0 for line in lines]
-
-    def run(bounded):
-        gated = attend_lines(query_ref, key_ref, [bias_ref], oks, bounded, **sizes)
-        for i in range(per):
-            update = out_of(gated[i, 0], w_out_ref)
-            upd_ref[:, i] = update.reshape(upd_ref.shape[0], *upd_ref.shape[2:])
-            features = x_ref[:, i].reshape(-1, x_ref.shape[-1]).astype(jnp.float32)
-            normed = layer_norm(features + update.astype(jnp.float32))
-            got = lax.dot_general(
-                w_bias_ref[...], normed, (((1,), (1,)), ((), ())), preferred_element_type=jnp.float32
+    gated = attend_lines(query_ref, key_ref, [bias_ref], oks, None, **sizes)
+    for i in range(per):
+        update = out_of(gated[i, 0], w_out_ref)
+        upd_ref[:, i] = update.reshape(upd_ref.shape[0], *upd_ref.shape[2:])
+        features = x_ref[:, i].reshape(-1, x_ref.shape[-1]).astype(jnp.float32)
+        normed = layer_norm(features + update.astype(jnp.float32))
+        got = lax.dot_general(
+            w_bias_ref[...], normed, (((1,), (1,)), ((), ())), preferred_element_type=jnp.float32
+        )
+        for h in range(nbias_ref.shape[0]):
+            nbias_ref[h, pl.ds(lines[i], 1), :] = got[h : h + 1]
+        if len(next_ref.shape) == 4:
+            devices, _, cols, channels = next_ref.shape
+            narrow_count = upd_ref.shape[0]
+            spread = normed.astype(jnp.float32).reshape(
+                narrow_count, devices // narrow_count, cols, channels
             )
-            for h in range(nbias_ref.shape[0]):
-                nbias_ref[h, pl.ds(lines[i], 1), :] = got[h : h + 1]
-            if len(next_ref.shape) == 4:
-                devices, _, cols, channels = next_ref.shape
-                narrow_count = upd_ref.shape[0]
-                spread = normed.astype(jnp.float32).reshape(
-                    narrow_count, devices // narrow_count, cols, channels
-                )
-                spread = spread.transpose(1, 0, 2, 3).reshape(devices, cols, channels)
-                next_ref[:, i] = spread.astype(jnp.bfloat16)
-            else:
-                next_ref[i] = normed
-
-    either_way(bounded_ref, lines, run)
+            spread = spread.transpose(1, 0, 2, 3).reshape(devices, cols, channels)
+            next_ref[:, i] = spread.astype(jnp.bfloat16)
+        else:
+            next_ref[i] = normed
 
 
 def line_specs(projected, plan, per, first, parts, skip):
@@ -408,7 +401,7 @@
     return specs, [cut, projected]
 
 
-def attend_rows(row_ok, bounded, projected, lines, bias, w_out, w_bias_rows, chunk, before, plan):
+def attend_rows(row_ok, projected, lines, bias, w_out, w_bias_rows, chunk, before, plan):
     blocks, chunks, piece, own, wide_count = plan
     pieces, count, cols, channels = lines.shape
     length = pieces * cols
@@ -422,23 +415,23 @@
     per = lines_per_step(count, 2)
     queries = blocks * piece
     line_block = pl.BlockSpec(
-        (pieces, per, inner, None, piece, channels), lambda i, *_: (0, i, 0, chunk, 0, 0)
+        (pieces, per, inner, None, piece, channels), lambda i, ok: (0, i, 0, chunk, 0, 0)
     )
     if direct:
         next_shape = (wide_count * pieces, count, own, channels)
         next_spec = pl.BlockSpec(
-            (wide_count * pieces, per, own, channels), lambda i, *_: (0, i, 0, 0)
+            (wide_count * pieces, per, own, channels), lambda i, ok: (0, i, 0, 0)
         )
     else:
         next_shape = (count, queries, channels)
-        next_spec = pl.BlockSpec((per, queries, channels), lambda i, *_: (i, 0, 0))
+        next_spec = pl.BlockSpec((per, queries, channels), lambda i, ok: (i, 0, 0))
     nbias_shape = (head_count, count, queries)
     scores = count * head_count * length * queries
     in_specs, operands = line_specs(projected, plan, per, chunk, 1, 0)
     in_specs += [
         pl.BlockSpec(
             (head_count, blocks, None, piece, length),
-            lambda i, *_: (0, 0, chunk, 0, 0),
+            lambda i, ok: (0, 0, chunk, 0, 0),
             pipeline_mode=pl.Buffered(1),
         ),
         once(w_out.shape),
@@ -450,7 +443,7 @@
     if before is not None:
         in_specs.append(pl.BlockSpec(memory_space=pl.ANY))
         operands.append(before)
-        aliases = {len(operands) + 1: 0}
+        aliases = {len(operands): 0}
     upd, nxt, nbias = pl.pallas_call(
         functools.partial(attend_rows_kernel, head_count=head_count, head_dim=head_dim),
         out_shape=[
@@ -459,10 +452,10 @@
             jax.ShapeDtypeStruct(nbias_shape, jnp.float32),
         ],
         grid_spec=pltpu.PrefetchScalarGridSpec(
-            num_scalar_prefetch=2,
+            num_scalar_prefetch=1,
             grid=(count // per,),
             in_specs=in_specs,
-            out_specs=[line_block, next_spec, pl.BlockSpec(nbias_shape, lambda i, *_: (0, 0, 0))],
+            out_specs=[line_block, next_spec, pl.BlockSpec(nbias_shape, lambda i, ok: (0, 0, 0))],
         ),
         input_output_aliases=aliases,
         compiler_params=params(),
@@ -470,7 +463,7 @@
             flops=4 * scores * 128, bytes_accessed=8 * lines.size, transcendentals=scores
         ),
         name="attend_rows",
-    )(row_ok, bounded, *operands)
+    )(row_ok, *operands)
     if not direct:
         nxt = nxt.reshape(count, pieces, wide_count, own, channels).transpose(2, 1, 0, 3, 4)
         nxt = nxt.reshape(wide_count * pieces, count, own, channels)
@@ -517,7 +510,7 @@
     width = w_out.shape[0]
     head_dim = width // head_count
     scores = count * head_count * length * blocks * parts * piece
-    per = lines_per_step(count, 2) if parts == 1 else 1
+    per = lines_per_step(count, 2) if parts == 1 and count > own else 1
     if own % 8 == 0:
         out_shape = (blocks, parts * piece, count, width)
         out_spec = pl.BlockSpec(out_shape, lambda i, *_: (0, 0, 0, 0))
@@ -547,20 +540,20 @@
     )(col_ok, bounded, *operands, *biases, w_out)
 
 
-def settle_kernel(*refs, order, plan):
+def settle_kernel(*refs, places, plan):
     _, chunks, piece, own, wide_count = plan
     tile_rows = chunks * piece
     out_ref = refs[-1]
-    for step, j in enumerate(order):
-        ref, first = (refs[0], step * own) if len(refs) < chunks else (refs[step], 0)
+    for j, (which, step) in enumerate(places):
+        first = step * own
         for w in range(wide_count):
             inner, within = divmod(w * own, piece)
             col = inner * tile_rows + j * piece + within
-            out_ref[:, col : col + own, :] = ref[w, :, first : first + own, :]
-
-
-def settle(parts, first_row, before, order, plan, shape):
-    wide_count, rows, _, _ = parts[0].shape
+            out_ref[:, col : col + own, :] = refs[which][w, :, first : first + own, :]
+
+
+def settle(parts, first_row, before, places, plan, shape):
+    wide_count, rows = parts[0].shape[:2]
     block = 16
     skip = first_row // block
     in_specs = [
@@ -573,7 +566,7 @@
         operands.append(before)
         aliases = {len(parts): 0}
     return pl.pallas_call(
-        functools.partial(settle_kernel, order=order, plan=plan),
+        functools.partial(settle_kernel, places=places, plan=plan),
         out_shape=jax.ShapeDtypeStruct(shape, jnp.bfloat16),
         grid=(rows // block,),
         in_specs=in_specs,
@@ -636,7 +629,7 @@
         tiled=True,
     )
     packed_start = pack_projection(w_proj_start, head_count, head_dim)
-    projected, bounded = project(lines, packed_start, head_count, head_dim, "rows")
+    projected = project(lines, packed_start, head_count, head_dim, "rows")
     if dense:
         bias = place_bias(key_ok, gathered, wide_count, tile_rows, tile_cols)
     else:
@@ -653,7 +646,7 @@
     upd = None
     for step, j in enumerate(order):
         upd, nxt, nbias = attend_rows(
-            row_ok, bounded, projected, lines, bias, w_out_start, w_bias_rows, j, upd, plan
+            row_ok, projected, lines, bias, w_out_start, w_bias_rows, j, upd, plan
         )
         waiting.append((j, nbias))
         if step in (0, chunks - 1):
@@ -687,54 +680,61 @@
     update_start = update_start.reshape(tile_rows, tile_cols, channels)
 
     packed_end = pack_projection(w_proj_end, head_count, head_dim)
-    projected_end, col_ok, bounded_end = None, [], []
+    soon = max(chunks - 1, 1)
+    home_of = [(0, step) if step < soon else (soon, step - soon) for step in range(chunks)]
+    projected_end, col_ok, bounded_end = {}, [], []
     for step, j in enumerate(order):
+        group, place = home_of[step]
         lines_end = columns[j]
         if own % 8:
             lines_end = lines_end.transpose(1, 0, 2)
-        projected_end, bounded = project(
+        projected_end[group], bounded = project(
             lines_end,
             packed_end,
             head_count,
             head_dim,
             "plain" if own % 8 else "columns",
-            projected_end,
-            step * own,
-            chunks * own,
+            projected_end.get(group),
+            place * own,
+            (soon if group == 0 else chunks - soon) * own,
         )
         at = wide_at * own + jnp.arange(own)
         at = narrow_at * tile_cols + at // piece * tile_rows + j * piece + at % piece
         col_ok.append(key_ok[at])
         bounded_end.append(bounded)
 
-    got = attend_columns(
-        jnp.concatenate(col_ok),
-        jnp.concatenate(bounded_end),
-        projected_end,
-        [next_biases[order[0]]],
-        w_out_end,
-        order[0],
-        0,
-        plan,
-    )
-    got = lax.all_to_all(got, "wide", split_axis=0, concat_axis=0, tiled=True)
-    if chunks == 1:
-        return (update_start, got.transpose(2, 0, 1, 3).reshape(pair_act.shape))
-    settled = settle([got], (chunks - 1) * piece, None, order, plan, pair_act.shape)
-    late = []
-    for step, j in enumerate(order):
-        got = attend_columns(
-            col_ok[step],
-            bounded_end[step],
-            projected_end,
-            [next_biases[k] for k in range(chunks - 1)],
+    def columns_of(step, count, chosen):
+        return attend_columns(
+            jnp.concatenate(col_ok[step : step + count]),
+            jnp.concatenate(bounded_end[step : step + count]),
+            projected_end[home_of[step][0]],
+            [next_biases[k] for k in chosen],
             w_out_end,
-            0,
-            step * own,
+            chosen[0],
+            home_of[step][1] * own,
             plan,
         )
+
+    early = []
+    for step, count in ((0, soon), (soon, chunks - soon)):
+        if count:
+            got = columns_of(step, count, order[:1])
+            got = lax.all_to_all(got, "wide", split_axis=0, concat_axis=0, tiled=True)
+            early.append(got)
+    if chunks == 1:
+        got = early[0]
+        if own % 8:
+            got = got.transpose(0, 2, 1, 3)
+        return (update_start, got.transpose(1, 0, 2, 3).reshape(pair_act.shape))
+    places = [(home_of[order.index(j)]) for j in range(chunks)]
+    places = [(0 if group == 0 else 1, place) for group, place in places]
+    settled = settle(early, (chunks - 1) * piece, None, places, plan, pair_act.shape)
+    late = []
+    for step in range(chunks):
+        got = columns_of(step, 1, list(range(chunks - 1)))
         late.append(lax.all_to_all(got, "wide", split_axis=0, concat_axis=0, tiled=True))
-    return (update_start, settle(late, 0, settled, order, plan, pair_act.shape))
+    places = [(order.index(j), 0) for j in range(chunks)]
+    return (update_start, settle(late, 0, settled, places, plan, pair_act.shape))
 
 
 def solution(mesh):

time: 577 us -> 584 us (1.012)
  Pallas kernels: 283 us -> 289 us
    pallas_call x3, Pallas kernels: 101 us -> 111 us  [attend_rows(): pl.pallas_call(functools.partial(attend_rows_kernel, head_count=head_coun...]
    all_to_all x1 -> x2, starting transfers between devices: 3.61 us -> 9.59 us  [on_device(): got = lax.all_to_all(got, 'wide', split_axis=0, concat_axis=0, tiled=True)]
    pallas_call x4 -> x5, Pallas kernels: 95 us -> 100 us  [attend_columns(): pl.pallas_call(functools.partial(attend_columns_kernel, parts=parts, head...]
    unnamed x46 -> x42, local copies, waits for them, and re-layouts: 12.1 us -> 12.1 us
  transfers between devices with their start and end apart: 13 -> 14, of which waited for: 8 -> 8; matrix products, arithmetic and copies ran while one was open for 3% -> 3% of each run, Pallas kernels for 40% -> 41%
where the time goes in v5:
time: 584 us; the launch traced here: 582 us
  Pallas kernels  289 us (49%)
  waiting for transfers between devices  152 us (26%)
  blocking collectives  56.7 us (10%)
  starting transfers between devices  37.4 us (6%)
  local copies, waits for them, and re-layouts  23 us (4%)
  between operations  14.2 us (2%)
  other arithmetic  9.35 us (2%)
    pallas_call x3, Pallas kernels, attend_rows(): pl.pallas_call(functools.partial(attend_rows_kernel, head_count=head_coun...  111 us
    pallas_call x5, Pallas kernels, attend_columns(): pl.pallas_call(functools.partial(attend_columns_kernel, parts=parts, head...  100 us
    all_to_all x1, waiting for transfers between devices, on_device(): lax.all_to_all(tile_in.reshape(narrow_count, row_count, tile_cols, channe...  66.6 us
    all_to_all x1, blocking collectives, on_device(): lax.all_to_all(nxt, both_axes, split_axis=0, concat_axis=0, tiled=True)  56.7 us
    ppermute x3, waiting for transfers between devices, on_device(): arrived.append(lax.ppermute(leaving[k - 1], 'narrow', ring))  47.4 us
    pallas_call x4, Pallas kernels, project(): pl.pallas_call(functools.partial(project_kernel, head_count=head_count, h...  45.7 us
    all_to_all x2, waiting for transfers between devices, on_device(): lax.all_to_all(nxt, both_axes, split_axis=0, concat_axis=0, tiled=True)  27.4 us
    pallas_call x3, Pallas kernels, turn_bias(): pl.pallas_call(turn_bias_kernel, out_shape=jax.ShapeDtypeStruct((head_cou...  14.7 us
  transfers between devices with their start and end apart: 14, of which 8 were waited for; matrix products, arithmetic and copies ran while one was open for 3% of the time, Pallas kernels for 41%

profile of v5, /device:TPU:0, one launch (start us, length us, event | category | flops | bytes accessed | tf_op | source)
XLA Modules:
  0.0 581.9 jit_solution(3232771683702389059)
XLA Ops:
  7.2 0.7 pad.7.w_ref
  7.9 2.3 copy-done.1
  10.2 8.0 %tile_bias.1 = f32[4,96,192]{2,1,0:T(8,128)S(1)} custom-call(bf16[96,192,128]{2,1,0:T(8,128)(2,1)S(1)} %copy-done.1, bf16[16,128]{1,0:T(8,128)(2,1)S(1)} %pad.7.w_ref), custom_call_target="tpu_custom_call" | custom-call | flops 75497472 | bytes 4718592 | tf_op jit(solution)/shard_map/tile_bias/pallas_call | solution.py:63
  18.3 0.8 maximum_maximum_fusion
  19.2 5.1 all-to-all-start
  24.4 0.7 dynamic_slice.13.row_ok_ref
  25.7 0.6 pad.8.w_bias_ref
  26.3 0.7 pad_maximum_fusion.w_ref
  27.0 0.7 fusion.rest_0_
  27.7 66.6 %all-to-all-done.x_ref = bf16[4,24,192,128]{3,2,1,0:T(8,128)(2,1)} async-done(((bf16[4,24,192,128]{3,2,1,0:T(8,128)(2,1)}), bf16[4,24,192,128]{3,2,1,0:T(8,128)(2,1)}, u32[]{:S(2)}, u32[]{:S(2)}) %all-to-all-start) | async-done | bytes 4718624 | tf_op jit(solution)/shard_map/all_to_all | solution.py:624
  94.4 19.1 %shard_map.95.key_ref = bf16[24,6,768,128]{3,2,1,0:T(8,128)(2,1)} custom-call(bf16[4,24,192,128]{3,2,1,0:T(8,128)(2,1)} %all-to-all-done.x_ref, bf16[128,768]{1,0:T(8,128)(2,1)} %pad_maximum_fusion.w_ref, bf16[256,128]{1,0:T(8,128)(2,1)} %fusion.rest_0_), custom_call_target="tpu_custom_call" | custom-call | flops 3623878656 | bytes 33030144 | tf_op jit(solution)/shard_map/pallas_call | solution.py:246
  113.5 3.1 all-gather.7.cloned.1.call-done
  116.6 3.7 copy-done.2
  120.3 3.0 place_bias.1
  123.3 3.7 copy-done
  127.0 36.9 %attend_rows.3 = (bf16[4,24,2,3,32,128]{5,4,3,2,1,0:T(8,128)(2,1)}, bf16[32,24,8,128]{3,2,1,0:T(8,128)(2,1)}, f32[4,24,256]{2,1,0:T(8,128)}) custom-call(s32[24]{0:T(128)} %dynamic_slice.13.row_ok_ref, bf16[24,6,8,3,32,128]{5,4,3,2,1,0:T(8,128)(2,1)} %bitcast.39, bf16[24,6,768,128]{3,2,1,0:T(8,128)(2,1)} %shard_map.95.key_ref, ...), custom_call_target="tpu_custom_call" | custom-call | flops 9663676416 | bytes 18874368 | tf_op jit(solution)/shard_map/attend_rows/pallas_call | solution.py:447
  163.9 3.3 all-to-all-start.1
  167.3 36.9 %attend_rows.4 = (bf16[4,24,2,3,32,128]{5,4,3,2,1,0:T(8,128)(2,1)}, bf16[32,24,8,128]{3,2,1,0:T(8,128)(2,1)}, f32[4,24,256]{2,1,0:T(8,128)}) custom-call(s32[24]{0:T(128)} %dynamic_slice.13.row_ok_ref, bf16[24,6,8,3,32,128]{5,4,3,2,1,0:T(8,128)(2,1)} %bitcast.40, bf16[24,6,768,128]{3,2,1,0:T(8,128)(2,1)} %shard_map.95.key_ref, ...), custom_call_target="tpu_custom_call", output_to_operand_aliasing={{0}: (7, {})} | custom-call | flops 9663676416 | bytes 18874368 | tf_op jit(solution)/shard_map/attend_rows/pallas_call | solution.py:447
  204.2 37.0 %attend_rows.5 = (bf16[4,24,2,3,32,128]{5,4,3,2,1,0:T(8,128)(2,1)}, bf16[32,24,8,128]{3,2,1,0:T(8,128)(2,1)}, f32[4,24,256]{2,1,0:T(8,128)}) custom-call(s32[24]{0:T(128)} %dynamic_slice.13.row_ok_ref, bf16[24,6,8,3,32,128]{5,4,3,2,1,0:T(8,128)(2,1)} %bitcast.41, bf16[24,6,768,128]{3,2,1,0:T(8,128)(2,1)} %shard_map.95.key_ref, ...), custom_call_target="tpu_custom_call", output_to_operand_aliasing={{0}: (7, {})} | custom-call | flops 9663676416 | bytes 18874368 | tf_op jit(solution)/shard_map/attend_rows/pallas_call | solution.py:447
  241.2 1.6 pad_maximum_fusion.2
  242.9 56.7 %all_to_all.45 = bf16[32,24,8,128]{3,2,1,0:T(8,128)(2,1)} all-to-all(bf16[32,24,8,128]{3,2,1,0:T(8,128)(2,1)} %get-tuple-element.38), channel_id=1, replica_groups=mesh['wide'=8,'narrow'=4] {'wide','narrow'}, dimensions={0} | all-to-all | bytes 3145728 | tf_op jit(solution)/shard_map/all_to_all | solution.py:664
  299.6 3.2 all-to-all-start.2
  302.8 0.6 gather_fusion
  304.1 0.6 gather_fusion.1
  304.8 1.2 gather_fusion.2
  306.0 0.6 pad_add_fusion.col_ok_ref
  306.6 0.7 pad_maximum_fusion.1.w_ref
  307.3 8.8 %shard_map.96 = (bf16[16,6,768,128]{3,2,1,0:T(8,128)(2,1)}, f32[8,8,128]{2,1,0:T(8,128)}) custom-call(bf16[768,8,128]{2,1,0:T(8,128)(2,1)} %bitcast.54, bf16[128,768]{1,0:T(8,128)(2,1)} %pad_maximum_fusion.1.w_ref, bf16[256,128]{1,0:T(8,128)(2,1)} %fusion.rest_0_), custom_call_target="tpu_custom_call" | custom-call | flops 1207959552 | bytes 11010048 | tf_op jit(solution)/shard_map/pallas_call | solution.py:246
  316.1 8.9 %shard_map.98 = (bf16[8,6,768,128]{3,2,1,0:T(8,128)(2,1)}, f32[8,8,128]{2,1,0:T(8,128)}) custom-call(bf16[768,8,128]{2,1,0:T(8,128)(2,1)} %bitcast.55, bf16[128,768]{1,0:T(8,128)(2,1)} %pad_maximum_fusion.1.w_ref, bf16[256,128]{1,0:T(8,128)(2,1)} %fusion.rest_0_), custom_call_target="tpu_custom_call" | custom-call | flops 1207959552 | bytes 11010048 | tf_op jit(solution)/shard_map/pallas_call | solution.py:246
  325.0 27.4 %all-to-all-done.2 = bf16[32,24,8,128]{3,2,1,0:T(8,128)(2,1)S(1)} async-done(((bf16[32,24,8,128]{3,2,1,0:T(8,128)(2,1)}), bf16[32,24,8,128]{3,2,1,0:T(8,128)(2,1)S(1)}, u32[]{:S(2)}, u32[]{:S(2)}) %all-to-all-start.2) | async-done | bytes 1572896 | tf_op jit(solution)/shard_map/all_to_all | solution.py:664
  352.4 1.1 copy-done.4
  353.5 8.9 %shard_map.97 = (bf16[16,6,768,128]{3,2,1,0:T(8,128)(2,1)}, f32[8,8,128]{2,1,0:T(8,128)}) custom-call(bf16[768,8,128]{2,1,0:T(8,128)(2,1)} %bitcast.52, bf16[128,768]{1,0:T(8,128)(2,1)} %pad_maximum_fusion.1.w_ref, bf16[256,128]{1,0:T(8,128)(2,1)} %fusion.rest_0_, bf16[16,6,768,128]{3,2,1,0:T(8,128)(2,1)} %get-tuple-element.33.rest_1_), custom_call_target="tpu_custom_call", output_to_operand_aliasing={{0}: (3, {})} | custom-call | flops 1207959552 | bytes 11010048 | tf_op jit(solution)/shard_map/pallas_call | solution.py:246
  362.4 1.0 multiply_reduce_fusion.1
  363.4 1.0 multiply_reduce_fusion.2
  364.3 1.0 multiply_reduce_fusion
  365.3 0.5 compare_convert_fusion.1.bounded_ref
  365.8 4.9 turn_bias.5.rest_0_
  370.7 13.6 %attend_columns.9 = bf16[8,32,8,128]{3,2,1,0:T(8,128)(2,1)} custom-call(s32[8]{0:T(128)} %gather_fusion.2, s32[8]{0:T(128)} %compare_convert_fusion.1.bounded_ref, bf16[8,6,8,3,32,128]{5,4,3,2,1,0:T(8,128)(2,1)} %bitcast.45, bf16[8,6,768,128]{3,2,1,0:T(8,128)(2,1)} %get-tuple-element.40.key_ref, f32[4,256,768]{2,1,0:T(8,128)} %turn_bias.5.rest_0_, ...), custom_call_target="tpu_custom_call" | custom-call | flops 3221225472 | bytes 6291456 | tf_op jit(solution)/shard_map/attend_columns/pallas_call | solution.py:523
  384.3 3.6 all-to-all-start.8
  387.9 0.7 pad_add_fusion.1.bounded_ref
  388.6 21.2 %attend_columns.8 = bf16[8,32,16,128]{3,2,1,0:T(8,128)(2,1)} custom-call(s32[16]{0:T(128)} %pad_add_fusion.col_ok_ref, s32[16]{0:T(128)} %pad_add_fusion.1.bounded_ref, bf16[16,6,8,3,32,128]{5,4,3,2,1,0:T(8,128)(2,1)} %bitcast.42, bf16[16,6,768,128]{3,2,1,0:T(8,128)(2,1)} %get-tuple-element.34.key_ref, f32[4,256,768]{2,1,0:T(8,128)} %turn_bias.5.rest_0_, ...), custom_call_target="tpu_custom_call" | custom-call | flops 6442450944 | bytes 12582912 | tf_op jit(solution)/shard_map/attend_columns/pallas_call | solution.py:523
  409.8 6.0 %all-to-all-start.7 = ((bf16[8,32,16,128]{3,2,1,0:T(8,128)(2,1)}), bf16[8,32,16,128]{3,2,1,0:T(8,128)(2,1)S(1)}, u32[]{:S(2)}, u32[]{:S(2)}) async-start(bf16[8,32,16,128]{3,2,1,0:T(8,128)(2,1)} %attend_columns.8), calls=%async_computation.7 | async-start | bytes 2097152 | tf_op jit(solution)/shard_map/all_to_all | solution.py:722
  415.8 4.9 turn_bias.3.rest_0_
  420.7 4.9 turn_bias.4.rest_1_
  425.6 21.8 %attend_columns.5 = bf16[8,64,8,128]{3,2,1,0:T(8,128)(2,1)} custom-call(s32[8]{0:T(128)} %copy-done.17, s32[8]{0:T(128)} %copy-done.16, bf16[16,6,8,3,32,128]{5,4,3,2,1,0:T(8,128)(2,1)} %bitcast.43, bf16[16,6,768,128]{3,2,1,0:T(8,128)(2,1)} %get-tuple-element.34.key_ref, f32[4,256,768]{2,1,0:T(8,128)} %turn_bias.3.rest_0_, f32[4,256,768]{2,1,0:T(8,128)} %turn_bias.4.rest_1_, ...), custom_call_target="tpu_custom_call" | custom-call | flops 6442450944 | bytes 6291456 | tf_op jit(solution)/shard_map/attend_columns/pallas_call | solution.py:523
  447.4 6.0 %all-to-all-start.3 = ((bf16[8,64,8,128]{3,2,1,0:T(8,128)(2,1)}), bf16[8,64,8,128]{3,2,1,0:T(8,128)(2,1)S(1)}, u32[]{:S(2)}, u32[]{:S(2)}) async-start(bf16[8,64,8,128]{3,2,1,0:T(8,128)(2,1)} %attend_columns.5), calls=%async_computation.3 | async-start | bytes 2097152 | tf_op jit(solution)/shard_map/all_to_all | solution.py:735
  453.4 21.8 %attend_columns.6 = bf16[8,64,8,128]{3,2,1,0:T(8,128)(2,1)} custom-call(s32[8]{0:T(128)} %copy-done.18, s32[8]{0:T(128)} %copy-done.15, bf16[16,6,8,3,32,128]{5,4,3,2,1,0:T(8,128)(2,1)} %bitcast.44, bf16[16,6,768,128]{3,2,1,0:T(8,128)(2,1)} %get-tuple-element.34.key_ref, f32[4,256,768]{2,1,0:T(8,128)} %turn_bias.3.rest_0_, f32[4,256,768]{2,1,0:T(8,128)} %turn_bias.4.rest_1_, ...), custom_call_target="tpu_custom_call" | custom-call | flops 6442450944 | bytes 6291456 | tf_op jit(solution)/shard_map/attend_columns/pallas_call | solution.py:523
  475.2 3.4 all-to-all-done.3.refs_0_
  478.6 3.6 all-to-all-start.4
  482.2 21.8 %attend_columns.7 = bf16[8,64,8,128]{3,2,1,0:T(8,128)(2,1)} custom-call(s32[8]{0:T(128)} %gather_fusion.2, s32[8]{0:T(128)} %compare_convert_fusion.1.bounded_ref, bf16[8,6,8,3,32,128]{5,4,3,2,1,0:T(8,128)(2,1)} %bitcast.46, bf16[8,6,768,128]{3,2,1,0:T(8,128)(2,1)} %get-tuple-element.40.key_ref, f32[4,256,768]{2,1,0:T(8,128)} %turn_bias.3.rest_0_, ...), custom_call_target="tpu_custom_call" | custom-call | flops 6442450944 | bytes 6291456 | tf_op jit(solution)/shard_map/attend_columns/pallas_call | solution.py:523
  504.0 4.0 all-to-all-done.4.refs_1_
  507.9 3.6 all-to-all-start.6
  511.6 2.2 constant_dynamic-slice_fusion
  513.9 1.5 collective-permute-start.1
  515.4 1.4 collective-permute-start.2
  516.8 24.7 %collective-permute-done = bf16[1,24,192,128]{3,2,1,0:T(8,128)(2,1)S(1)} collective-permute-done((bf16[1,24,192,128]{3,2,1,0:T(8,128)(2,1)S(1)}, bf16[1,24,192,128]{3,2,1,0:T(8,128)(2,1)S(1)}, u32[]{:S(2)}, u32[]{:S(2)}) %collective-permute-start) | collective-permute-done | bytes 1179680 | tf_op jit(solution)/shard_map/ppermute | solution.py:675
  541.5 1.1 constant_dynamic-update-slice_fusion.2
  542.5 0.2 collective-permute-done.1
  542.8 1.1 constant_dynamic-update-slice_fusion.1
  543.9 22.5 %collective-permute-done.2 = bf16[1,24,192,128]{3,2,1,0:T(8,128)(2,1)S(1)} collective-permute-done((bf16[1,24,192,128]{3,2,1,0:T(8,128)(2,1)S(1)}, bf16[1,24,192,128]{3,2,1,0:T(8,128)(2,1)S(1)}, u32[]{:S(2)}, u32[]{:S(2)}) %collective-permute-start.2) | collective-permute-done | bytes 1179680 | tf_op jit(solution)/shard_map/ppermute | solution.py:675
  566.4 1.1 constant_dynamic-update-slice_fusion
  567.5 2.5 settle.2.refs_3_
  569.9 1.0 copy-done.7
  570.9 4.4 settle.3
  (73 shorter events, 1.6 us)
Async XLA Ops:
  7.2 109.4 %all-gather.7.cloned.1.call-start = ((), (), s32[]{:S(2)}) async-start(), calls=%async_computation.9 | async-start | bytes 9732096 | tf_op jit(solution)/shard_map/all_gather | solution.py:622
  7.9 2.3 copy-start.1
  19.2 5.2 copy-start.14
  19.2 5.9 %copy-start.11 = (bf16[128,512]{1,0:T(8,128)(2,1)S(1)}, bf16[128,512]{1,0:T(8,128)(2,1)}, u32[]{:S(2)}) copy-start(bf16[128,512]{1,0:T(8,128)(2,1)} %param.10) | copy-start | bytes 393220
  19.2 6.5 %copy-start.19 = (bf16[128,4]{0,1:T(4,128)(2,1)S(1)}, bf16[128,4]{0,1:T(4,128)(2,1)}, u32[]{:S(2)}) copy-start(bf16[128,4]{0,1:T(4,128)(2,1)} %param.14) | copy-start | bytes 3076
  19.2 75.2 %all-to-all-start = ((bf16[4,24,192,128]{3,2,1,0:T(8,128)(2,1)}), bf16[4,24,192,128]{3,2,1,0:T(8,128)(2,1)}, u32[]{:S(2)}, u32[]{:S(2)}) async-start(bf16[4,24,192,128]{3,2,1,0:T(8,128)(2,1)} %bitcast.37), calls=%async_computation | async-start | bytes 9437184 | tf_op jit(solution)/shard_map/all_to_all | solution.py:624
  24.3 341.5 %all-gather.11.cloned.1.call-start = ((), (), s32[]{:S(2)}) async-start(), calls=%async_computation.11 | async-start | bytes 3244032 | tf_op jit(solution)/shard_map/all_gather | solution.py:653
  24.4 92.2 %copy-start.3 = (s32[1,768]{1,0:T(1,128)}, s32[1,768]{1,0:T(1,128)S(1)}, u32[]{:S(2)}) copy-start(s32[1,768]{1,0:T(1,128)S(1)} %broadcast_in_dim.2.key_ok_ref) | copy-start | bytes 9220
  116.6 3.7 copy-start.2
  123.3 3.7 copy-start
  163.9 79.0 %all-to-all-start.1 = ((bf16[32,24,8,128]{3,2,1,0:T(8,128)(2,1)}), bf16[32,24,8,128]{3,2,1,0:T(8,128)(2,1)S(1)}, u32[]{:S(2)}, u32[]{:S(2)}) async-start(bf16[32,24,8,128]{3,2,1,0:T(8,128)(2,1)} %get-tuple-element.30), calls=%async_computation.1 | async-start | bytes 3145728 | tf_op jit(solution)/shard_map/all_to_all | solution.py:664
  167.2 248.6 %all-gather.9.cloned.1.call-start = ((), (), s32[]{:S(2)}) async-start(), calls=%async_computation.10 | async-start | bytes 6488064 | tf_op jit(solution)/shard_map/all_gather | solution.py:653
  204.2 37.1 %copy-start.13 = (f32[4,24,256]{2,1,0:T(8,128)S(1)}, f32[4,24,256]{2,1,0:T(8,128)}, u32[]{:S(2)}) copy-start(f32[4,24,256]{2,1,0:T(8,128)} %get-tuple-element.35) | copy-start | bytes 294916
  241.2 62.2 %copy-start.12 = (bf16[128,512]{1,0:T(8,128)(2,1)S(1)}, bf16[128,512]{1,0:T(8,128)(2,1)}, u32[]{:S(2)}) copy-start(bf16[128,512]{1,0:T(8,128)(2,1)} %param.13) | copy-start | bytes 393220
  242.9 64.4 %copy-start.10 = (bf16[32,24,8,128]{3,2,1,0:T(8,128)(2,1)}, bf16[32,24,8,128]{3,2,1,0:T(8,128)(2,1)S(1)}, u32[]{:S(2)}) copy-start(bf16[32,24,8,128]{3,2,1,0:T(8,128)(2,1)S(1)} %all-to-all-done.1) | copy-start | bytes 4718596
  299.6 52.8 %all-to-all-start.2 = ((bf16[32,24,8,128]{3,2,1,0:T(8,128)(2,1)}), bf16[32,24,8,128]{3,2,1,0:T(8,128)(2,1)S(1)}, u32[]{:S(2)}, u32[]{:S(2)}) async-start(bf16[32,24,8,128]{3,2,1,0:T(8,128)(2,1)} %get-tuple-element.32), calls=%async_computation.2 | async-start | bytes 3145728 | tf_op jit(solution)/shard_map/all_to_all | solution.py:664
  303.4 21.6 %copy-start.17 = (s32[8]{0:T(128)}, s32[8]{0:T(128)S(1)}, u32[]{:S(2)}) copy-start(s32[8]{0:T(128)S(1)} %gather_fusion) | copy-start | bytes 100
  304.7 20.3 %copy-start.18 = (s32[8]{0:T(128)}, s32[8]{0:T(128)S(1)}, u32[]{:S(2)}) copy-start(s32[8]{0:T(128)S(1)} %gather_fusion.1) | copy-start | bytes 100
  352.4 1.1 copy-start.4
  384.3 25.5 %all-to-all-start.8 = ((bf16[8,32,8,128]{3,2,1,0:T(8,128)(2,1)}), bf16[8,32,8,128]{3,2,1,0:T(8,128)(2,1)S(1)}, u32[]{:S(2)}, u32[]{:S(2)}) async-start(bf16[8,32,8,128]{3,2,1,0:T(8,128)(2,1)} %attend_columns.9), calls=%async_computation.8 | async-start | bytes 1048576 | tf_op jit(solution)/shard_map/all_to_all | solution.py:722
  387.9 21.9 %copy-start.15 = (s32[8]{0:T(128)}, s32[8]{0:T(128)S(1)}, u32[]{:S(2)}) copy-start(s32[8]{0:T(128)S(1)} %get-tuple-element.57.bounded_ref) | copy-start | bytes 100
  387.9 21.9 %copy-start.16 = (s32[8]{0:T(128)}, s32[8]{0:T(128)S(1)}, u32[]{:S(2)}) copy-start(s32[8]{0:T(128)S(1)} %get-tuple-element.58.bounded_ref) | copy-start | bytes 100
  409.8 10.9 %copy-start.9 = (bf16[8,32,8,128]{3,2,1,0:T(8,128)(2,1)}, bf16[8,32,8,128]{3,2,1,0:T(8,128)(2,1)S(1)}, u32[]{:S(2)}) copy-start(bf16[8,32,8,128]{3,2,1,0:T(8,128)(2,1)S(1)} %all-to-all-done.8.refs_1_) | copy-start | bytes 1572868
  409.8 37.6 %all-to-all-start.7 = ((bf16[8,32,16,128]{3,2,1,0:T(8,128)(2,1)}), bf16[8,32,16,128]{3,2,1,0:T(8,128)(2,1)S(1)}, u32[]{:S(2)}, u32[]{:S(2)}) async-start(bf16[8,32,16,128]{3,2,1,0:T(8,128)(2,1)} %attend_columns.8), calls=%async_computation.7 | async-start | bytes 2097152 | tf_op jit(solution)/shard_map/all_to_all | solution.py:722
  447.4 27.8 %copy-start.8 = (bf16[8,32,16,128]{3,2,1,0:T(8,128)(2,1)}, bf16[8,32,16,128]{3,2,1,0:T(8,128)(2,1)S(1)}, u32[]{:S(2)}) copy-start(bf16[8,32,16,128]{3,2,1,0:T(8,128)(2,1)S(1)} %all-to-all-done.7.refs_0_) | copy-start | bytes 3145732
  447.4 31.2 %all-to-all-start.3 = ((bf16[8,64,8,128]{3,2,1,0:T(8,128)(2,1)}), bf16[8,64,8,128]{3,2,1,0:T(8,128)(2,1)S(1)}, u32[]{:S(2)}, u32[]{:S(2)}) async-start(bf16[8,64,8,128]{3,2,1,0:T(8,128)(2,1)} %attend_columns.5), calls=%async_computation.3 | async-start | bytes 2097152 | tf_op jit(solution)/shard_map/all_to_all | solution.py:735
  478.6 25.4 %copy-start.5 = (bf16[8,64,8,128]{3,2,1,0:T(8,128)(2,1)}, bf16[8,64,8,128]{3,2,1,0:T(8,128)(2,1)S(1)}, u32[]{:S(2)}) copy-start(bf16[8,64,8,128]{3,2,1,0:T(8,128)(2,1)S(1)} %all-to-all-done.3.refs_0_) | copy-start | bytes 3145732
  478.6 29.3 %all-to-all-start.4 = ((bf16[8,64,8,128]{3,2,1,0:T(8,128)(2,1)}), bf16[8,64,8,128]{3,2,1,0:T(8,128)(2,1)S(1)}, u32[]{:S(2)}, u32[]{:S(2)}) async-start(bf16[8,64,8,128]{3,2,1,0:T(8,128)(2,1)} %attend_columns.6), calls=%async_computation.4 | async-start | bytes 2097152 | tf_op jit(solution)/shard_map/all_to_all | solution.py:735
  507.9 34.6 %copy-start.6 = (bf16[8,64,8,128]{3,2,1,0:T(8,128)(2,1)}, bf16[8,64,8,128]{3,2,1,0:T(8,128)(2,1)S(1)}, u32[]{:S(2)}) copy-start(bf16[8,64,8,128]{3,2,1,0:T(8,128)(2,1)S(1)} %all-to-all-done.4.refs_1_) | copy-start | bytes 3145732
  507.9 62.0 %all-to-all-start.6 = ((bf16[8,64,8,128]{3,2,1,0:T(8,128)(2,1)}), bf16[8,64,8,128]{3,2,1,0:T(8,128)(2,1)S(1)}, u32[]{:S(2)}, u32[]{:S(2)}) async-start(bf16[8,64,8,128]{3,2,1,0:T(8,128)(2,1)} %attend_columns.7), calls=%async_computation.6 | async-start | bytes 2097152 | tf_op jit(solution)/shard_map/all_to_all | solution.py:735
  513.8 27.7 %collective-permute-start = (bf16[1,24,192,128]{3,2,1,0:T(8,128)(2,1)S(1)}, bf16[1,24,192,128]{3,2,1,0:T(8,128)(2,1)S(1)}, u32[]{:S(2)}, u32[]{:S(2)}) collective-permute-start(bf16[1,24,192,128]{3,2,1,0:T(8,128)(2,1)S(1)} %get-tuple-element.27), channel_id=1, source_target_pairs={{0,1},{1,2},{2,3},{3,0},{4,5},{5,6},{6,7},{7,4},{8,9},{9,10},{10,1... | collective-permute-start | bytes 3538952 | tf_op jit(solution)/shard_map/ppermute | solution.py:675
  513.9 28.9 %collective-permute-start.1 = (bf16[1,24,192,128]{3,2,1,0:T(8,128)(2,1)S(1)}, bf16[1,24,192,128]{3,2,1,0:T(8,128)(2,1)S(1)}, u32[]{:S(2)}, u32[]{:S(2)}) collective-permute-start(bf16[1,24,192,128]{3,2,1,0:T(8,128)(2,1)S(1)} %get-tuple-element.28), channel_id=1, source_target_pairs={{0,2},{1,3},{2,0},{3,1},{4,6},{5,7},{6,4},{7,5},{8,10},{9,11},{10,... | collective-permute-start | bytes 3538952 | tf_op jit(solution)/shard_map/ppermute | solution.py:675
  515.4 51.0 %collective-permute-start.2 = (bf16[1,24,192,128]{3,2,1,0:T(8,128)(2,1)S(1)}, bf16[1,24,192,128]{3,2,1,0:T(8,128)(2,1)S(1)}, u32[]{:S(2)}, u32[]{:S(2)}) collective-permute-start(bf16[1,24,192,128]{3,2,1,0:T(8,128)(2,1)S(1)} %get-tuple-element.29), channel_id=1, source_target_pairs={{0,3},{1,0},{2,1},{3,2},{4,7},{5,4},{6,5},{7,6},{8,11},{9,8},{10,9... | collective-permute-start | bytes 3538952 | tf_op jit(solution)/shard_map/ppermute | solution.py:675
  569.9 1.0 copy-start.7
Sparse Core Ops, SparseCore 0:
  19.3 97.2 all-gather.6
  164.0 64.0 all-gather.10
  243.0 97.8 all-gather.8

commit v6 on v5

--- a/solution.py
+++ b/solution.py
@@ -718,17 +718,15 @@
     early = []
     for step, count in ((0, soon), (soon, chunks - soon)):
         if count:
-            got = columns_of(step, count, order[:1])
-            got = lax.all_to_all(got, "wide", split_axis=0, concat_axis=0, tiled=True)
-            early.append(got)
+            early.append(columns_of(step, count, order[:1]))
+    got = early[0] if chunks == 1 else jnp.concatenate(early, axis=2)
+    got = lax.all_to_all(got, "wide", split_axis=0, concat_axis=0, tiled=True)
     if chunks == 1:
-        got = early[0]
         if own % 8:
             got = got.transpose(0, 2, 1, 3)
         return (update_start, got.transpose(1, 0, 2, 3).reshape(pair_act.shape))
-    places = [(home_of[order.index(j)]) for j in range(chunks)]
-    places = [(0 if group == 0 else 1, place) for group, place in places]
-    settled = settle(early, (chunks - 1) * piece, None, places, plan, pair_act.shape)
+    places = [(0, order.index(j)) for j in range(chunks)]
+    settled = settle([got], (chunks - 1) * piece, None, places, plan, pair_act.shape)
     late = []
     for step in range(chunks):
         got = columns_of(step, 1, list(range(chunks - 1)))

time: 584 us -> 585 us (level)
  waiting for transfers between devices: 152 us -> 161 us
  starting transfers between devices: 37.4 us -> 29.6 us
    unnamed x42 -> x44, local copies, waits for them, and re-layouts: 12.1 us -> 12.2 us
  transfers between devices with their start and end apart: 14 -> 13, of which waited for: 8 -> 10; matrix products, arithmetic and copies ran while one was open for 3% -> 4% of each run, Pallas kernels for 41% -> 41%
where the time goes in v6:
time: 585 us; the launch traced here: 583 us
  Pallas kernels  290 us (50%)
  waiting for transfers between devices  161 us (28%)
  blocking collectives  53.6 us (9%)
  starting transfers between devices  29.6 us (5%)
  local copies, waits for them, and re-layouts  22.9 us (4%)
  between operations  14.1 us (2%)
  other arithmetic  12.1 us (2%)
    pallas_call x3, Pallas kernels, attend_rows(): pl.pallas_call(functools.partial(attend_rows_kernel, head_count=head_coun...  111 us
    pallas_call x5, Pallas kernels, attend_columns(): pl.pallas_call(functools.partial(attend_columns_kernel, parts=parts, head...  100 us
    all_to_all x1, waiting for transfers between devices, on_device(): lax.all_to_all(tile_in.reshape(narrow_count, row_count, tile_cols, channe...  66.7 us
    all_to_all x1, blocking collectives, on_device(): lax.all_to_all(nxt, both_axes, split_axis=0, concat_axis=0, tiled=True)  53.6 us
    ppermute x3, waiting for transfers between devices, on_device(): arrived.append(lax.ppermute(leaving[k - 1], 'narrow', ring))  47.4 us
    pallas_call x4, Pallas kernels, project(): pl.pallas_call(functools.partial(project_kernel, head_count=head_count, h...  45.7 us
    all_to_all x2, waiting for transfers between devices, on_device(): lax.all_to_all(nxt, both_axes, split_axis=0, concat_axis=0, tiled=True)  29.7 us
    pallas_call x3, Pallas kernels, turn_bias(): pl.pallas_call(turn_bias_kernel, out_shape=jax.ShapeDtypeStruct((head_cou...  14.7 us
  transfers between devices with their start and end apart: 13, of which 10 were waited for; matrix products, arithmetic and copies ran while one was open for 4% of the time, Pallas kernels for 41%

profile of v6, /device:TPU:0, one launch (start us, length us, event | category | flops | bytes accessed | tf_op | source)
XLA Modules:
  0.0 582.7 jit_solution(6333457993203764917)
XLA Ops:
  7.2 0.7 pad.7.w_ref
  7.9 2.3 copy-done.1
  10.2 8.0 %tile_bias.1 = f32[4,96,192]{2,1,0:T(8,128)S(1)} custom-call(bf16[96,192,128]{2,1,0:T(8,128)(2,1)S(1)} %copy-done.1, bf16[16,128]{1,0:T(8,128)(2,1)S(1)} %pad.7.w_ref), custom_call_target="tpu_custom_call" | custom-call | flops 75497472 | bytes 4718592 | tf_op jit(solution)/shard_map/tile_bias/pallas_call | solution.py:63
  18.3 0.8 maximum_maximum_fusion
  19.2 5.1 all-to-all-start
  24.4 0.6 dynamic_slice.13.row_ok_ref
  25.6 0.6 pad.8.w_bias_ref
  26.2 0.7 pad_maximum_fusion.1.w_ref
  26.9 0.7 fusion.rest_0_
  27.7 66.7 %all-to-all-done.x_ref = bf16[4,24,192,128]{3,2,1,0:T(8,128)(2,1)} async-done(((bf16[4,24,192,128]{3,2,1,0:T(8,128)(2,1)}), bf16[4,24,192,128]{3,2,1,0:T(8,128)(2,1)}, u32[]{:S(2)}, u32[]{:S(2)}) %all-to-all-start) | async-done | bytes 4718624 | tf_op jit(solution)/shard_map/all_to_all | solution.py:624
  94.4 19.1 %shard_map.95.key_ref = bf16[24,6,768,128]{3,2,1,0:T(8,128)(2,1)} custom-call(bf16[4,24,192,128]{3,2,1,0:T(8,128)(2,1)} %all-to-all-done.x_ref, bf16[128,768]{1,0:T(8,128)(2,1)} %pad_maximum_fusion.1.w_ref, bf16[256,128]{1,0:T(8,128)(2,1)} %fusion.rest_0_), custom_call_target="tpu_custom_call" | custom-call | flops 3623878656 | bytes 33030144 | tf_op jit(solution)/shard_map/pallas_call | solution.py:246
  113.5 3.1 all-gather.7.cloned.1.call-done
  116.6 3.7 copy-done.2
  120.3 3.0 place_bias.1
  123.3 3.7 copy-done
  127.0 36.9 %attend_rows.3 = (bf16[4,24,2,3,32,128]{5,4,3,2,1,0:T(8,128)(2,1)}, bf16[32,24,8,128]{3,2,1,0:T(8,128)(2,1)}, f32[4,24,256]{2,1,0:T(8,128)}) custom-call(s32[24]{0:T(128)} %dynamic_slice.13.row_ok_ref, bf16[24,6,8,3,32,128]{5,4,3,2,1,0:T(8,128)(2,1)} %bitcast.39, bf16[24,6,768,128]{3,2,1,0:T(8,128)(2,1)} %shard_map.95.key_ref, ...), custom_call_target="tpu_custom_call" | custom-call | flops 9663676416 | bytes 18874368 | tf_op jit(solution)/shard_map/attend_rows/pallas_call | solution.py:447
  163.9 36.9 %attend_rows.4 = (bf16[4,24,2,3,32,128]{5,4,3,2,1,0:T(8,128)(2,1)}, bf16[32,24,8,128]{3,2,1,0:T(8,128)(2,1)}, f32[4,24,256]{2,1,0:T(8,128)}) custom-call(s32[24]{0:T(128)} %dynamic_slice.13.row_ok_ref, bf16[24,6,8,3,32,128]{5,4,3,2,1,0:T(8,128)(2,1)} %bitcast.40, bf16[24,6,768,128]{3,2,1,0:T(8,128)(2,1)} %shard_map.95.key_ref, ...), custom_call_target="tpu_custom_call", output_to_operand_aliasing={{0}: (7, {})} | custom-call | flops 9663676416 | bytes 18874368 | tf_op jit(solution)/shard_map/attend_rows/pallas_call | solution.py:447
  200.8 3.4 all-to-all-start.2
  204.3 37.1 %attend_rows.5 = (bf16[4,24,2,3,32,128]{5,4,3,2,1,0:T(8,128)(2,1)}, bf16[32,24,8,128]{3,2,1,0:T(8,128)(2,1)}, f32[4,24,256]{2,1,0:T(8,128)}) custom-call(s32[24]{0:T(128)} %dynamic_slice.13.row_ok_ref, bf16[24,6,8,3,32,128]{5,4,3,2,1,0:T(8,128)(2,1)} %bitcast.41, bf16[24,6,768,128]{3,2,1,0:T(8,128)(2,1)} %shard_map.95.key_ref, ...), custom_call_target="tpu_custom_call", output_to_operand_aliasing={{0}: (7, {})} | custom-call | flops 9663676416 | bytes 18874368 | tf_op jit(solution)/shard_map/attend_rows/pallas_call | solution.py:447
  241.4 1.6 pad_maximum_fusion.3
  243.0 7.0 %all-to-all-done.2 = bf16[32,24,8,128]{3,2,1,0:T(8,128)(2,1)S(1)} async-done(((bf16[32,24,8,128]{3,2,1,0:T(8,128)(2,1)}), bf16[32,24,8,128]{3,2,1,0:T(8,128)(2,1)S(1)}, u32[]{:S(2)}, u32[]{:S(2)}) %all-to-all-start.2) | async-done | bytes 1572896 | tf_op jit(solution)/shard_map/all_to_all | solution.py:664
  250.1 53.6 %all_to_all.40 = bf16[32,24,8,128]{3,2,1,0:T(8,128)(2,1)} all-to-all(bf16[32,24,8,128]{3,2,1,0:T(8,128)(2,1)S(1)} %copy-done.11), channel_id=1, replica_groups=mesh['wide'=8,'narrow'=4] {'wide','narrow'}, dimensions={0} | all-to-all | bytes 3145728 | tf_op jit(solution)/shard_map/all_to_all | solution.py:664
  303.6 3.4 all-to-all-start.5
  307.0 0.6 gather_fusion
  308.3 0.6 gather_fusion.1
  309.0 1.2 gather_fusion.2
  310.2 0.6 pad_add_fusion.col_ok_ref
  310.8 0.7 pad_maximum_fusion.2.w_ref
  311.5 8.8 %shard_map.96 = (bf16[16,6,768,128]{3,2,1,0:T(8,128)(2,1)}, f32[8,8,128]{2,1,0:T(8,128)}) custom-call(bf16[768,8,128]{2,1,0:T(8,128)(2,1)} %bitcast.55, bf16[128,768]{1,0:T(8,128)(2,1)} %pad_maximum_fusion.2.w_ref, bf16[256,128]{1,0:T(8,128)(2,1)} %fusion.rest_0_), custom_call_target="tpu_custom_call" | custom-call | flops 1207959552 | bytes 11010048 | tf_op jit(solution)/shard_map/pallas_call | solution.py:246
  320.4 8.9 %shard_map.97 = (bf16[16,6,768,128]{3,2,1,0:T(8,128)(2,1)}, f32[8,8,128]{2,1,0:T(8,128)}) custom-call(bf16[768,8,128]{2,1,0:T(8,128)(2,1)} %bitcast.52, bf16[128,768]{1,0:T(8,128)(2,1)} %pad_maximum_fusion.2.w_ref, bf16[256,128]{1,0:T(8,128)(2,1)} %fusion.rest_0_, bf16[16,6,768,128]{3,2,1,0:T(8,128)(2,1)} %get-tuple-element.33.rest_1_), custom_call_target="tpu_custom_call", output_to_operand_aliasing={{0}: (3, {})} | custom-call | flops 1207959552 | bytes 11010048 | tf_op jit(solution)/shard_map/pallas_call | solution.py:246
  329.3 1.0 multiply_reduce_fusion.1
  330.3 1.0 multiply_reduce_fusion.2
  331.3 0.6 pad_add_fusion.1.bounded_ref
  331.9 22.7 %all-to-all-done.5 = bf16[32,24,8,128]{3,2,1,0:T(8,128)(2,1)S(1)} async-done(((bf16[32,24,8,128]{3,2,1,0:T(8,128)(2,1)}), bf16[32,24,8,128]{3,2,1,0:T(8,128)(2,1)S(1)}, u32[]{:S(2)}, u32[]{:S(2)}) %all-to-all-start.5) | async-done | bytes 1572896 | tf_op jit(solution)/shard_map/all_to_all | solution.py:664
  354.6 1.1 copy-done.10
  355.7 8.8 %shard_map.98 = (bf16[8,6,768,128]{3,2,1,0:T(8,128)(2,1)}, f32[8,8,128]{2,1,0:T(8,128)}) custom-call(bf16[768,8,128]{2,1,0:T(8,128)(2,1)} %bitcast.54, bf16[128,768]{1,0:T(8,128)(2,1)} %pad_maximum_fusion.2.w_ref, bf16[256,128]{1,0:T(8,128)(2,1)} %fusion.rest_0_), custom_call_target="tpu_custom_call" | custom-call | flops 1207959552 | bytes 11010048 | tf_op jit(solution)/shard_map/pallas_call | solution.py:246
  364.6 1.0 multiply_reduce_fusion
  366.1 4.9 turn_bias.5.rest_0_
  371.0 13.6 %attend_columns.9 = bf16[8,32,8,128]{3,2,1,0:T(8,128)(2,1)} custom-call(s32[8]{0:T(128)} %gather_fusion.2, s32[8]{0:T(128)} %compare_convert_fusion.1.bounded_ref, bf16[8,6,8,3,32,128]{5,4,3,2,1,0:T(8,128)(2,1)} %bitcast.45, bf16[8,6,768,128]{3,2,1,0:T(8,128)(2,1)} %get-tuple-element.40.key_ref, f32[4,256,768]{2,1,0:T(8,128)} %turn_bias.5.rest_0_, ...), custom_call_target="tpu_custom_call" | custom-call | flops 3221225472 | bytes 6291456 | tf_op jit(solution)/shard_map/attend_columns/pallas_call | solution.py:523
  384.6 21.3 %attend_columns.8 = bf16[8,32,16,128]{3,2,1,0:T(8,128)(2,1)} custom-call(s32[16]{0:T(128)} %pad_add_fusion.col_ok_ref, s32[16]{0:T(128)} %pad_add_fusion.1.bounded_ref, bf16[16,6,8,3,32,128]{5,4,3,2,1,0:T(8,128)(2,1)} %bitcast.42, bf16[16,6,768,128]{3,2,1,0:T(8,128)(2,1)} %get-tuple-element.34.key_ref, f32[4,256,768]{2,1,0:T(8,128)} %turn_bias.5.rest_0_, ...), custom_call_target="tpu_custom_call" | custom-call | flops 6442450944 | bytes 12582912 | tf_op jit(solution)/shard_map/attend_columns/pallas_call | solution.py:523
  405.9 2.6 pad_maximum_fusion
  408.5 3.8 all-to-all-start.7
  412.4 4.9 turn_bias.3.rest_0_
  417.3 4.9 turn_bias.4.rest_1_
  422.2 21.8 %attend_columns.5 = bf16[8,64,8,128]{3,2,1,0:T(8,128)(2,1)} custom-call(s32[8]{0:T(128)} %copy-done.18, s32[8]{0:T(128)} %copy-done.17, bf16[16,6,8,3,32,128]{5,4,3,2,1,0:T(8,128)(2,1)} %bitcast.43, bf16[16,6,768,128]{3,2,1,0:T(8,128)(2,1)} %get-tuple-element.34.key_ref, f32[4,256,768]{2,1,0:T(8,128)} %turn_bias.3.rest_0_, f32[4,256,768]{2,1,0:T(8,128)} %turn_bias.4.rest_1_, ...), custom_call_target="tpu_custom_call" | custom-call | flops 6442450944 | bytes 6291456 | tf_op jit(solution)/shard_map/attend_columns/pallas_call | solution.py:523
  444.0 5.6 all-to-all-done.7.refs_0_
  449.6 3.6 all-to-all-start.3
  453.2 21.8 %attend_columns.6 = bf16[8,64,8,128]{3,2,1,0:T(8,128)(2,1)} custom-call(s32[8]{0:T(128)} %copy-done.19, s32[8]{0:T(128)} %copy-done.16, bf16[16,6,8,3,32,128]{5,4,3,2,1,0:T(8,128)(2,1)} %bitcast.44, bf16[16,6,768,128]{3,2,1,0:T(8,128)(2,1)} %get-tuple-element.34.key_ref, f32[4,256,768]{2,1,0:T(8,128)} %turn_bias.3.rest_0_, f32[4,256,768]{2,1,0:T(8,128)} %turn_bias.4.rest_1_, ...), custom_call_target="tpu_custom_call" | custom-call | flops 6442450944 | bytes 6291456 | tf_op jit(solution)/shard_map/attend_columns/pallas_call | solution.py:523
  475.0 4.1 all-to-all-done.3.refs_0_
  479.1 3.6 all-to-all-start.4
  482.8 21.8 %attend_columns.7 = bf16[8,64,8,128]{3,2,1,0:T(8,128)(2,1)} custom-call(s32[8]{0:T(128)} %gather_fusion.2, s32[8]{0:T(128)} %compare_convert_fusion.1.bounded_ref, bf16[8,6,8,3,32,128]{5,4,3,2,1,0:T(8,128)(2,1)} %bitcast.46, bf16[8,6,768,128]{3,2,1,0:T(8,128)(2,1)} %get-tuple-element.40.key_ref, f32[4,256,768]{2,1,0:T(8,128)} %turn_bias.3.rest_0_, ...), custom_call_target="tpu_custom_call" | custom-call | flops 6442450944 | bytes 6291456 | tf_op jit(solution)/shard_map/attend_columns/pallas_call | solution.py:523
  504.6 4.1 all-to-all-done.4.refs_1_
  508.7 3.6 all-to-all-start.6
  512.4 2.2 constant_dynamic-slice_fusion
  514.7 1.5 collective-permute-start.1
  516.2 1.4 collective-permute-start.2
  517.6 24.7 %collective-permute-done = bf16[1,24,192,128]{3,2,1,0:T(8,128)(2,1)S(1)} collective-permute-done((bf16[1,24,192,128]{3,2,1,0:T(8,128)(2,1)S(1)}, bf16[1,24,192,128]{3,2,1,0:T(8,128)(2,1)S(1)}, u32[]{:S(2)}, u32[]{:S(2)}) %collective-permute-start) | collective-permute-done | bytes 1179680 | tf_op jit(solution)/shard_map/ppermute | solution.py:675
  542.3 1.1 constant_dynamic-update-slice_fusion.2
  543.6 1.1 constant_dynamic-update-slice_fusion.1
  544.7 22.5 %collective-permute-done.2 = bf16[1,24,192,128]{3,2,1,0:T(8,128)(2,1)S(1)} collective-permute-done((bf16[1,24,192,128]{3,2,1,0:T(8,128)(2,1)S(1)}, bf16[1,24,192,128]{3,2,1,0:T(8,128)(2,1)S(1)}, u32[]{:S(2)}, u32[]{:S(2)}) %collective-permute-start.2) | collective-permute-done | bytes 1179680 | tf_op jit(solution)/shard_map/ppermute | solution.py:675
  567.2 1.1 constant_dynamic-update-slice_fusion
  568.2 2.5 settle.2.refs_3_
  570.7 1.0 copy-done.8
  571.7 4.4 settle.3
  (74 shorter events, 2.4 us)
Async XLA Ops:
  7.2 109.4 %all-gather.7.cloned.1.call-start = ((), (), s32[]{:S(2)}) async-start(), calls=%async_computation.8 | async-start | bytes 9732096 | tf_op jit(solution)/shard_map/all_gather | solution.py:622
  7.9 2.3 copy-start.1
  19.2 5.2 copy-start.15
  19.2 5.8 copy-start.12
  19.2 6.5 %copy-start.20 = (bf16[128,4]{0,1:T(4,128)(2,1)S(1)}, bf16[128,4]{0,1:T(4,128)(2,1)}, u32[]{:S(2)}) copy-start(bf16[128,4]{0,1:T(4,128)(2,1)} %param.14) | copy-start | bytes 3076
  19.2 75.2 %all-to-all-start = ((bf16[4,24,192,128]{3,2,1,0:T(8,128)(2,1)}), bf16[4,24,192,128]{3,2,1,0:T(8,128)(2,1)}, u32[]{:S(2)}, u32[]{:S(2)}) async-start(bf16[4,24,192,128]{3,2,1,0:T(8,128)(2,1)} %bitcast.37), calls=%async_computation | async-start | bytes 9437184 | tf_op jit(solution)/shard_map/all_to_all | solution.py:624
  24.3 341.8 %all-gather.11.cloned.1.call-start = ((), (), s32[]{:S(2)}) async-start(), calls=%async_computation.10 | async-start | bytes 3244032 | tf_op jit(solution)/shard_map/all_gather | solution.py:653
  24.4 92.2 %copy-start.3 = (s32[1,768]{1,0:T(1,128)}, s32[1,768]{1,0:T(1,128)S(1)}, u32[]{:S(2)}) copy-start(s32[1,768]{1,0:T(1,128)S(1)} %broadcast_in_dim.2.key_ok_ref) | copy-start | bytes 9220
  116.6 3.7 copy-start.2
  123.3 3.7 copy-start
  200.8 49.2 %all-to-all-start.2 = ((bf16[32,24,8,128]{3,2,1,0:T(8,128)(2,1)}), bf16[32,24,8,128]{3,2,1,0:T(8,128)(2,1)S(1)}, u32[]{:S(2)}, u32[]{:S(2)}) async-start(bf16[32,24,8,128]{3,2,1,0:T(8,128)(2,1)} %get-tuple-element.32), calls=%async_computation.2 | async-start | bytes 3145728 | tf_op jit(solution)/shard_map/all_to_all | solution.py:664
  204.2 208.2 %all-gather.9.cloned.1.call-start = ((), (), s32[]{:S(2)}) async-start(), calls=%async_computation.9 | async-start | bytes 6488064 | tf_op jit(solution)/shard_map/all_gather | solution.py:653
  204.2 37.1 %copy-start.14 = (f32[4,24,256]{2,1,0:T(8,128)S(1)}, f32[4,24,256]{2,1,0:T(8,128)}, u32[]{:S(2)}) copy-start(f32[4,24,256]{2,1,0:T(8,128)} %get-tuple-element.35) | copy-start | bytes 294916
  204.2 45.8 %copy-start.11 = (bf16[32,24,8,128]{3,2,1,0:T(8,128)(2,1)S(1)}, bf16[32,24,8,128]{3,2,1,0:T(8,128)(2,1)}, u32[]{:S(2)}) copy-start(bf16[32,24,8,128]{3,2,1,0:T(8,128)(2,1)} %get-tuple-element.30) | copy-start | bytes 4718596
  250.1 53.6 %copy-start.4 = (bf16[32,24,8,128]{3,2,1,0:T(8,128)(2,1)}, bf16[32,24,8,128]{3,2,1,0:T(8,128)(2,1)S(1)}, u32[]{:S(2)}) copy-start(bf16[32,24,8,128]{3,2,1,0:T(8,128)(2,1)S(1)} %all-to-all-done.2) | copy-start | bytes 4718596
  250.1 57.6 %copy-start.13 = (bf16[128,512]{1,0:T(8,128)(2,1)S(1)}, bf16[128,512]{1,0:T(8,128)(2,1)}, u32[]{:S(2)}) copy-start(bf16[128,512]{1,0:T(8,128)(2,1)} %param.13) | copy-start | bytes 393220
  303.6 51.0 %all-to-all-start.5 = ((bf16[32,24,8,128]{3,2,1,0:T(8,128)(2,1)}), bf16[32,24,8,128]{3,2,1,0:T(8,128)(2,1)S(1)}, u32[]{:S(2)}, u32[]{:S(2)}) async-start(bf16[32,24,8,128]{3,2,1,0:T(8,128)(2,1)} %get-tuple-element.38), calls=%async_computation.5 | async-start | bytes 3145728 | tf_op jit(solution)/shard_map/all_to_all | solution.py:664
  307.7 12.7 %copy-start.18 = (s32[8]{0:T(128)}, s32[8]{0:T(128)S(1)}, u32[]{:S(2)}) copy-start(s32[8]{0:T(128)S(1)} %gather_fusion) | copy-start | bytes 100
  309.0 20.3 %copy-start.19 = (s32[8]{0:T(128)}, s32[8]{0:T(128)S(1)}, u32[]{:S(2)}) copy-start(s32[8]{0:T(128)S(1)} %gather_fusion.1) | copy-start | bytes 100
  331.3 39.7 %copy-start.16 = (s32[8]{0:T(128)}, s32[8]{0:T(128)S(1)}, u32[]{:S(2)}) copy-start(s32[8]{0:T(128)S(1)} %get-tuple-element.57.bounded_ref) | copy-start | bytes 100
  331.3 39.7 %copy-start.17 = (s32[8]{0:T(128)}, s32[8]{0:T(128)S(1)}, u32[]{:S(2)}) copy-start(s32[8]{0:T(128)S(1)} %get-tuple-element.58.bounded_ref) | copy-start | bytes 100
  354.6 1.1 copy-start.10
  384.6 21.3 %copy-start.9 = (bf16[8,32,8,128]{3,2,1,0:T(8,128)(2,1)S(1)}, bf16[8,32,8,128]{3,2,1,0:T(8,128)(2,1)}, u32[]{:S(2)}) copy-start(bf16[8,32,8,128]{3,2,1,0:T(8,128)(2,1)} %attend_columns.9) | copy-start | bytes 1572868
  408.5 41.0 %all-to-all-start.7 = ((bf16[8,32,24,128]{3,2,1,0:T(8,128)(2,1)}), bf16[8,32,24,128]{3,2,1,0:T(8,128)(2,1)S(1)}, u32[]{:S(2)}, u32[]{:S(2)}) async-start(bf16[8,32,24,128]{3,2,1,0:T(8,128)(2,1)} %pad_maximum_fusion), calls=%async_computation.7 | async-start | bytes 3145728 | tf_op jit(solution)/shard_map/all_to_all | solution.py:723
  449.6 25.4 %copy-start.5 = (bf16[8,32,24,128]{3,2,1,0:T(8,128)(2,1)}, bf16[8,32,24,128]{3,2,1,0:T(8,128)(2,1)S(1)}, u32[]{:S(2)}) copy-start(bf16[8,32,24,128]{3,2,1,0:T(8,128)(2,1)S(1)} %all-to-all-done.7.refs_0_) | copy-start | bytes 4718596
  449.6 29.6 %all-to-all-start.3 = ((bf16[8,64,8,128]{3,2,1,0:T(8,128)(2,1)}), bf16[8,64,8,128]{3,2,1,0:T(8,128)(2,1)S(1)}, u32[]{:S(2)}, u32[]{:S(2)}) async-start(bf16[8,64,8,128]{3,2,1,0:T(8,128)(2,1)} %attend_columns.5), calls=%async_computation.3 | async-start | bytes 2097152 | tf_op jit(solution)/shard_map/all_to_all | solution.py:733
  479.1 25.4 %copy-start.6 = (bf16[8,64,8,128]{3,2,1,0:T(8,128)(2,1)}, bf16[8,64,8,128]{3,2,1,0:T(8,128)(2,1)S(1)}, u32[]{:S(2)}) copy-start(bf16[8,64,8,128]{3,2,1,0:T(8,128)(2,1)S(1)} %all-to-all-done.3.refs_0_) | copy-start | bytes 3145732
  479.1 29.6 %all-to-all-start.4 = ((bf16[8,64,8,128]{3,2,1,0:T(8,128)(2,1)}), bf16[8,64,8,128]{3,2,1,0:T(8,128)(2,1)S(1)}, u32[]{:S(2)}, u32[]{:S(2)}) async-start(bf16[8,64,8,128]{3,2,1,0:T(8,128)(2,1)} %attend_columns.6), calls=%async_computation.4 | async-start | bytes 2097152 | tf_op jit(solution)/shard_map/all_to_all | solution.py:733
  508.7 5.9 %copy-start.7 = (bf16[8,64,8,128]{3,2,1,0:T(8,128)(2,1)}, bf16[8,64,8,128]{3,2,1,0:T(8,128)(2,1)S(1)}, u32[]{:S(2)}) copy-start(bf16[8,64,8,128]{3,2,1,0:T(8,128)(2,1)S(1)} %all-to-all-done.4.refs_1_) | copy-start | bytes 3145732
  508.7 62.0 %all-to-all-start.6 = ((bf16[8,64,8,128]{3,2,1,0:T(8,128)(2,1)}), bf16[8,64,8,128]{3,2,1,0:T(8,128)(2,1)S(1)}, u32[]{:S(2)}, u32[]{:S(2)}) async-start(bf16[8,64,8,128]{3,2,1,0:T(8,128)(2,1)} %attend_columns.7), calls=%async_computation.6 | async-start | bytes 2097152 | tf_op jit(solution)/shard_map/all_to_all | solution.py:733
  514.6 27.7 %collective-permute-start = (bf16[1,24,192,128]{3,2,1,0:T(8,128)(2,1)S(1)}, bf16[1,24,192,128]{3,2,1,0:T(8,128)(2,1)S(1)}, u32[]{:S(2)}, u32[]{:S(2)}) collective-permute-start(bf16[1,24,192,128]{3,2,1,0:T(8,128)(2,1)S(1)} %get-tuple-element.27), channel_id=1, source_target_pairs={{0,1},{1,2},{2,3},{3,0},{4,5},{5,6},{6,7},{7,4},{8,9},{9,10},{10,1... | collective-permute-start | bytes 3538952 | tf_op jit(solution)/shard_map/ppermute | solution.py:675
  514.7 28.9 %collective-permute-start.1 = (bf16[1,24,192,128]{3,2,1,0:T(8,128)(2,1)S(1)}, bf16[1,24,192,128]{3,2,1,0:T(8,128)(2,1)S(1)}, u32[]{:S(2)}, u32[]{:S(2)}) collective-permute-start(bf16[1,24,192,128]{3,2,1,0:T(8,128)(2,1)S(1)} %get-tuple-element.28), channel_id=1, source_target_pairs={{0,2},{1,3},{2,0},{3,1},{4,6},{5,7},{6,4},{7,5},{8,10},{9,11},{10,... | collective-permute-start | bytes 3538952 | tf_op jit(solution)/shard_map/ppermute | solution.py:675
  516.2 51.0 %collective-permute-start.2 = (bf16[1,24,192,128]{3,2,1,0:T(8,128)(2,1)S(1)}, bf16[1,24,192,128]{3,2,1,0:T(8,128)(2,1)S(1)}, u32[]{:S(2)}, u32[]{:S(2)}) collective-permute-start(bf16[1,24,192,128]{3,2,1,0:T(8,128)(2,1)S(1)} %get-tuple-element.29), channel_id=1, source_target_pairs={{0,3},{1,0},{2,1},{3,2},{4,7},{5,4},{6,5},{7,6},{8,11},{9,8},{10,9... | collective-permute-start | bytes 3538952 | tf_op jit(solution)/shard_map/ppermute | solution.py:675
  570.7 1.0 copy-start.8
Sparse Core Ops, SparseCore 0:
  19.3 97.2 all-gather.6
  164.0 70.3 all-gather.10
  243.1 98.8 all-gather.8
